TPU v7x, 32 devices: a whole 2x2x4 slice. The times are simulated.
32 devices in a mesh: rep: 2 (over y), fsdp: 16 (over z, x, core).
Axes of the slice: x: 2, y: 2, z: 4, core: 2. Of those that a mesh axis runs over, the one named last changes fastest.
Arguments:
- block_input: bfloat16 [24576, 768], P(('rep', 'fsdp')), may hold values from -6 to 6
- cotangent: bfloat16 [24576, 768], P(('rep', 'fsdp')), may hold values from -6 to 6
- tie_index: int32 [1], replicated, may hold values from 0 to 11
- prefix_len: int32 [32, 1], P(('rep', 'fsdp')), may hold values from 1 to 2048, as said below
- pre_gain: bfloat16 [12, 768], P(None, 'fsdp'), may hold values from 0.5 to 1.5
- pre_shift: bfloat16 [12, 768], P(None, 'fsdp'), may hold values from -1.75 to 1.75
- w_qkv: bfloat16 [12, 768, 2304], P(None, 'fsdp'), may hold values from -0.3125 to 0.3125
- b_qv: bfloat16 [12, 1536], P(None, 'fsdp'), may hold values from -1.75 to 1.75
- w_out: bfloat16 [12, 768, 768], P(None, 'fsdp'), may hold values from -1.25 to 1.25
- b_out: bfloat16 [12, 768], P(None, 'fsdp'), may hold values from -1.75 to 1.75
- mid_gain: bfloat16 [12, 768], P(None, 'fsdp'), may hold values from 0.5 to 1.5
- mid_shift: bfloat16 [12, 768], P(None, 'fsdp'), may hold values from -1.75 to 1.75
- w_fc: bfloat16 [12, 768, 3072], P(None, 'fsdp'), may hold values from -0.21875 to 0.21875
- b_fc: bfloat16 [12, 3072], P(None, 'fsdp'), may hold values from -1.75 to 1.75
- w_proj: bfloat16 [12, 3072, 768], P(None, 'fsdp'), may hold values from -0.109375 to 0.109375
- b_proj: bfloat16 [12, 768], P(None, 'fsdp'), may hold values from -1.75 to 1.75
Outputs:
- block_output: bfloat16 [24576, 768], P(('rep', 'fsdp'))
- input_grad: float32 [24576, 768], P(('rep', 'fsdp'))
- dpre_gain: float32 [768], P('fsdp')
- dpre_shift: float32 [768], P('fsdp')
- dw_qkv: float32 [768, 2304], P('fsdp')
- db_qv: float32 [1536], P('fsdp')
- dw_out: float32 [768, 768], P('fsdp')
- db_out: float32 [768], P('fsdp')
- dmid_gain: float32 [768], P('fsdp')
- dmid_shift: float32 [768], P('fsdp')
- dw_fc: float32 [768, 3072], P('fsdp')
- db_fc: float32 [3072], P('fsdp')
- dw_proj: float32 [3072, 768], P('fsdp')
- db_proj: float32 [768], P('fsdp')
Inputs may be any that keep to these rules, and one draw needn't show every extreme that they name: `tie_index`: the entry of every bank that the block uses. `prefix_len`: row d holds, for each continuation on device d of rep+fsdp in order, how many of its group's first prompt tokens it attends to; on the last device of every group the last continuation attends to all 2048.
All inputs are finite; a program needn't handle non-finite values.
Results may differ from a plain program's by a relative error of at most 0.014.
Values may be sent and summed in bfloat16 or wider, within the bound.
A program may use at most 256 MiB of HBM per device.

v0:
```python
from functools import partial

import jax
import jax.numpy as jnp
from jax import lax
from jax.sharding import PartitionSpec as P

D = 768
HEADS = 12
HEAD = 64
GROUP_DEV = 4
CONT = 256
PROMPT_DEV = 512
CONT_DEV = 1


MASKED = -1e30


def partner_2(block, axis, apart):
    count = lax.axis_size(axis)
    route = []
    for low in range(count):
        high = low | 1 << apart
        if high != low and high < count:
            route += [(low, high), (high, low)]
    return lax.ppermute(block, axis, route)


def layer_norm(values, gain, shift):
    center = values - jnp.mean(values, axis=-1, keepdims=True)
    spread = jnp.mean(center * center, axis=-1, keepdims=True)
    return center * lax.rsqrt(spread + 1e-05) * gain + shift


def outer(left, right):
    return lax.dot_general(
        left, right, (((0,), (0,)), ((), ())), preferred_element_type=jnp.float32
    )


def by_heads(matrix):
    return matrix.reshape(matrix.shape[0], HEADS, HEAD).transpose(1, 0, 2)


def from_heads(stacked):
    return stacked.transpose(1, 0, 2).reshape(stacked.shape[1], HEADS * HEAD)


def head_forward(key_mask, members):
    head_q, head_k, head_v = members
    scores = jnp.einsum("qd,kd->qk", head_q, head_k, preferred_element_type=jnp.float32) * 0.125
    scores = jnp.where(key_mask, scores, MASKED)
    peak = jnp.max(scores, axis=1, keepdims=True)
    raised = jnp.exp(scores - peak)
    totals = jnp.sum(raised, axis=1, keepdims=True)
    weights = (raised / totals).astype(jnp.bfloat16)
    return (
        jnp.dot(weights, head_v, preferred_element_type=jnp.float32),
        (peak + jnp.log(totals))[:, 0],
    )


def head_backward(key_mask, members):
    head_q, head_k, head_v, head_grad, head_lse = members
    scores = jnp.einsum("qd,kd->qk", head_q, head_k, preferred_element_type=jnp.float32) * 0.125
    scores = jnp.where(key_mask, scores, MASKED)
    probs = jnp.exp(scores - head_lse[:, None])
    dprobs = jnp.einsum("qd,kd->qk", head_grad, head_v, preferred_element_type=jnp.float32)
    inner = jnp.sum(probs * dprobs, axis=1, keepdims=True)
    dscore = (probs * (dprobs - inner)).astype(jnp.bfloat16)
    grad_q = 0.125 * jnp.einsum("qk,kd->qd", dscore, head_k, preferred_element_type=jnp.float32)
    grad_k = 0.125 * jnp.einsum("qk,qd->kd", dscore, head_q, preferred_element_type=jnp.float32)
    grad_v = jnp.einsum(
        "qk,qd->kd", probs.astype(jnp.bfloat16), head_grad, preferred_element_type=jnp.float32
    )
    return (grad_q, grad_k, grad_v)


def attend_forward(queries, keys, values, key_mask):
    stacked, lse_rows = lax.map(
        partial(head_forward, key_mask), (by_heads(queries), by_heads(keys), by_heads(values))
    )
    return (from_heads(stacked), lse_rows)


def attend_backward(queries, keys, values, grad_out, lse_rows, key_mask):
    grad_q, grad_k, grad_v = lax.map(
        partial(head_backward, key_mask),
        (by_heads(queries), by_heads(keys), by_heads(values), by_heads(grad_out), lse_rows),
    )
    return (from_heads(grad_q), from_heads(grad_k), from_heads(grad_v))


def body(
    block_input,
    cotangent,
    tie_index,
    prefix_len,
    pre_gain,
    pre_shift,
    w_qkv,
    b_qv,
    w_out,
    b_out,
    mid_gain,
    mid_shift,
    w_fc,
    b_fc,
    w_proj,
    b_proj,
):
    chosen_index = tie_index[0]

    def chosen(bank):
        return lax.dynamic_index_in_dim(bank, chosen_index, 0, keepdims=False)

    gain_one, shift_one, qkv_part, bias_qv = (
        chosen(pre_gain),
        chosen(pre_shift),
        chosen(w_qkv),
        chosen(b_qv),
    )
    out_part, bias_out = (chosen(w_out), chosen(b_out))
    gain_two, shift_two, fc_part, bias_fc = (
        chosen(mid_gain),
        chosen(mid_shift),
        chosen(w_fc),
        chosen(b_fc),
    )
    proj_part, bias_proj = (chosen(w_proj), chosen(b_proj))
    gain_one, shift_one, qkv_full, bias_qv, out_full, bias_out = (
        lax.all_gather(gain_one, "fsdp", axis=0, tiled=True),
        lax.all_gather(shift_one, "fsdp", axis=0, tiled=True),
        lax.all_gather(qkv_part, "fsdp", axis=0, tiled=True),
        lax.all_gather(bias_qv, "fsdp", axis=0, tiled=True),
        lax.all_gather(out_part, "fsdp", axis=0, tiled=True),
        lax.all_gather(bias_out, "fsdp", axis=0, tiled=True),
    )
    group_pos = lax.axis_index("fsdp") % GROUP_DEV
    levels = GROUP_DEV.bit_length() - 1
    inputs = block_input.astype(jnp.float32)
    normed, norm_back = jax.vjp(
        layer_norm, inputs, gain_one.astype(jnp.float32), shift_one.astype(jnp.float32)
    )
    normed_low = normed.astype(jnp.bfloat16)
    mixed = jnp.dot(normed_low, qkv_full, preferred_element_type=jnp.float32)
    bias_float = bias_qv.astype(jnp.float32)
    queries = (mixed[:, :D] + bias_float[:D]).astype(jnp.bfloat16)
    keys = mixed[:, D : 2 * D].astype(jnp.bfloat16)
    values = (mixed[:, 2 * D :] + bias_float[D:]).astype(jnp.bfloat16)
    key_pair = jnp.stack([keys[:PROMPT_DEV], values[:PROMPT_DEV]])
    for level in range(levels):
        partner = partner_2(key_pair, "fsdp", level)
        lower_side = (group_pos >> level) % 2 == 0
        key_pair = jnp.where(
            lower_side,
            jnp.concatenate([key_pair, partner], axis=1),
            jnp.concatenate([partner, key_pair], axis=1),
        )
    prompt_rows = group_pos * PROMPT_DEV + jnp.arange(PROMPT_DEV)
    key_slots = jnp.arange(PROMPT_DEV * GROUP_DEV)
    prompt_mask = key_slots[None, :] <= prompt_rows[:, None]
    cont_rows = CONT_DEV * CONT
    which_cont = jnp.arange(cont_rows) // CONT
    place_cont = jnp.arange(cont_rows) % CONT
    reach_row = jnp.sum(
        jnp.where(which_cont[:, None] == jnp.arange(CONT_DEV)[None, :], prefix_len[0][None, :], 0),
        axis=1,
    )
    own_mask = (which_cont[:, None] == which_cont[None, :]) & (
        place_cont[None, :] <= place_cont[:, None]
    )
    cont_mask = jnp.concatenate([key_slots[None, :] < reach_row[:, None], own_mask], axis=1)
    cont_keys = jnp.concatenate([key_pair[0], keys[PROMPT_DEV:]], axis=0)
    cont_values = jnp.concatenate([key_pair[1], values[PROMPT_DEV:]], axis=0)
    prompt_out, prompt_lse = attend_forward(
        queries[:PROMPT_DEV], key_pair[0], key_pair[1], prompt_mask
    )
    cont_out, cont_lse = attend_forward(queries[PROMPT_DEV:], cont_keys, cont_values, cont_mask)
    attended = jnp.concatenate([prompt_out, cont_out], axis=0).astype(jnp.bfloat16)
    gain_two, shift_two, fc_full, bias_fc, proj_full, bias_proj = (
        lax.all_gather(gain_two, "fsdp", axis=0, tiled=True),
        lax.all_gather(shift_two, "fsdp", axis=0, tiled=True),
        lax.all_gather(fc_part, "fsdp", axis=0, tiled=True),
        lax.all_gather(bias_fc, "fsdp", axis=0, tiled=True),
        lax.all_gather(proj_part, "fsdp", axis=0, tiled=True),
        lax.all_gather(bias_proj, "fsdp", axis=0, tiled=True),
    )
    middle = (
        inputs
        + jnp.dot(attended, out_full, preferred_element_type=jnp.float32)
        + bias_out.astype(jnp.float32)
    )
    hidden_in, mid_back = jax.vjp(
        layer_norm, middle, gain_two.astype(jnp.float32), shift_two.astype(jnp.float32)
    )
    hidden_low = hidden_in.astype(jnp.bfloat16)
    gate = jnp.dot(hidden_low, fc_full, preferred_element_type=jnp.float32) + bias_fc.astype(
        jnp.float32
    )
    activ, gelu_back = jax.vjp(partial(jax.nn.gelu, approximate=True), gate)
    activ_low = activ.astype(jnp.bfloat16)
    output = (
        middle
        + jnp.dot(activ_low, proj_full, preferred_element_type=jnp.float32)
        + bias_proj.astype(jnp.float32)
    )
    fc_back, proj_back = (
        lax.all_gather(fc_part, "fsdp", axis=0, tiled=True),
        lax.all_gather(proj_part, "fsdp", axis=0, tiled=True),
    )
    grad_out = cotangent.astype(jnp.float32)
    dbias_proj = jnp.sum(grad_out, axis=0)
    dweight_proj = outer(activ_low, cotangent)
    grad_act = jnp.einsum("td,fd->tf", cotangent, proj_back, preferred_element_type=jnp.float32)
    (grad_gate,) = gelu_back(grad_act)
    gate_low = grad_gate.astype(jnp.bfloat16)
    dbias_fc = jnp.sum(gate_low.astype(jnp.float32), axis=0)
    dweight_fc = outer(hidden_low, gate_low)
    grad_hidden = jnp.einsum("tf,df->td", gate_low, fc_back, preferred_element_type=jnp.float32)
    grad_middle, dgain_two, dshift_two = mid_back(grad_hidden)
    grad_middle = grad_middle + grad_out
    mlp_a, mlp_b, mlp_c, mlp_d, mlp_e, mlp_f = (
        lax.psum_scatter(dgain_two, "fsdp", scatter_dimension=0, tiled=True),
        lax.psum_scatter(dshift_two, "fsdp", scatter_dimension=0, tiled=True),
        lax.psum_scatter(dweight_fc, "fsdp", scatter_dimension=0, tiled=True),
        lax.psum_scatter(dbias_fc, "fsdp", scatter_dimension=0, tiled=True),
        lax.psum_scatter(dweight_proj, "fsdp", scatter_dimension=0, tiled=True),
        lax.psum_scatter(dbias_proj, "fsdp", scatter_dimension=0, tiled=True),
    )
    qkv_back, out_back = (
        lax.all_gather(qkv_part, "fsdp", axis=0, tiled=True),
        lax.all_gather(out_part, "fsdp", axis=0, tiled=True),
    )
    branch_low = grad_middle.astype(jnp.bfloat16)
    dbias_out = jnp.sum(branch_low.astype(jnp.float32), axis=0)
    dweight_out = outer(attended, branch_low)
    grad_att = jnp.einsum(
        "td,ed->te", branch_low, out_back, preferred_element_type=jnp.float32
    ).astype(jnp.bfloat16)
    pq_grad, pk_grad, pv_grad = attend_backward(
        queries[:PROMPT_DEV],
        key_pair[0],
        key_pair[1],
        grad_att[:PROMPT_DEV],
        prompt_lse,
        prompt_mask,
    )
    cq_grad, ck_grad, cv_grad = attend_backward(
        queries[PROMPT_DEV:], cont_keys, cont_values, grad_att[PROMPT_DEV:], cont_lse, cont_mask
    )
    prompt_len = PROMPT_DEV * GROUP_DEV
    shared = jnp.stack([pk_grad + ck_grad[:prompt_len], pv_grad + cv_grad[:prompt_len]])
    for level in reversed(range(levels)):
        half_rows = shared.shape[1] // 2
        lower_half = shared[:, :half_rows]
        upper_half = shared[:, half_rows:]
        lower_side = (group_pos >> level) % 2 == 0
        outgoing = jnp.where(lower_side, upper_half, lower_half)
        kept_half = jnp.where(lower_side, lower_half, upper_half)
        shared = kept_half + partner_2(outgoing.astype(jnp.bfloat16), "fsdp", level).astype(
            outgoing.dtype
        )
    grad_keys = jnp.concatenate([shared[0], ck_grad[prompt_len:]], axis=0)
    grad_values = jnp.concatenate([shared[1], cv_grad[prompt_len:]], axis=0)
    grad_queries = jnp.concatenate([pq_grad, cq_grad], axis=0)
    grad_mixed = jnp.concatenate([grad_queries, grad_keys, grad_values], axis=1).astype(
        jnp.bfloat16
    )
    column_sums = jnp.sum(grad_mixed.astype(jnp.float32), axis=0)
    dbias_qv = jnp.concatenate([column_sums[:D], column_sums[2 * D :]])
    dweight_qkv = outer(normed_low, grad_mixed)
    grad_normed = jnp.einsum("te,de->td", grad_mixed, qkv_back, preferred_element_type=jnp.float32)
    grad_input, dgain_one, dshift_one = norm_back(grad_normed)
    grad_input = grad_input + grad_middle
    attn_a, attn_b, attn_c, attn_d, attn_e, attn_f = (
        lax.psum_scatter(dgain_one, "fsdp", scatter_dimension=0, tiled=True),
        lax.psum_scatter(dshift_one, "fsdp", scatter_dimension=0, tiled=True),
        lax.psum_scatter(dweight_qkv, "fsdp", scatter_dimension=0, tiled=True),
        lax.psum_scatter(dbias_qv, "fsdp", scatter_dimension=0, tiled=True),
        lax.psum_scatter(dweight_out, "fsdp", scatter_dimension=0, tiled=True),
        lax.psum_scatter(dbias_out, "fsdp", scatter_dimension=0, tiled=True),
    )
    summed = (
        lax.psum(attn_a.astype(jnp.bfloat16), "rep").astype(jnp.float32),
        lax.psum(attn_b.astype(jnp.bfloat16), "rep").astype(jnp.float32),
        lax.psum(attn_c.astype(jnp.bfloat16), "rep").astype(jnp.float32),
        lax.psum(attn_d.astype(jnp.bfloat16), "rep").astype(jnp.float32),
        lax.psum(attn_e.astype(jnp.bfloat16), "rep").astype(jnp.float32),
        lax.psum(attn_f.astype(jnp.bfloat16), "rep").astype(jnp.float32),
        lax.psum(mlp_a.astype(jnp.bfloat16), "rep").astype(jnp.float32),
        lax.psum(mlp_b.astype(jnp.bfloat16), "rep").astype(jnp.float32),
        lax.psum(mlp_c.astype(jnp.bfloat16), "rep").astype(jnp.float32),
        lax.psum(mlp_d.astype(jnp.bfloat16), "rep").astype(jnp.float32),
        lax.psum(mlp_e.astype(jnp.bfloat16), "rep").astype(jnp.float32),
        lax.psum(mlp_f.astype(jnp.bfloat16), "rep").astype(jnp.float32),
    )
    return (
        output.astype(jnp.bfloat16),
        grad_input,
        summed[0],
        summed[1],
        summed[2],
        summed[3],
        summed[4],
        summed[5],
        summed[6],
        summed[7],
        summed[8],
        summed[9],
        summed[10],
        summed[11],
    )


def solution(mesh):
    return jax.shard_map(
        body,
        mesh=mesh,
        in_specs=(
            P(("rep", "fsdp"), None),
            P(("rep", "fsdp"), None),
            P(),
            P(("rep", "fsdp"), None),
            P(None, "fsdp"),
            P(None, "fsdp"),
            P(None, "fsdp", None),
            P(None, "fsdp"),
            P(None, "fsdp", None),
            P(None, "fsdp"),
            P(None, "fsdp"),
            P(None, "fsdp"),
            P(None, "fsdp", None),
            P(None, "fsdp"),
            P(None, "fsdp", None),
            P(None, "fsdp"),
        ),
        out_specs=(
            P(("rep", "fsdp"), None),
            P(("rep", "fsdp"), None),
            P("fsdp"),
            P("fsdp"),
            P("fsdp", None),
            P("fsdp"),
            P("fsdp", None),
            P("fsdp"),
            P("fsdp"),
            P("fsdp"),
            P("fsdp", None),
            P("fsdp"),
            P("fsdp", None),
            P("fsdp"),
        ),
        check_vma=False,
    )
```

profile of v0, /device:TPU:0, one launch (start us, length us, event | category | flops | bytes accessed | tf_op | source)
XLA Modules:
  0.0 1080.0 jit_solution(15808150474617322025)
XLA Ops:
  21.0 63.5 %all-reduce.17 = (bf16[1536]{0:T(1024)(128)(2,1)S(1)}, bf16[768]{0:T(1024)(128)(2,1)S(1)}, bf16[768]{0:T(1024)(128)(2,1)S(1)}, bf16[768]{0:T(1024)(128)(2,1)S(1)...) all-reduce(bf16[1536]{0:T(1024)(128)(2,1)S(1)} %dynamic-update-slic, ...), channel_id=5, replica_groups=mesh['rep'=2,'fsdp'=16] {'fsdp'}, use_global_device_ids=true, to_apply=%add.2 | all-reduce | flops 9216 | bytes 36864
  86.8 5.1 fusion.156
  96.0 3.7 collective-permute-done
  99.7 3.6 maximum_select_fusion.1
  118.2 74.6 %collective-permute-done.1 = bf16[2,1024,768]{2,1,0:T(8,128)(2,1)} collective-permute-done((bf16[2,1024,768]{2,1,0:T(8,128)(2,1)}, bf16[2,1024,768]{2,1,0:T(8,128)(2,1)}, u32[]{:S(2)}, u32[]{:S(2)}) %collective-permute-start.1) | collective-permute-done | bytes 3145760 | tf_op jit(solution)/shard_map/ppermute | solution.py:27
  192.7 5.7 maximum_select_fusion
  201.5 4.9 copy.80
  206.4 6.6 copy.83
  213.0 4.8 copy.81
  217.8 6.6 copy.84
  224.4 112.6 %while.56 = (s32[]{:T(128)}, bf16[12,512,64]{1,2,0:T(8,128)(2,1)S(1)}, f32[12,512]{1,0:T(8,128)}, bf16[12,512,64]{2,1,0:T(8,128)(2,1)}, bf16[12,2048,64]{2,1,0:T...) while((s32[]{:T(128)}, ...), condition=%wide.region_5.6_spmd.clone, body=%wide.region_2.5_spmd.clone.sunk | while | flops 277872128 | bytes 30695548 | solution.py:81
  230.5 3.3 fusion.221
  239.9 3.3 fusion.221
  249.3 3.3 fusion.221
  258.6 3.3 fusion.221
  268.0 3.3 fusion.221
  277.4 3.3 fusion.221
  286.8 3.3 fusion.221
  296.2 3.3 fusion.221
  305.5 3.3 fusion.221
  314.9 3.3 fusion.221
  324.3 3.3 fusion.221
  333.7 3.3 fusion.221
  337.0 4.2 maximum_bitcast_fusion.1
  341.2 7.9 copy.90
  349.2 4.0 maximum_bitcast_fusion
  353.2 7.9 copy.89
  361.9 79.2 %while.54 = (s32[]{:T(128)}, bf16[12,256,64]{1,2,0:T(8,128)(2,1)}, f32[12,256]{1,0:T(8,128)}, bf16[12,256,64]{2,1,0:T(8,128)(2,1)}, bf16[12,2304,64]{2,1,0:T(8,1...) while((s32[]{:T(128)}, bf16[12,256,64]{1,2,0:T(8,128)(2,1)}, ...), condition=%wide.region_9.10_spmd, body=%wide.region_6.9_spmd.sunk | while | flops 155713280 | bytes 8990817 | solution.py:81
  445.0 9.4 fusion.101
  454.4 13.9 %convert_reduce_fusion = (f32[3072]{0:T(1024)}, bf16[768,3072]{1,0:T(8,128)(2,1)S(1)}) fusion(f32[768,3072]{1,0:T(8,128)} %fusion.101, f32[3072]{0:T(1024)} %convert_element_type.235, bf16[768,768]{1,0:T(8,128)(2,1)S(1)} %copy-done.29, bf16[1,3072,768]{2,1,0:T(8,128)(2,1)} %all-gather.23.cloned.1.call-done), kind=kOutput, calls=%fused_computation.122 | convolution fusion | flops 3678139392 | bytes 20078592 | tf_op jit(solution)/shard_map/td,fd->tf/dot_general | solution.py:216
  468.3 5.9 fusion.159
  477.3 3.1 multiply_reduce_fusion.2
  492.5 9.0 fusion.147
  502.2 144.9 %while.57 = (s32[]{:T(128)}, bf16[12,512,64]{1,2,0:T(8,128)(2,1)S(1)}, f32[12,2048,64]{1,2,0:T(8,128)}, f32[12,2048,64]{1,2,0:T(8,128)}, bf16[12,512,64]{2,1,0:T...) while((s32[]{:T(128)}, ...), condition=%wide.region_16.17_spmd.clone, body=%wide.region_14.16_spmd.clone.sunk | while | flops 681737728 | bytes 34751600 | solution.py:88
  648.3 13.5 %fusion.148 = f32[3072,768]{1,0:T(8,128)} fusion(bf16[768,768]{1,0:T(8,128)(2,1)} %param.25, f32[768,3072]{1,0:T(8,128)} %fusion.101, f32[3072]{0:T(1024)S(1)} %copy-done.48), kind=kOutput, calls=%fused_computation.251 | convolution fusion | flops 3647471616 | bytes 20066304 | tf_op jit(solution)/shard_map/dot_general | solution.py:37
  662.6 136.3 %while.55 = (s32[]{:T(128)}, bf16[12,256,64]{1,2,0:T(8,128)(2,1)}, f32[12,2304,64]{1,2,0:T(8,128)}, f32[12,2304,64]{1,2,0:T(8,128)}, bf16[12,256,64]{2,1,0:T(8,1...) while((s32[]{:T(128)}, bf16[12,256,64]{1,2,0:T(8,128)(2,1)}, ...), condition=%wide.region_19.20_spmd, body=%wide.region_17.19_spmd.sunk | while | flops 382959360 | bytes 21571696 | solution.py:88
  799.0 5.9 slice_add_fusion.1
  804.9 5.9 slice_add_fusion
  812.9 68.7 %collective-permute-done.2 = bf16[2,1024,768]{1,2,0:T(8,128)(2,1)S(1)} collective-permute-done((bf16[2,1024,768]{1,2,0:T(8,128)(2,1)S(1)}, bf16[2,1024,768]{1,2,0:T(8,128)(2,1)S(1)}, u32[]{:S(2)}, u32[]{:S(2)}) %collective-permute-start.2) | collective-permute-done | bytes 3145760 | tf_op jit(solution)/shard_map/ppermute | solution.py:27
  890.4 6.0 fusion.144
  899.4 12.0 %add_convert_fusion.1 = bf16[768,768]{0,1:T(8,128)(2,1)} fusion(f32[768,768]{0,1:T(8,128)S(1)} %copy-done.6, bf16[1,3072,768]{2,1,0:T(8,128)(2,1)} %all-gather.23.cloned.1.call-done, f32[768]{0:T(1024)S(1)} %convert_element_type.236, f32[768,3072]{1,0:T(8,128)} %fusion.101, f32[3072]{0:T(1024)} %convert_element_type.235), kind=kOutput, calls=%fused_computation.177 | convolution fusion | flops 3649241088 | bytes 17710080 | tf_op jit(solution)/shard_map/dot_general | solution.py:206
  915.5 8.1 fusion.158
  928.3 11.6 %convert_reduce_fusion.1 = f32[2304]{0:T(1024)} fusion(bf16[256,768]{0,1:T(8,128)(2,1)S(1)} %bitcast.337, bf16[512,768]{0,1:T(8,128)(2,1)S(1)} %copy-done.16, bf16[256,768]{0,1:T(8,128)(2,1)S(1)} %bitcast.334, bf16[512,768]{0,1:T(8,128)(2,1)S(1)} %copy-done.14, bf16[256,768]{0,1:T(8,128)(2,1)S(1)} %bitcast.340, bf16[512,768]{0,1:T(8,128)(2,1)S(1)} %bitcast.327), kind=kLoop, calls=%fused_computation.124 | loop fusion | flops 23000832 | bytes 3548160 | tf_op jit(solution)/shard_map/reduce_sum | solution.py:271
  943.5 40.5 %reduce-scatter.5.cloned.1.call-done = f32[48,2304]{1,0:T(8,128)} async-done(((f32[768,2304]{1,0:T(8,128)}), f32[48,2304]{1,0:T(8,128)}) %reduce-scatter.5.cloned.1.call-update) | async-done | bytes 442384 | tf_op jit(solution)/shard_map/reduce_scatter | solution.py:280
  987.8 5.1 convert_reduce_fusion.3
  992.9 60.5 %all-reduce.16 = (bf16[768]{0:T(1024)(128)(2,1)S(1)}, bf16[768]{0:T(1024)(128)(2,1)S(1)}, bf16[1536]{0:T(1024)(128)(2,1)S(1)}, bf16[768]{0:T(1024)(128)(2,1)S(1)...) all-reduce(f32[768]{0:T(1024)} %get-tuple-element.360, ...), channel_id=14, replica_groups=mesh['rep'=2,'fsdp'=16] {'fsdp'}, use_global_device_ids=true, to_apply=%region_23.24.clone | all-reduce | flops 9216 | bytes 55296
  1054.0 4.9 all-reduce.18
  1063.1 3.2 copy.106
  (562 shorter events, 528.5 us)
Async XLA Ops:
  7.2 4.4 copy-start
  7.2 79.6 %all-gather.17.cloned.1.call-start = ((), (), s32[]{:S(2)}) async-start(), calls=%async_computation.8 | async-start | bytes 3760128 | tf_op jit(solution)/shard_map/all_gather | solution.py:135
  9.9 431.1 %all-gather.19.cloned.1.call-start = ((), (), s32[]{:S(2)}) async-start(), calls=%async_computation.9 | async-start | bytes 1253376 | tf_op jit(solution)/shard_map/all_gather | solution.py:137
  11.5 433.5 %all-gather.21.cloned.1.call-start = ((), (), s32[]{:S(2)}) async-start(), calls=%async_computation.10 | async-start | bytes 5013504 | tf_op jit(solution)/shard_map/all_gather | solution.py:185
  12.3 442.1 %all-gather.23.cloned.1.call-start = ((), (), s32[]{:S(2)}) async-start(), calls=%async_computation.11 | async-start | bytes 5013504 | tf_op jit(solution)/shard_map/all_gather | solution.py:187
  84.5 7.4 copy-start.39
  84.5 7.4 copy-start.49
  86.1 355.0 %copy-start.3 = (bf16[768,768]{0,1:T(8,128)(2,1)}, bf16[768,768]{0,1:T(8,128)(2,1)S(1)}, u32[]{:S(2)}) copy-start(bf16[768,768]{0,1:T(8,128)(2,1)S(1)} %copy.78) | copy-start | bytes 3538948
  86.3 5.6 copy-start.35
  86.7 5.2 copy-start.44
  86.7 5.2 copy-start.41
  91.9 2.7 copy-start.33
  96.0 3.8 collective-permute-start
  103.3 89.4 %collective-permute-start.1 = (bf16[2,1024,768]{2,1,0:T(8,128)(2,1)}, bf16[2,1024,768]{2,1,0:T(8,128)(2,1)}, u32[]{:S(2)}, u32[]{:S(2)}) collective-permute-start(bf16[2,1024,768]{2,1,0:T(8,128)(2,1)} %maximum_select_fusion.1), channel_id=1, source_target_pairs={{0,2},{2,0},{1,3},{3,1},{4,6},{6,4},{5,7},{7,5},{8,10},{10,8},{9,1... | collective-permute-start | bytes 9437192 | tf_op jit(solution)/shard_map/ppermute | solution.py:27
  105.0 8.8 copy-start.10
  105.0 808.8 %reduce-scatter.7.cloned.1.call-start = ((), (), s32[]{:S(2)}) async-start(), calls=%async_computation.5 | async-start | bytes 2506752 | tf_op jit(solution)/shard_map/reduce_scatter | solution.py:282
  337.0 4.3 copy-start.31
  337.0 4.3 copy-start.37
  443.9 48.7 %copy-start.5 = (f32[768,768]{0,1:T(8,128)}, f32[768,768]{0,1:T(8,128)S(1)}, u32[]{:S(2)}) copy-start(f32[768,768]{0,1:T(8,128)S(1)} %get-tuple-element.487) | copy-start | bytes 7077892
  445.0 9.4 copy-start.29
  454.4 13.9 %copy-start.12 = (bf16[1,768,3072]{2,1,0:T(8,128)(2,1)S(1)}, bf16[1,768,3072]{2,1,0:T(8,128)(2,1)}, u32[]{:S(2)}) copy-start(bf16[1,768,3072]{2,1,0:T(8,128)(2,1)} %all-gather.21.cloned.1.call-done) | copy-start | bytes 14155780
  468.3 6.0 copy-start.52
  477.3 3.1 copy-start.47
  477.3 3.1 copy-start.8
  481.1 3.5 copy-start.32
  481.1 3.5 copy-start.34
  481.2 2.4 copy-start.43
  484.6 2.7 copy-start.51
  487.2 452.7 %reduce-scatter.9.cloned.1.call-start = ((), (), s32[]{:S(2)}) async-start(), calls=%async_computation.6 | async-start | bytes 10027008 | tf_op jit(solution)/shard_map/reduce_scatter | solution.py:227
  501.5 440.2 %reduce-scatter.11.cloned.1.call-start = ((), (), s32[]{:S(2)}) async-start(), calls=%async_computation.7 | async-start | bytes 10027008 | tf_op jit(solution)/shard_map/reduce_scatter | solution.py:229
  502.2 144.9 %slice-start = ((bf16[768,768]{0,1:T(8,128)(2,1)}), bf16[256,768]{0,1:T(8,128)(2,1)S(1)}, s32[]{:S(2)}) async-start(bf16[768,768]{0,1:T(8,128)(2,1)} %copy-done.22), calls=%async_computation.13 | async-start | bytes 786432 | tf_op jit(solution)/shard_map/slice | solution.py:251
  502.2 146.1 %copy-start.48 = (f32[3072]{0:T(1024)S(1)}, f32[3072]{0:T(1024)}, u32[]{:S(2)}) copy-start(f32[3072]{0:T(1024)} %convert_element_type.235) | copy-start | bytes 36868
  647.1 14.7 %copy-start.17 = (bf16[12,512,64]{1,2,0:T(8,128)(2,1)}, bf16[12,512,64]{1,2,0:T(8,128)(2,1)S(1)}, u32[]{:S(2)}) copy-start(bf16[12,512,64]{1,2,0:T(8,128)(2,1)S(1)} %get-tuple-element.201) | copy-start | bytes 2359300
  661.8 322.3 %reduce-scatter.5.cloned.1.call-start = ((), (), s32[]{:S(2)}) async-start(), calls=%async_computation.4 | async-start | bytes 7520256 | tf_op jit(solution)/shard_map/reduce_scatter | solution.py:280
  811.9 69.7 %collective-permute-start.2 = (bf16[2,1024,768]{1,2,0:T(8,128)(2,1)S(1)}, bf16[2,1024,768]{1,2,0:T(8,128)(2,1)S(1)}, u32[]{:S(2)}, u32[]{:S(2)}) collective-permute-start(bf16[2,1024,768]{1,2,0:T(8,128)(2,1)S(1)} %select_convert_fusion), channel_id=1, source_target_pairs={{0,2},{2,0},{1,3},{3,1},{4,6},{6,4},{5,7},{7,5},{8,10},{10,8},{9,1... | collective-permute-start | bytes 9437192 | tf_op jit(solution)/shard_map/ppermute | solution.py:27
  883.8 3.5 collective-permute-start.3
  885.1 3.4 copy-start.23
  888.3 2.1 copy-start.27
  888.5 8.0 copy-start.13
  896.5 2.9 copy-start.6
  896.5 169.8 %all-reduce.22.cloned.1.call-start = ((), (), s32[]{:S(2)}) async-start(), calls=%async_computation.12 | async-start | bytes 1769472 | tf_op jit(solution)/shard_map/psum | solution.py:288
  926.0 2.3 copy-start.14
  926.0 2.3 copy-start.16
  926.0 2.3 copy-start.19
  926.0 2.3 copy-start.24
  926.0 2.3 copy-start.26
  926.0 2.3 copy-start.28
  1063.1 10.1 copy-start.1
  (30 other events, 51.5 us)
Sparse Core Ops, SparseCore 0:
  10.9 50.0 all-gather.16
  63.9 37.3 all-gather.18
  103.5 67.8 all-gather.20
  173.5 54.2 all-gather.22
  487.4 60.3 reduce-scatter.6
  552.3 110.3 reduce-scatter.8
  666.8 111.1 reduce-scatter.10
  896.6 87.4 reduce-scatter.4
  987.7 36.5 all-reduce.21
where the time goes:
time: 1100 us; the launch traced here: 1080 us
  matrix products  458 us (42%)
  waiting for transfers between devices  189 us (17%)
  local copies, waits for them, and re-layouts  166 us (15%)
  blocking collectives  129 us (12%)
  other arithmetic  115 us (10%)
  between operations  20.4 us (2%)
    ppermute x4, waiting for transfers between devices, partner_2(): return lax.ppermute(block, axis, route)  148 us
    unnamed x2, blocking collectives  124 us
    dot_general x24, matrix products, head_forward(): jnp.dot(weights, head_v, preferred_element_type=jnp.float32)  67.4 us
    dot_general x24, matrix products, head_backward(): jnp.einsum('qd,kd->qk', head_q, head_k, preferred_element_type=jnp.float32)  59.8 us
    dot_general x24, matrix products, head_backward(): jnp.einsum('qk,qd->kd', probs.astype(jnp.bfloat16), head_grad, preferred_...  51.6 us
    dot_general x24, matrix products, head_backward(): jnp.einsum('qk,qd->kd', dscore, head_q, preferred_element_type=jnp.float32)  51.5 us
    dot_general x24, matrix products, head_backward(): jnp.einsum('qk,kd->qd', dscore, head_k, preferred_element_type=jnp.float32)  48.2 us
    dot_general x24, matrix products, head_forward(): jnp.einsum('qd,kd->qk', head_q, head_k, preferred_element_type=jnp.float32)  47.5 us
  transfers between devices with their start and end apart: 13, of which 5 were waited for; matrix products, arithmetic and copies ran while one was open for 62% of the time, Pallas kernels for 0%

commit v1 on v0

v1 whole, which is shorter than its diff:
```python
from functools import partial

import jax
import jax.numpy as jnp
from jax import lax
from jax.experimental import pallas as pl
from jax.experimental.pallas import tpu as pltpu
from jax.sharding import PartitionSpec as P

D = 768
HEADS = 12
HEAD = 64
FF = 3072
GROUP = 4
PROMPT = 512
CONT = 256
TOK = 768
ROWS = GROUP * TOK
OWN = HEADS // GROUP
SLICE = OWN * HEAD
WIDE = 3 * SLICE
PAIR = TOK // 2
CHUNK = 256
NEG = -1e30
EPS = 1e-5
GELU_A = 0.7978845608028654
GELU_B = 0.044715

f32 = jnp.float32
bf16 = jnp.bfloat16
MESH = pl.DeviceIdType.MESH
ANY = pl.BlockSpec(memory_space=pl.ANY)


def params(mib, **more):
    return pltpu.CompilerParams(vmem_limit_bytes=mib << 20, **more)


def dot(a, b):
    return jnp.dot(a, b, preferred_element_type=f32)


def dot_nt(a, b):
    return lax.dot_general(a, b, (((1,), (1,)), ((), ())), preferred_element_type=f32)


def dot_tn(a, b):
    return lax.dot_general(a, b, (((0,), (0,)), ((), ())), preferred_element_type=f32)


def moments(x):
    center = x - jnp.mean(x, axis=-1, keepdims=True)
    scale = lax.rsqrt(jnp.mean(center * center, axis=-1, keepdims=True) + EPS)
    return center * scale, scale


def greet(peers):
    sem = pltpu.get_barrier_semaphore()
    for peer in peers:
        pl.semaphore_signal(sem, inc=1, device_id={"fsdp": peer}, device_id_type=MESH)
    pl.semaphore_wait(sem, len(peers))


def gather_kernel(n, parts, x_ref, w_ref, xg_ref, wg_ref, xs, xr, ws, wr, local):
    me = lax.axis_index("fsdp")
    pos = lax.rem(me, GROUP)
    near, far = me ^ 1, me ^ 2
    greet([me ^ i for i in range(1, n)])
    own = pltpu.make_async_copy(x_ref, xg_ref.at[pos], local.at[0])
    own.start()
    own_w = pltpu.make_async_copy(w_ref.at[pos], wg_ref.at[me], local.at[1])
    own_w.start()
    rows = TOK // parts

    def piece(src, slot, part, i, peer):
        at = pl.ds(part * rows, rows)
        return pltpu.make_async_remote_copy(
            src_ref=src.at[at],
            dst_ref=xg_ref.at[slot, at],
            send_sem=xs.at[i],
            recv_sem=xr.at[i],
            device_id={"fsdp": peer},
            device_id_type=MESH,
        )

    across = [piece(x_ref, pos, part, part, far) for part in range(parts)]
    for copy in across:
        copy.start()
    beside = pltpu.make_async_remote_copy(
        src_ref=x_ref,
        dst_ref=xg_ref.at[pos],
        send_sem=xs.at[2 * parts],
        recv_sem=xr.at[2 * parts],
        device_id={"fsdp": near},
        device_id_type=MESH,
    )
    beside.start()
    slices = []
    for i in range(1, n):
        peer = me ^ i
        copy = pltpu.make_async_remote_copy(
            src_ref=w_ref.at[lax.rem(peer, GROUP)],
            dst_ref=wg_ref.at[me],
            send_sem=ws.at[i],
            recv_sem=wr.at[i],
            device_id={"fsdp": peer},
            device_id_type=MESH,
        )
        copy.start()
        slices.append(copy)
    passed = []
    for part in range(parts):
        across[part].wait_recv()
        copy = piece(xg_ref.at[pos ^ 2], pos ^ 2, part, parts + part, near)
        copy.start()
        passed.append(copy)
    for copy in across:
        copy.wait_send()
    beside.wait()
    own.wait()
    own_w.wait()
    for copy in passed + slices:
        copy.wait()


def gather_group(n, x, pieces):
    parts = 4
    dma = pltpu.SemaphoreType.DMA
    return pl.pallas_call(
        partial(gather_kernel, n, parts),
        name="gather_group",
        out_shape=(
            jax.ShapeDtypeStruct((GROUP,) + x.shape, x.dtype),
            jax.ShapeDtypeStruct((n,) + pieces.shape[1:], pieces.dtype),
        ),
        in_specs=[ANY, ANY],
        out_specs=(ANY, ANY),
        scratch_shapes=[
            dma((2 * parts + 1,)),
            dma((2 * parts + 1,)),
            dma((n,)),
            dma((n,)),
            dma((2,)),
        ],
        compiler_params=params(32, collective_id=0, has_side_effects=True),
    )(x, pieces)


def swap_kernel(count, x_ref, o_ref, send, recv, local):
    me = lax.axis_index("fsdp")
    greet([me ^ i for i in range(1, count)])
    slot = lax.rem(me, count)
    own = pltpu.make_async_copy(x_ref.at[slot], o_ref.at[slot], local)
    own.start()
    copies = []
    for i in range(1, count):
        copy = pltpu.make_async_remote_copy(
            src_ref=x_ref.at[slot ^ i],
            dst_ref=o_ref.at[slot],
            send_sem=send.at[i],
            recv_sem=recv.at[i],
            device_id={"fsdp": me ^ i},
            device_id_type=MESH,
        )
        copy.start()
        copies.append(copy)
    own.wait()
    for copy in copies:
        copy.wait()


def swap(x, collective_id, name):
    count = x.shape[0]
    dma = pltpu.SemaphoreType.DMA
    return pl.pallas_call(
        partial(swap_kernel, count),
        name=name,
        out_shape=jax.ShapeDtypeStruct(x.shape, x.dtype),
        in_specs=[ANY],
        out_specs=ANY,
        scratch_shapes=[dma((count,)), dma((count,)), dma],
        compiler_params=params(32, collective_id=collective_id, has_side_effects=True),
    )(x)


def project_kernel(x_ref, w_ref, g_ref, s_ref, b_ref, a_ref, q_ref, k_ref, v_ref):
    n, _ = moments(x_ref[...].astype(f32))
    a_low = (n * g_ref[...] + s_ref[...]).astype(bf16)
    a_ref[...] = a_low
    mixed = (dot(a_low, w_ref[...]) + b_ref[...]).astype(bf16)
    ones = jnp.ones((x_ref.shape[0], HEAD), bf16)
    for h in range(OWN):
        q = mixed[:, h * HEAD : (h + 1) * HEAD] * 0.125
        k = mixed[:, SLICE + h * HEAD : SLICE + (h + 1) * HEAD]
        v = mixed[:, 2 * SLICE + h * HEAD : 2 * SLICE + (h + 1) * HEAD]
        q_ref[h] = jnp.concatenate([q.astype(bf16), jnp.zeros_like(ones)], axis=1)
        k_ref[h] = jnp.concatenate([k, ones], axis=1)
        v_ref[h] = jnp.concatenate([v, ones], axis=1)


def project(x, w, gain, shift, bias):
    tile = 384
    heads = jax.ShapeDtypeStruct((OWN, ROWS, 2 * HEAD), bf16)
    head_spec = pl.BlockSpec((OWN, tile, 2 * HEAD), lambda i: (0, i, 0))
    whole = lambda i: (0, 0)
    return pl.pallas_call(
        project_kernel,
        name="project",
        grid=(ROWS // tile,),
        out_shape=(jax.ShapeDtypeStruct((ROWS, D), bf16), heads, heads, heads),
        in_specs=[
            pl.BlockSpec((tile, D), lambda i: (i, 0)),
            pl.BlockSpec((D, WIDE), whole),
            pl.BlockSpec((1, D), whole),
            pl.BlockSpec((1, D), whole),
            pl.BlockSpec((1, WIDE), whole),
        ],
        out_specs=(pl.BlockSpec((tile, D), lambda i: (i, 0)), head_spec, head_spec, head_spec),
        compiler_params=params(48),
    )(x, w, gain, shift, bias)


def lanes(rows):
    return lax.broadcasted_iota(jnp.int32, (rows, 2 * HEAD), 1)


def split_columns(base, lane, column):
    hi = column.astype(bf16).astype(f32)
    mid = (column - hi).astype(bf16).astype(f32)
    low = column - hi - mid
    tail = jnp.where(lane == HEAD, -hi, jnp.where(lane == HEAD + 1, -mid, -low))
    return jnp.where(lane < HEAD, base, jnp.where(lane < HEAD + 3, tail, 0.0)).astype(bf16)


def below(rows, cols, low_key):
    row = lax.broadcasted_iota(jnp.int32, (rows, cols), 0)
    col = lax.broadcasted_iota(jnp.int32, (rows, cols), 1)
    return row <= col if low_key else col <= row


def attend_kernel(reach_ref, q_ref, k_ref, v_ref, o_ref, f_ref, x_ref):
    T = CONT
    lane = lanes(T)
    causal = below(T, T, False)

    def tile(at, blocks):
        q = q_ref[0, pl.ds(at, T), :]
        scores = []
        for start, size, mask in blocks:
            s = dot_nt(q, k_ref[0, pl.ds(start, size), :])
            scores.append(s if mask is None else jnp.where(mask, s, NEG))
        peak = scores[0].max(axis=1, keepdims=True)
        for s in scores[1:]:
            peak = jnp.maximum(peak, s.max(axis=1, keepdims=True))
        total = jnp.zeros((T, 2 * HEAD), f32)
        for s, (start, size, _) in zip(scores, blocks):
            total += dot(jnp.exp(s - peak).astype(bf16), v_ref[0, pl.ds(start, size), :])
        mass = total[:, HEAD : HEAD + 1]
        f_ref[0, pl.ds(at, T), :] = total / mass
        lse = peak + jnp.log(mass)
        x_ref[0, pl.ds(at, T), :] = split_columns(q.astype(f32), lane, lse)

    for p in range(GROUP):
        past = [(i * TOK, PROMPT, None) for i in range(p)]
        base = p * TOK
        tile(base, past + [(base, T, causal)])
        tile(base + T, past + [(base, T, None), (base + T, T, causal)])

    def cont(c, carry):
        at = pl.multiple_of(c * TOK + PROMPT, CONT)
        reach = reach_ref[c]
        col = lax.broadcasted_iota(jnp.int32, (T, PROMPT), 1)
        blocks = [(i * TOK, PROMPT, col < reach - i * PROMPT) for i in range(GROUP)]
        tile(at, blocks + [(at, T, causal)])
        return carry

    lax.fori_loop(0, GROUP, cont, 0)

    half = lanes(PAIR) < HEAD
    for p in range(GROUP):
        top = f_ref[0, p * TOK : p * TOK + PAIR, :]
        low = f_ref[0, p * TOK + PAIR : (p + 1) * TOK, :]
        o_ref[p, 0] = jnp.where(half, top, pltpu.roll(low, HEAD, 1)).astype(bf16)


def attend(reach, q, k, v):
    head = lambda h: (h, 0, 0)
    spec = pl.BlockSpec((1, ROWS, 2 * HEAD), head)
    return pl.pallas_call(
        attend_kernel,
        name="attend",
        grid=(OWN,),
        out_shape=(
            jax.ShapeDtypeStruct((GROUP, OWN, PAIR, 2 * HEAD), bf16),
            jax.ShapeDtypeStruct((OWN, ROWS, 2 * HEAD), f32),
            jax.ShapeDtypeStruct((OWN, ROWS, 2 * HEAD), bf16),
        ),
        in_specs=[pl.BlockSpec(memory_space=pltpu.SMEM), spec, spec, spec],
        out_specs=(
            pl.BlockSpec((GROUP, 1, PAIR, 2 * HEAD), lambda h: (0, h, 0, 0)),
            spec,
            spec,
        ),
        compiler_params=params(56),
    )(reach, q, k, v)


def attend_back_kernel(
    reach_ref, q_ref, k_ref, v_ref, f_ref, g_ref, dq_ref, dk_ref, dv_ref, g_s, dq_s, kt_s, dk_s, dv_s
):
    T = CONT
    half = lanes(PAIR) < HEAD
    lane = lanes(PAIR)
    for p in range(GROUP):
        packed = g_ref[p, 0].astype(f32)
        for i, block in enumerate((packed, pltpu.roll(packed, HEAD, 1))):
            at = p * TOK + i * PAIR
            prod = jnp.where(half, block * f_ref[0, at : at + PAIR, :], 0.0)
            inner = jnp.sum(prod, axis=1, keepdims=True)
            g_s[at : at + PAIR, :] = split_columns(block, lane, inner)
        kt_s[:, p * TOK : (p + 1) * TOK] = k_ref[0, p * TOK : (p + 1) * TOK, :].T[:HEAD]
    dq_s[...] = jnp.zeros_like(dq_s)

    def block(keys, size, rows, count, mask, first, key_at):
        kb = k_ref[0, pl.ds(keys, size), :]
        vb = v_ref[0, pl.ds(keys, size), :]
        q = q_ref[0, pl.ds(rows, count), :]
        g = g_s[pl.ds(rows, count), :]
        probs = jnp.exp(dot_nt(kb, q))
        if mask is not None:
            probs = jnp.where(mask, probs, 0.0)
        ds = (probs * dot_nt(vb, g)).astype(bf16)
        dv = dot(probs.astype(bf16), g)
        dk = dot(ds, q)
        at = pl.ds(key_at, size)
        dv_s[at, :] = dv if first else dv_s[at, :] + dv
        dk_s[at, :] = dk if first else dk_s[at, :] + dk
        dq_s[:, pl.ds(rows, count)] += dot(kt_s[:, pl.ds(keys, size)], ds)

    causal = below(T, T, True)
    for p in range(GROUP):
        base = p * TOK
        block(base, T, base, T, causal, True, 0)
        block(base + T, T, base + T, T, causal, True, T)
        block(base, T, base + T, T, None, False, 0)

        def later(i, carry):
            rows = pl.multiple_of(i * TOK, CONT)
            block(base, PROMPT, rows, PROMPT, None, False, 0)
            return carry

        lax.fori_loop(p + 1, GROUP, later, 0)

        def cont(c, carry):
            rows = pl.multiple_of(c * TOK + PROMPT, CONT)
            key = lax.broadcasted_iota(jnp.int32, (PROMPT, T), 0)
            block(base, PROMPT, rows, T, key < reach_ref[c] - p * PROMPT, False, 0)
            return carry

        lax.fori_loop(0, GROUP, cont, 0)
        dk_ref[0, base : base + PROMPT, :] = dk_s[:, :HEAD].astype(bf16)
        dv_ref[0, base : base + PROMPT, :] = dv_s[:, :HEAD].astype(bf16)

    def own(c, carry):
        at = pl.multiple_of(c * TOK + PROMPT, CONT)
        block(at, T, at, T, causal, True, 0)
        dk_ref[0, pl.ds(at, T), :] = dk_s[:T, :HEAD].astype(bf16)
        dv_ref[0, pl.ds(at, T), :] = dv_s[:T, :HEAD].astype(bf16)
        return carry

    lax.fori_loop(0, GROUP, own, 0)
    for i in range(ROWS // PROMPT):
        at = i * PROMPT
        dq_ref[0, at : at + PROMPT, :] = (dq_s[:, at : at + PROMPT].T * 0.125).astype(bf16)


def attend_back(reach, q, k, v, f, g):
    head = lambda h: (h, 0, 0)
    spec = pl.BlockSpec((1, ROWS, 2 * HEAD), head)
    out = jax.ShapeDtypeStruct((OWN, ROWS, HEAD), bf16)
    out_spec = pl.BlockSpec((1, ROWS, HEAD), head)
    return pl.pallas_call(
        attend_back_kernel,
        name="attend_back",
        grid=(OWN,),
        out_shape=(out, out, out),
        in_specs=[pl.BlockSpec(memory_space=pltpu.SMEM), spec, spec, spec, spec]
        + [pl.BlockSpec((GROUP, 1, PAIR, 2 * HEAD), lambda h: (0, h, 0, 0))],
        out_specs=(out_spec, out_spec, out_spec),
        scratch_shapes=[
            pltpu.VMEM((ROWS, 2 * HEAD), bf16),
            pltpu.VMEM((HEAD, ROWS), f32),
            pltpu.VMEM((HEAD, ROWS), bf16),
            pltpu.VMEM((PROMPT, 2 * HEAD), f32),
            pltpu.VMEM((PROMPT, 2 * HEAD), f32),
        ],
        compiler_params=params(56),
    )(reach, q, k, v, f, g)


def middle_kernel(
    x_ref, o_ref, dy_ref, wo_ref, bo_ref, g_ref, s_ref, wf_ref, bf_ref, wp_ref, bp_ref,
    y_ref, dwf_ref, dwp_ref, dbf_ref, dwo_ref, dh_ref, do_ref, small_ref,
    o_s, h_s, b_s, bt_s, y_s, dn_s,
):
    step = pl.program_id(0)
    half = lanes(PAIR) < HEAD

    @pl.when(step == 0)
    def _():
        for t in range(HEADS // 2):
            one = o_ref[2 * t // OWN, 2 * t % OWN].astype(f32)
            two = o_ref[(2 * t + 1) // OWN, (2 * t + 1) % OWN].astype(f32)
            at = slice(2 * t * HEAD, (2 * t + 2) * HEAD)
            o_s[:PAIR, at] = jnp.where(half, one, pltpu.roll(two, HEAD, 1)).astype(bf16)
            o_s[PAIR:, at] = jnp.where(half, pltpu.roll(one, HEAD, 1), two).astype(bf16)
        h = x_ref[...].astype(f32) + dot(o_s[...], wo_ref[...]) + bo_ref[...]
        h_s[...] = h
        n, _ = moments(h)
        b_low = (n * g_ref[...] + s_ref[...]).astype(bf16)
        b_s[...] = b_low
        bt_s[...] = b_low.T
        y_s[...] = jnp.zeros_like(y_s)
        dn_s[...] = jnp.zeros_like(dn_s)

    dy = dy_ref[...]
    u = dot(b_s[...], wf_ref[...]) + bf_ref[...]
    square = u * u
    t = jnp.tanh(GELU_A * (u + GELU_B * (square * u)))
    m_low = (0.5 * u * (1.0 + t)).astype(bf16)
    slope = 0.5 * (1.0 + t) + 0.5 * u * (1.0 - t * t) * (GELU_A * (1.0 + 3.0 * GELU_B * square))
    y_s[...] += dot(m_low, wp_ref[...])
    du = (dot_nt(dy, wp_ref[...]) * slope).astype(bf16)
    dbf_ref[...] = jnp.sum(du.astype(f32), axis=0, keepdims=True)
    dn_s[...] += dot_nt(du, wf_ref[...])
    dwf_ref[...] = dot(bt_s[...], du).astype(bf16)
    dwp_ref[...] = dot_tn(m_low, dy).astype(bf16)

    @pl.when(step == pl.num_programs(0) - 1)
    def _():
        h = h_s[...]
        y_ref[...] = (h + y_s[...] + bp_ref[...]).astype(bf16)
        n, r = moments(h)
        dn = dn_s[...]
        grad = dy_ref[...].astype(f32)
        small_ref[...] = jnp.zeros_like(small_ref)
        small_ref[0:1, :] = jnp.sum(grad, axis=0, keepdims=True)
        small_ref[1:2, :] = jnp.sum(dn * n, axis=0, keepdims=True)
        small_ref[2:3, :] = jnp.sum(dn, axis=0, keepdims=True)
        e = dn * g_ref[...]
        lean = jnp.mean(e, axis=-1, keepdims=True) + n * jnp.mean(e * n, axis=-1, keepdims=True)
        dh = grad + r * (e - lean)
        dh_ref[...] = dh
        dh_low = dh.astype(bf16)
        small_ref[3:4, :] = jnp.sum(dh_low.astype(f32), axis=0, keepdims=True)
        dwo_ref[...] = dot_tn(o_s[...], dh_low).astype(bf16)
        h_s[...] = dot_nt(dh_low, wo_ref[...])
        for t in range(HEADS // 2):
            at = slice(2 * t * HEAD, (2 * t + 2) * HEAD)
            top, low = h_s[:PAIR, at], h_s[PAIR:, at]
            one = jnp.where(half, top, pltpu.roll(low, HEAD, 1))
            two = jnp.where(half, pltpu.roll(top, HEAD, 1), low)
            do_ref[2 * t // OWN, 2 * t % OWN] = one.astype(bf16)
            do_ref[(2 * t + 1) // OWN, (2 * t + 1) % OWN] = two.astype(bf16)


def middle(x, o, dy, wo, bo, gain, shift, wf, bf, wp, bp):
    fixed2 = lambda i: (0, 0)
    fixed4 = lambda i: (0, 0, 0, 0)
    square = pl.BlockSpec((TOK, D), fixed2)
    row = pl.BlockSpec((1, D), fixed2)
    heads = pl.BlockSpec((GROUP, OWN, PAIR, 2 * HEAD), fixed4)
    columns = pl.BlockSpec((D, CHUNK), lambda i: (0, i))
    down = pl.BlockSpec((CHUNK, D), lambda i: (i, 0))
    line = pl.BlockSpec((1, CHUNK), lambda i: (0, i))
    shape = jax.ShapeDtypeStruct
    return pl.pallas_call(
        middle_kernel,
        name="middle",
        grid=(FF // CHUNK,),
        out_shape=(
            shape((TOK, D), bf16),
            shape((D, FF), bf16),
            shape((FF, D), bf16),
            shape((1, FF), f32),
            shape((D, D), bf16),
            shape((TOK, D), f32),
            shape((GROUP, OWN, PAIR, 2 * HEAD), bf16),
            shape((8, D), f32),
        ),
        in_specs=[square, heads, square, square, row, row, row, columns, line, down, row],
        out_specs=(
            square, columns, down, line, square, square, heads, pl.BlockSpec((8, D), fixed2),
        ),
        scratch_shapes=[
            pltpu.VMEM((TOK, D), bf16),
            pltpu.VMEM((TOK, D), f32),
            pltpu.VMEM((TOK, D), bf16),
            pltpu.VMEM((D, TOK), bf16),
            pltpu.VMEM((TOK, D), f32),
            pltpu.VMEM((TOK, D), f32),
        ],
        compiler_params=params(60),
    )(x, o, dy, wo, bo, gain, shift, wf, bf, wp, bp)


def unproject_kernel(dq_ref, dk_ref, dv_ref, a_ref, w_ref, dn_ref, dw_ref, db_ref):
    step = pl.program_id(0)
    mixed = jnp.concatenate(
        [ref[h] for ref in (dq_ref, dk_ref, dv_ref) for h in range(OWN)], axis=1
    )
    dn_ref[...] = dot_nt(mixed, w_ref[...]).astype(bf16)
    dw = dot_tn(a_ref[...], mixed)
    db = jnp.sum(mixed.astype(f32), axis=0, keepdims=True)

    @pl.when(step == 0)
    def _():
        dw_ref[...] = dw
        db_ref[...] = db

    @pl.when(step > 0)
    def _():
        dw_ref[...] += dw
        db_ref[...] += db


def unproject(dq, dk, dv, a, w):
    tile = 768
    head = pl.BlockSpec((OWN, tile, HEAD), lambda i: (0, i, 0))
    whole = lambda i: (0, 0)
    shape = jax.ShapeDtypeStruct
    return pl.pallas_call(
        unproject_kernel,
        name="unproject",
        grid=(ROWS // tile,),
        out_shape=(shape((ROWS, D), bf16), shape((D, WIDE), f32), shape((1, WIDE), f32)),
        in_specs=[
            head, head, head,
            pl.BlockSpec((tile, D), lambda i: (i, 0)),
            pl.BlockSpec((D, WIDE), whole),
        ],
        out_specs=(
            pl.BlockSpec((tile, D), lambda i: (i, 0)),
            pl.BlockSpec((D, WIDE), whole),
            pl.BlockSpec((1, WIDE), whole),
        ),
        compiler_params=params(48),
    )(dq, dk, dv, a, w)


def finish_kernel(x_ref, dh_ref, g_ref, one_ref, two_ref, three_ref, out_ref):
    n, r = moments(x_ref[...].astype(f32))
    dn = one_ref[...].astype(f32) + two_ref[...].astype(f32) + three_ref[...].astype(f32)
    e = dn * g_ref[...]
    lean = jnp.mean(e, axis=-1, keepdims=True) + n * jnp.mean(e * n, axis=-1, keepdims=True)
    out_ref[...] = dh_ref[...] + r * (e - lean)


def finish(x, dh, gain, one, two, three):
    tile = 256
    rows = pl.BlockSpec((tile, D), lambda i: (i, 0))
    return pl.pallas_call(
        finish_kernel,
        name="finish",
        grid=(TOK // tile,),
        out_shape=jax.ShapeDtypeStruct((TOK, D), f32),
        in_specs=[rows, rows, pl.BlockSpec((1, D), lambda i: (0, 0)), rows, rows, rows],
        out_specs=rows,
        compiler_params=params(48),
    )(x, dh, gain, one, two, three)


def flip(block, bit):
    count = lax.axis_size("fsdp")
    return lax.ppermute(block, "fsdp", [(i, i ^ bit) for i in range(count)])


def over_replicas(block):
    count = lax.axis_size("rep")
    held = lax.optimization_barrier(block)
    if count == 2:
        other = lax.ppermute(held, "rep", [(0, 1), (1, 0)])
        return held.astype(f32) + other.astype(f32)
    return lax.psum(held.astype(f32), "rep")


def body(
    block_input, cotangent, tie_index, prefix_len, pre_gain, pre_shift, w_qkv, b_qv, w_out, b_out,
    mid_gain, mid_shift, w_fc, b_fc, w_proj, b_proj,
):
    n = lax.axis_size("fsdp")
    me = lax.axis_index("fsdp")
    pos = lax.rem(me, GROUP)
    rows = D // n
    index = tie_index[0]

    def chosen(bank):
        return lax.dynamic_index_in_dim(bank, index, 0, keepdims=False)

    vectors = (pre_gain, pre_shift, b_qv, b_out, mid_gain, mid_shift, b_fc, b_proj)
    sizes = [bank.shape[1] for bank in vectors]
    count = sum(sizes)
    small = jnp.concatenate([chosen(bank) for bank in vectors])
    high = -(-(rows + 2) // 16) * 16
    reach = prefix_len[0]
    reach_row = jnp.concatenate([reach // 16, reach % 16]).astype(bf16)
    wq = chosen(w_qkv).reshape(rows, 3, GROUP, SLICE).transpose(2, 0, 1, 3).reshape(GROUP, rows, WIDE)
    extra = jnp.stack(
        [jnp.pad(small, (0, WIDE - count)), jnp.pad(reach_row, (0, WIDE - reach_row.shape[0]))]
    )
    extra = jnp.pad(extra, ((0, high - rows - 2), (0, 0)))
    pieces = jnp.concatenate([wq, jnp.broadcast_to(extra, (GROUP,) + extra.shape)], axis=1)

    wo = lax.all_gather(chosen(w_out), "fsdp", axis=0, tiled=True)
    wf = lax.all_gather(chosen(w_fc), "fsdp", axis=0, tiled=True)
    wp = lax.all_gather(chosen(w_proj), "fsdp", axis=0, tiled=True)

    xg, wg = gather_group(n, block_input, pieces)
    wq = wg[:, :rows].reshape(D, WIDE)
    smalls = wg[:, rows, :count].astype(f32)
    group_rows = lax.dynamic_slice_in_dim(wg[:, rows + 1, :2], me - pos, GROUP, 0)
    reaches = (group_rows[:, 0].astype(f32) * 16 + group_rows[:, 1].astype(f32)).astype(jnp.int32)
    cuts = [sum(sizes[:i]) for i in range(len(sizes) + 1)]
    g1, s1, bqv, bo, g2, s2, bf, bp = (
        smalls[:, cuts[i] : cuts[i + 1]].reshape(1, -1) for i in range(len(sizes))
    )
    own_bias = lax.dynamic_index_in_dim(bqv.reshape(2, GROUP, SLICE), pos, 1, keepdims=False)
    bias = jnp.concatenate([own_bias[0], jnp.zeros((SLICE,), f32), own_bias[1]])[None]

    a_low, q, k, v = project(xg.reshape(ROWS, D), wq, g1, s1, bias)
    o_send, o_full, qx = attend(reaches, q, k, v)
    o_recv = swap(o_send, 1, "swap_o")
    y, dwf, dwp, dbf, dwo, dh, do_send, sums = middle(
        block_input, o_recv, cotangent, wo, bo, g2, s2, wf, bf, wp, bp
    )
    dwf = lax.psum_scatter(dwf, "fsdp", scatter_dimension=0, tiled=True)
    dwp = lax.psum_scatter(dwp, "fsdp", scatter_dimension=0, tiled=True)
    dwo = lax.psum_scatter(dwo, "fsdp", scatter_dimension=0, tiled=True)
    do_recv = swap(do_send, 2, "swap_do")
    dq, dk, dv = attend_back(reaches, qx, k, v, o_full, do_recv)
    dn, dwq, db = unproject(dq, dk, dv, a_low, wq)

    dn = dn.reshape(GROUP, TOK, D)
    block_of = lambda bit: lax.dynamic_index_in_dim(dn, pos ^ bit, 0, keepdims=False)
    beside = flip(block_of(1), 1)
    across = flip(block_of(3), 1)
    across = flip((across.astype(f32) + block_of(2).astype(f32)).astype(bf16), 2)

    wq_wide = wq.astype(f32)
    dshift = jnp.sum(wq_wide * db, axis=1)
    dgain = jnp.sum(wq_wide * (dwq - s1.reshape(D, 1) * db), axis=1) / g1.reshape(D)
    where = (jnp.arange(GROUP) == pos).astype(f32)[:, None]
    dbias = jnp.concatenate(
        [(where * db[:, :SLICE]).reshape(-1), (where * db[:, 2 * SLICE :]).reshape(-1)]
    )
    line = jnp.concatenate(
        [
            part.reshape(n, -1)
            for part in (dgain, dshift, dbias, sums[3], sums[1], sums[2], dbf, sums[0])
        ],
        axis=1,
    )
    line_hi = line.astype(bf16)
    line_low = (line - lax.reduce_precision(line, 8, 7)).astype(bf16)
    lines = jnp.pad(jnp.stack([line_hi, line_low], axis=1), ((0, 0), (0, 0), (0, WIDE - count)))
    lines = jnp.pad(lines, ((0, 0), (0, high - rows - 2), (0, 0)))
    back = jnp.concatenate([dwq.astype(bf16).reshape(n, rows, WIDE), lines], axis=1)
    back = swap(back, 3, "swap_grad")
    dwq = jnp.sum(back[:, :rows].astype(f32).reshape(n // GROUP, GROUP, rows, 3, SLICE), axis=0)
    dwq = dwq.transpose(1, 2, 0, 3).reshape(rows, 3 * D)
    line = jnp.sum(back[:, rows, :count].astype(f32) + back[:, rows + 1, :count].astype(f32), axis=0)

    grad = finish(block_input, dh, g1, block_of(0), beside, across)
    dwq = over_replicas(dwq.astype(bf16))
    dwo, dwf, dwp = over_replicas(dwo), over_replicas(dwf), over_replicas(dwp)
    line = over_replicas(line)
    dg1, ds1, dbqv, dbo, dg2, ds2, dbf, dbp = (
        line[cuts[i] : cuts[i + 1]] for i in range(len(sizes))
    )
    return (y, grad, dg1, ds1, dwq, dbqv, dwo, dbo, dg2, ds2, dwf, dbf, dwp, dbp)


def solution(mesh):
    tokens = P(("rep", "fsdp"), None)
    vector, matrix = P(None, "fsdp"), P(None, "fsdp", None)
    return jax.shard_map(
        body,
        mesh=mesh,
        in_specs=(
            tokens, tokens, P(), tokens, vector, vector, matrix, vector, matrix, vector,
            vector, vector, matrix, vector, matrix, vector,
        ),
        out_specs=(
            tokens, tokens, P("fsdp"), P("fsdp"), P("fsdp", None), P("fsdp"), P("fsdp", None),
            P("fsdp"), P("fsdp"), P("fsdp"), P("fsdp", None), P("fsdp"), P("fsdp", None), P("fsdp"),
        ),
        check_vma=False,
    )
```

time: 1100 us -> 476 us (0.43); the launches traced: 1080 us -> 475 us
  matrix products: 458 us -> 0 us
  Pallas kernels: 0 us -> 281 us
  blocking collectives: 129 us -> 0 us
  local copies, waits for them, and re-layouts: 166 us -> 47.9 us
  other arithmetic: 115 us -> 14.4 us
  waiting for transfers between devices: 189 us -> 107 us
    dot_general x180 -> x0, matrix products: 458 us -> none  [the longest x24 67.4 us: head_forward(): jnp.dot(weights, head_v, preferred_element_type=jnp.float32)]
    pallas_call x0 -> x10, Pallas kernels: none -> 281 us  [the longest x3 69 us: swap(): pl.pallas_call(partial(swap_kernel, count), name=name, out_shape=jax.Shap...]
    ppermute x4 -> x8, waiting for transfers between devices: 148 us -> 3.91 us  [the longest x5 3.91 us: over_replicas(): other = lax.ppermute(held, 'rep', [(0, 1), (1, 0)])]
    unnamed x2 -> x0, blocking collectives: 124 us -> none
    while x27 -> x0, local copies, waits for them, and re-layouts: 40.6 us -> none
    reduce_sum x34 -> x3, other arithmetic: 38.5 us -> 1.65 us  [the longest x1 1.3 us: body(): jnp.sum(back[:, :rows].astype(f32).reshape(n // GROUP, GROUP, rows, 3, SL...]
    all_gather x4 -> x3, waiting for transfers between devices: 0.03 us -> 33.1 us  [the longest x1 33.1 us: body(): wp = lax.all_gather(chosen(w_proj), 'fsdp', axis=0, tiled=True)]
    dynamic_update_slice x24 -> x0, local copies, waits for them, and re-layouts: 31.7 us -> none  [attend_forward(): lax.map(partial(head_forward, key_mask), (by_heads(queries), by_heads(key...]
  transfers between devices with their start and end apart: 13 -> 14, of which waited for: 5 -> 3; matrix products, arithmetic and copies ran while one was open for 62% -> 9% of each run, Pallas kernels for 0% -> 50%
where the time goes in v1:
time: 476 us; the launch traced here: 475 us
  Pallas kernels  281 us (59%)
  waiting for transfers between devices  107 us (22%)
  local copies, waits for them, and re-layouts  47.9 us (10%)
  between operations  16 us (3%)
  other arithmetic  14.4 us (3%)
  starting transfers between devices  8.8 us (2%)
    pallas_call x3, Pallas kernels, swap(): pl.pallas_call(partial(swap_kernel, count), name=name, out_shape=jax.Shap...  69 us
    reduce_scatter x1, waiting for transfers between devices, body(): dwf = lax.psum_scatter(dwf, 'fsdp', scatter_dimension=0, tiled=True)  68.7 us
    pallas_call x1, Pallas kernels, attend_back(): pl.pallas_call(attend_back_kernel, name='attend_back', grid=(OWN,), out_s...  57.2 us
    pallas_call x1, Pallas kernels, gather_group(): pl.pallas_call(partial(gather_kernel, n, parts), name='gather_group', out...  50.6 us
    pallas_call x1, Pallas kernels, middle(): pl.pallas_call(middle_kernel, name='middle', grid=(FF // CHUNK,), out_sha...  45.6 us
    all_gather x1, waiting for transfers between devices, body(): wp = lax.all_gather(chosen(w_proj), 'fsdp', axis=0, tiled=True)  33.1 us
    pallas_call x1, Pallas kernels, attend(): pl.pallas_call(attend_kernel, name='attend', grid=(OWN,), out_shape=(jax....  31.1 us
    unnamed x46, local copies, waits for them, and re-layouts  16.1 us
  transfers between devices with their start and end apart: 14, of which 3 were waited for; matrix products, arithmetic and copies ran while one was open for 9% of the time, Pallas kernels for 50%

profile of v1, /device:TPU:0, one launch (start us, length us, event | category | flops | bytes accessed | tf_op | source)
XLA Modules:
  0.0 475.1 jit_solution(2953917921654868572)
XLA Ops:
  8.0 1.7 constant_dynamic-slice_fusion.3
  9.8 0.7 constant_dynamic-slice_fusion.2
  10.7 1.8 constant_dynamic-slice_fusion.1
  13.3 0.7 fusion.12
  16.9 1.0 constant_dynamic-slice_fusion.14
  18.7 50.6 %gather_group.1 = (bf16[4,768,768]{2,1,0:T(8,128)(2,1)S(1)}, bf16[16,64,576]{2,1,0:T(8,128)(2,1)S(1)}) custom-call(bf16[768,768]{1,0:T(8,128)(2,1)S(1)} %copy-done.2, bf16[4,64,576]{2,1,0:T(8,128)(2,1)S(1)} %pad_maximum_fusion.1.w_ref), custom_call_target="tpu_custom_call" | custom-call | tf_op jit(solution)/shard_map/gather_group/pallas_call | solution.py:129
  69.3 2.1 copy-done.6
  71.5 0.7 copy.44
  76.4 11.0 %project.1 = (bf16[3072,768]{1,0:T(8,128)(2,1)}, bf16[3,3072,128]{2,1,0:T(8,128)(2,1)S(1)}, bf16[3,3072,128]{2,1,0:T(8,128)(2,1)S(1)}, bf16[3,3072,128]{2,1,0:T(8,128)(2,1)}) custom-call(bf16[3072,768]{1,0:T(8,128)(2,1)} %bitcast.59, bf16[768,576]{1,0:T(8,128)(2,1)S(1)} %bitcast.57, f32[1,768]{1,0:T(1,128)S(1)} %reshape.467.g_ref, ...), custom_call_target="tpu_custom_call" | custom-call | tf_op jit(solution)/shard_map/project/pallas_call | solution.py:206
  87.3 1.4 copy-done.4
  88.7 1.5 copy-done.9
  90.8 31.1 %attend.1 = (bf16[4,3,384,128]{3,2,1,0:T(8,128)(2,1)}, f32[3,3072,128]{2,1,0:T(8,128)}, bf16[3,3072,128]{2,1,0:T(8,128)(2,1)}) custom-call(s32[4]{0:T(128)} %convert_bitcast_fusion.reach_ref, bf16[3,3072,128]{2,1,0:T(8,128)(2,1)} %copy-done.9, bf16[3,3072,128]{2,1,0:T(8,128)(2,1)} %copy-done.4, bf16[3,3072,128]{2,1,0:T(8,128)(2,1)} %get-tuple-element.41.v_ref), custom_call_target="tpu_custom_call" | custom-call | tf_op jit(solution)/shard_map/attend/pallas_call | solution.py:289
  121.9 1.3 copy-done.13
  123.2 18.5 %swap_o.1.o_ref = bf16[4,3,384,128]{3,2,1,0:T(8,128)(2,1)S(1)} custom-call(bf16[4,3,384,128]{3,2,1,0:T(8,128)(2,1)S(1)} %copy-done.13), custom_call_target="tpu_custom_call" | custom-call | tf_op jit(solution)/shard_map/swap_o/pallas_call | solution.py:175
  141.7 1.0 copy-done.7
  142.7 33.1 %all-gather.11.cloned.1.call-done = bf16[1,3072,768]{2,1,0:T(8,128)(2,1)} async-done(((bf16[1,192,768]{2,1,0:T(8,128)(2,1)}), bf16[1,3072,768]{2,1,0:T(8,128)(2,1)}) %all-gather.11.cloned.1.call-update) | async-done | bytes 4718608 | tf_op jit(solution)/shard_map/all_gather | solution.py:616
  175.8 45.6 %middle.1 = (bf16[768,768]{1,0:T(8,128)(2,1)}, bf16[768,3072]{1,0:T(8,128)(2,1)}, bf16[3072,768]{1,0:T(8,128)(2,1)}, f32[1,3072]{1,0:T(1,128)}, bf16[768,768]{1,...) custom-call(bf16[768,768]{1,0:T(8,128)(2,1)} %x_ref.5, ...), custom_call_target="tpu_custom_call" | custom-call | tf_op jit(solution)/shard_map/middle/pallas_call | solution.py:477
  224.6 1.5 slice_reduce_fusion
  226.1 0.8 concatenate.71
  226.9 1.4 concatenate.69
  229.6 15.3 %swap_do.1.g_ref = bf16[4,3,384,128]{3,2,1,0:T(8,128)(2,1)S(1)} custom-call(bf16[4,3,384,128]{3,2,1,0:T(8,128)(2,1)S(1)} %copy-done.12), custom_call_target="tpu_custom_call" | custom-call | tf_op jit(solution)/shard_map/swap_do/pallas_call | solution.py:175
  244.9 1.0 copy-done.5
  245.9 57.2 %attend_back.1 = (bf16[3,3072,64]{2,1,0:T(8,128)(2,1)}, bf16[3,3072,64]{2,1,0:T(8,128)(2,1)}, bf16[3,3072,64]{2,1,0:T(8,128)(2,1)}) custom-call(s32[4]{0:T(128)} %convert_bitcast_fusion.reach_ref, bf16[3,3072,128]{2,1,0:T(8,128)(2,1)} %get-tuple-element.45.q_ref, bf16[3,3072,128]{2,1,0:T(8,128)(2,1)} %copy-done.4, ...), custom_call_target="tpu_custom_call" | custom-call | tf_op jit(solution)/shard_map/attend_back/pallas_call | solution.py:382
  303.1 1.7 copy-done.10
  304.8 11.9 %unproject.1 = (bf16[3072,768]{1,0:T(8,128)(2,1)}, f32[768,576]{1,0:T(8,128)S(1)}, f32[1,576]{1,0:T(1,128)S(1)}) custom-call(bf16[3,3072,64]{2,1,0:T(8,128)(2,1)S(1)} %copy-done.10, bf16[3,3072,64]{2,1,0:T(8,128)(2,1)} %get-tuple-element.49.dk_ref, bf16[3,3072,64]{2,1,0:T(8,128)(2,1)} %get-tuple-element.50.dv_ref, ...), custom_call_target="tpu_custom_call" | custom-call | tf_op jit(solution)/shard_map/unproject/pallas_call | solution.py:532
  316.7 1.3 copy-done.11
  318.1 2.9 fusion.20
  321.1 3.9 dynamic-slice_bitcast_fusion
  326.4 35.1 %swap_grad.1 = bf16[16,64,576]{2,1,0:T(8,128)(2,1)S(1)} custom-call(bf16[16,64,576]{2,1,0:T(8,128)(2,1)S(1)} %pad_maximum_fusion.x_ref), custom_call_target="tpu_custom_call" | custom-call | tf_op jit(solution)/shard_map/swap_grad/pallas_call | solution.py:175
  361.8 3.0 fusion
  364.7 2.3 collective-permute-start.2
  367.2 1.5 collective-permute-start.3
  368.6 1.0 slice.123
  369.7 3.2 reshape.476
  372.9 1.3 reduce.2
  377.2 1.4 collective-permute-start.5
  379.2 3.9 collective-permute-done.4
  383.1 0.8 convert_add_fusion.3
  384.0 68.7 %reduce-scatter.6.cloned.1.call-done = bf16[48,3072]{1,0:T(8,128)(2,1)} async-done(((bf16[768,3072]{1,0:T(8,128)(2,1)}), bf16[48,3072]{1,0:T(8,128)(2,1)}) %reduce-scatter.6.cloned.1.call-update) | async-done | bytes 294928 | tf_op jit(solution)/shard_map/reduce_scatter | solution.py:636
  452.6 1.5 collective-permute-start.6
  454.1 1.6 convert_add_fusion.4
  455.7 1.0 copy-done.14
  456.7 1.3 copy-done.3
  457.9 1.3 copy-done.8
  459.2 1.3 copy-done.15
  460.5 5.0 %finish.1 = f32[768,768]{1,0:T(8,128)} custom-call(bf16[768,768]{1,0:T(8,128)(2,1)S(1)} %copy-done.3, f32[768,768]{1,0:T(8,128)} %get-tuple-element.44.dh_ref, f32[1,768]{1,0:T(1,128)S(1)} %reshape.467.g_ref, bf16[768,768]{1,0:T(8,128)(2,1)S(1)} %copy-done.8, bf16[768,768]{1,0:T(8,128)(2,1)S(1)} %copy-done.15, bf16[768,768]{1,0:T(8,128)(2,1)} %collective-permute-done.2.three_ref), custom_call_target="tpu_custom_call" | custom-call | tf_op jit(solution)/shard_map/finish/pallas_call | solution.py:562
  465.5 1.8 convert_add_fusion.1
  467.4 0.9 convert_add_fusion.2
  (127 shorter events, 18.8 us)
Async XLA Ops:
  7.2 2.7 copy-start
  7.2 135.5 %all-gather.7.cloned.1.call-start = ((), (), s32[]{:S(2)}) async-start(), calls=%async_computation.6 | async-start | bytes 1253376 | tf_op jit(solution)/shard_map/all_gather | solution.py:614
  9.8 132.9 %all-gather.9.cloned.1.call-start = ((), (), s32[]{:S(2)}) async-start(), calls=%async_computation.7 | async-start | bytes 5013504 | tf_op jit(solution)/shard_map/all_gather | solution.py:615
  10.6 8.1 %copy-start.2 = (bf16[768,768]{1,0:T(8,128)(2,1)S(1)}, bf16[768,768]{1,0:T(8,128)(2,1)}, u32[]{:S(2)}) copy-start(bf16[768,768]{1,0:T(8,128)(2,1)} %x_ref.5) | copy-start | bytes 3538948
  10.6 165.1 %all-gather.11.cloned.1.call-start = ((), (), s32[]{:S(2)}) async-start(), calls=%async_computation.8 | async-start | bytes 5013504 | tf_op jit(solution)/shard_map/all_gather | solution.py:616
  12.5 364.7 %reduce-scatter.4.cloned.1.call-start = ((), (), s32[]{:S(2)}) async-start(), calls=%async_computation.3 | async-start | bytes 1253376 | tf_op jit(solution)/shard_map/reduce_scatter | solution.py:638
  69.3 2.1 copy-start.6
  87.3 1.4 copy-start.4
  88.7 1.5 copy-start.9
  121.9 1.3 copy-start.13
  141.7 1.0 copy-start.7
  221.4 157.3 %reduce-scatter.8.cloned.1.call-start = ((), (), s32[]{:S(2)}) async-start(), calls=%async_computation.5 | async-start | bytes 5013504 | tf_op jit(solution)/shard_map/reduce_scatter | solution.py:637
  221.9 230.7 %reduce-scatter.6.cloned.1.call-start = ((), (), s32[]{:S(2)}) async-start(), calls=%async_computation.4 | async-start | bytes 5013504 | tf_op jit(solution)/shard_map/reduce_scatter | solution.py:636
  222.0 1.8 copy-start.21
  222.0 7.6 %copy-start.12 = (bf16[4,3,384,128]{3,2,1,0:T(8,128)(2,1)S(1)}, bf16[4,3,384,128]{3,2,1,0:T(8,128)(2,1)}, u32[]{:S(2)}) copy-start(bf16[4,3,384,128]{3,2,1,0:T(8,128)(2,1)} %get-tuple-element.47.x_ref) | copy-start | bytes 3538948
  244.9 1.0 copy-start.5
  303.1 1.7 copy-start.10
  316.7 1.3 copy-start.11
  321.1 4.2 copy-start.22
  321.1 4.6 copy-start.18
  321.1 4.6 copy-start.19
  321.1 4.6 copy-start.20
  325.0 36.8 %collective-permute-start.1 = (bf16[768,768]{1,0:T(8,128)(2,1)}, bf16[768,768]{1,0:T(8,128)(2,1)}, u32[]{:S(2)}, u32[]{:S(2)}) collective-permute-start(bf16[768,768]{1,0:T(8,128)(2,1)} %get-tuple-element.66), channel_id=1, source_target_pairs={{0,1},{1,0},{2,3},{3,2},{4,5},{5,4},{6,7},{7,6},{8,9},{9,8},{10,11... | collective-permute-start | bytes 3538952 | tf_op jit(solution)/shard_map/ppermute | solution.py:575
  361.5 94.2 %collective-permute-start = (bf16[768,768]{1,0:T(8,128)(2,1)}, bf16[768,768]{1,0:T(8,128)(2,1)S(1)}, u32[]{:S(2)}, u32[]{:S(2)}) collective-permute-start(bf16[768,768]{1,0:T(8,128)(2,1)} %get-tuple-element.67), channel_id=1, source_target_pairs={{0,1},{1,0},{2,3},{3,2},{4,5},{5,4},{6,7},{7,6},{8,9},{9,8},{10,11... | collective-permute-start | bytes 3538952 | tf_op jit(solution)/shard_map/ppermute | solution.py:575
  364.7 91.9 %collective-permute-start.2 = (bf16[768,768]{1,0:T(8,128)(2,1)}, bf16[768,768]{1,0:T(8,128)(2,1)}, u32[]{:S(2)}, u32[]{:S(2)}) collective-permute-start(bf16[768,768]{1,0:T(8,128)(2,1)} %fusion), channel_id=1, source_target_pairs={{0,2},{1,3},{2,0},{3,1},{4,6},{5,7},{6,4},{7,5},{8,10},{9,11},{10,... | collective-permute-start | bytes 3538952 | tf_op jit(solution)/shard_map/ppermute | solution.py:575
  367.2 8.2 %collective-permute-start.3 = (f32[576]{0:T(1024)S(1)}, f32[576]{0:T(1024)S(1)}, u32[]{:S(2)}, u32[]{:S(2)}) collective-permute-start(f32[576]{0:T(1024)S(1)} %add_reduce_fusion), channel_id=1, source_target_pairs={{0,16},{16,0},{1,17},{17,1},{2,18},{18,2},{3,19},{19,3},{4,20},{20... | collective-permute-start | bytes 6920 | tf_op jit(solution)/shard_map/ppermute | solution.py:582
  374.7 8.4 %collective-permute-start.4 = (bf16[48,2304]{1,0:T(8,128)(2,1)S(1)}, bf16[48,2304]{1,0:T(8,128)(2,1)S(1)}, u32[]{:S(2)}, u32[]{:S(2)}) collective-permute-start(bf16[48,2304]{1,0:T(8,128)(2,1)S(1)} %convert_element_type.136), channel_id=1, source_target_pairs={{0,16},{16,0},{1,17},{17,1},{2,18},{18,2},{3,19},{19,3},{4,20},{20... | collective-permute-start | bytes 663560 | tf_op jit(solution)/shard_map/ppermute | solution.py:582
  377.2 76.9 %collective-permute-start.5 = (bf16[48,768]{1,0:T(8,128)(2,1)}, bf16[48,768]{1,0:T(8,128)(2,1)S(1)}, u32[]{:S(2)}, u32[]{:S(2)}) collective-permute-start(bf16[48,768]{1,0:T(8,128)(2,1)} %reduce-scatter.4.cloned.1.call-done), channel_id=1, source_target_pairs={{0,16},{16,0},{1,17},{17,1},{2,18},{18,2},{3,19},{19,3},{4,20},{20... | collective-permute-start | bytes 221192 | tf_op jit(solution)/shard_map/ppermute | solution.py:582
  378.7 86.9 %collective-permute-start.7 = (bf16[192,768]{1,0:T(8,128)(2,1)}, bf16[192,768]{1,0:T(8,128)(2,1)}, u32[]{:S(2)}, u32[]{:S(2)}) collective-permute-start(bf16[192,768]{1,0:T(8,128)(2,1)} %reduce-scatter.8.cloned.1.call-done), channel_id=1, source_target_pairs={{0,16},{16,0},{1,17},{17,1},{2,18},{18,2},{3,19},{19,3},{4,20},{20... | collective-permute-start | bytes 884744 | tf_op jit(solution)/shard_map/ppermute | solution.py:582
  452.6 14.8 %collective-permute-start.6 = (bf16[48,3072]{1,0:T(8,128)(2,1)}, bf16[48,3072]{1,0:T(8,128)(2,1)S(1)}, u32[]{:S(2)}, u32[]{:S(2)}) collective-permute-start(bf16[48,3072]{1,0:T(8,128)(2,1)} %reduce-scatter.6.cloned.1.call-done), channel_id=1, source_target_pairs={{0,16},{16,0},{1,17},{17,1},{2,18},{18,2},{3,19},{19,3},{4,20},{20... | collective-permute-start | bytes 884744 | tf_op jit(solution)/shard_map/ppermute | solution.py:582
  455.7 1.0 copy-start.14
  456.7 1.3 copy-start.3
  457.9 1.3 copy-start.8
  459.2 1.3 copy-start.15
  460.5 5.0 %copy-start.16 = (bf16[192,768]{1,0:T(8,128)(2,1)S(1)}, bf16[192,768]{1,0:T(8,128)(2,1)}, u32[]{:S(2)}) copy-start(bf16[192,768]{1,0:T(8,128)(2,1)} %reduce-scatter.8.cloned.1.call-done) | copy-start | bytes 884740
  460.5 6.9 %copy-start.17 = (bf16[48,3072]{1,0:T(8,128)(2,1)S(1)}, bf16[48,3072]{1,0:T(8,128)(2,1)}, u32[]{:S(2)}) copy-start(bf16[48,3072]{1,0:T(8,128)(2,1)} %reduce-scatter.6.cloned.1.call-done) | copy-start | bytes 884740
  460.5 7.7 %copy-start.1 = (bf16[12,48,3072]{2,1,0:T(8,128)(2,1)S(1)}, bf16[12,48,3072]{2,1,0:T(8,128)(2,1)}, u32[]{:S(2)}) copy-start(bf16[12,48,3072]{2,1,0:T(8,128)(2,1)} %param.28) | copy-start | bytes 10616836
Sparse Core Ops, SparseCore 0:
  10.9 52.2 all-gather.6
  66.1 52.1 all-gather.8
  121.1 54.5 all-gather.10
  221.5 56.8 reduce-scatter.3
  282.1 92.3 reduce-scatter.7
  378.7 73.8 reduce-scatter.5

commit v2 on v1

--- a/solution.py
+++ b/solution.py
@@ -20,7 +20,9 @@
 SLICE = OWN * HEAD
 WIDE = 3 * SLICE
 PAIR = TOK // 2
-CHUNK = 256
+CHUNK = 768
+BLOCKS = 16
+UNIT = 432
 NEG = -1e30
 EPS = 1e-5
 GELU_A = 0.7978845608028654
@@ -398,13 +400,326 @@
     )(reach, q, k, v, f, g)
 
 
+def ring_of(me):
+    chip, core = me // 2, lax.rem(me, 2)
+    z, x = chip // 2, lax.rem(chip, 2)
+    chips = BLOCKS // 2
+    half = chips // 2
+    place = z * (1 - x) + (chips - 1 - z) * x
+
+    def device(at):
+        at = lax.rem(at + 2 * chips, chips)
+        side = at // half
+        z_at = at * (1 - side) + (chips - 1 - at) * side
+        return (z_at * 2 + side) * 2 + core
+
+    return place, device
+
+
+def forward_kernel(
+    x_ref, sm_ref, pc_ref, wp_ref, wo_ref, wf_ref,
+    wall_ref, smo_ref, wq_ref, a_ref, q_ref, k_ref, v_ref, f_ref, o_ref,
+    xg, smg, wg, w_s, q_s, k_s, v_s, f_s, o_s,
+    local, sm_send, sm_recv, w_send, w_recv, x_send, x_recv, r_send, r_recv, n_send, n_recv,
+    o_send, o_recv, out_sem,
+):
+    n = BLOCKS
+    me = lax.axis_index("fsdp")
+    pos = lax.rem(me, GROUP)
+    base = me - pos
+    near, far = me ^ 1, me ^ 2
+    place, device = ring_of(me)
+    parts = 4
+    part_rows = TOK // parts
+    T = CONT
+
+    def remote(src, dst, send, recv, peer):
+        return pltpu.make_async_remote_copy(
+            src_ref=src,
+            dst_ref=dst,
+            send_sem=send,
+            recv_sem=recv,
+            device_id={"fsdp": peer},
+            device_id_type=MESH,
+        )
+
+    greet([me ^ i for i in range(1, n)])
+
+    shard = [
+        pltpu.make_async_copy(wp_ref, wall_ref.at[me, pl.ds(0, 192)], local.at[0]),
+        pltpu.make_async_copy(wo_ref, wall_ref.at[me, pl.ds(192, 48)], local.at[1]),
+    ]
+    for c in range(4):
+        shard.append(
+            pltpu.make_async_copy(
+                wf_ref.at[:, pl.ds(c * D, D)], wall_ref.at[me, pl.ds(240 + 48 * c, 48)], local.at[2 + c]
+            )
+        )
+    own_x = pltpu.make_async_copy(x_ref, xg.at[pos], local.at[6])
+    own_w = pltpu.make_async_copy(pc_ref.at[pos], wg.at[me], local.at[7])
+    own_s = pltpu.make_async_copy(sm_ref, smg.at[me], local.at[8])
+    for copy in [own_s, own_x, own_w] + shard:
+        copy.start()
+
+    smalls, slices = [], []
+    for i in range(1, n):
+        copy = remote(sm_ref, smg.at[me], sm_send.at[i], sm_recv.at[i], me ^ i)
+        copy.start()
+        smalls.append(copy)
+    beside = remote(x_ref, xg.at[pos], x_send.at[2 * parts], x_recv.at[2 * parts], near)
+    beside.start()
+    for i in range(1, n):
+        peer = me ^ i
+        copy = remote(pc_ref.at[lax.rem(peer, GROUP)], wg.at[me], w_send.at[i], w_recv.at[i], peer)
+        copy.start()
+        slices.append(copy)
+
+    def x_part(src, slot, part, i, peer):
+        at = pl.ds(part * part_rows, part_rows)
+        return remote(src.at[at], xg.at[slot, at], x_send.at[i], x_recv.at[i], peer)
+
+    across = [x_part(x_ref, pos, part, part, far) for part in range(parts)]
+    for copy in across:
+        copy.start()
+
+    def hop(t, right):
+        at = place - t if right else place + t
+        block = wall_ref.at[device(at)]
+        i = t if right else 4 + t
+        return remote(block, block, r_send.at[i], r_recv.at[i], device(place + 1 if right else place - 1))
+
+    def beside_hop(t, right):
+        at = place - 1 - t if right else place + 1 + t
+        block = wall_ref.at[device(at)]
+        i = 1 + (t if right else 4 + t)
+        return remote(block, block, n_send.at[i], n_recv.at[i], near)
+
+    hops, shared = {}, []
+
+    def launch(t):
+        for right in (True, False):
+            if t < (4 if right else 3):
+                hops[t, right] = hop(t, right)
+                hops[t, right].start()
+
+    def arrive(t):
+        for right in (True, False):
+            if t < (4 if right else 3):
+                hops[t, right].wait_recv()
+        if t < 3:
+            launch(t + 1)
+        for right in (True, False):
+            if t < (4 if right else 3):
+                copy = beside_hop(t, right)
+                copy.start()
+                shared.append(copy)
+
+    for copy in shard:
+        copy.wait()
+    launch(0)
+    own_block = remote(wall_ref.at[me], wall_ref.at[me], n_send.at[0], n_recv.at[0], near)
+    own_block.start()
+    shared.append(own_block)
+
+    own_s.wait()
+    for copy in smalls:
+        copy.wait_recv()
+    rows48 = D // n
+    gain = jnp.concatenate([smg[d, 0:1, 0:rows48] for d in range(n)], axis=1).astype(f32)
+    shift = jnp.concatenate([smg[d, 0:1, rows48 : 2 * rows48] for d in range(n)], axis=1).astype(f32)
+    at = 2 * rows48
+    two = 2 * rows48
+    zeros = jnp.zeros((1, SLICE), bf16)
+    bias = jnp.concatenate(
+        [smg[2 * pos + i, 0:1, at : at + two] for i in range(2)]
+        + [zeros]
+        + [smg[n // 2 + 2 * pos + i, 0:1, at : at + two] for i in range(2)],
+        axis=1,
+    ).astype(f32)
+
+    def norm(slot):
+        def some(i, carry):
+            at = pl.ds(pl.multiple_of(i * PAIR, PAIR), PAIR)
+            n_rows, _ = moments(xg[slot, at, :].astype(f32))
+            xg[slot, at, :] = (n_rows * gain + shift).astype(bf16)
+            return carry
+
+        lax.fori_loop(0, 2, some, 0)
+
+    def project_block(slot):
+        def some(i, carry):
+            at = pl.ds(pl.multiple_of(i * PAIR, PAIR), PAIR)
+            out = pl.ds(pl.multiple_of(slot * TOK + i * PAIR, PAIR), PAIR)
+            mixed = (dot(xg[slot, at, :], w_s[...]) + bias).astype(bf16)
+            ones = jnp.ones((PAIR, HEAD), bf16)
+            for h in range(OWN):
+                q = mixed[:, h * HEAD : (h + 1) * HEAD] * 0.125
+                k = mixed[:, SLICE + h * HEAD : SLICE + (h + 1) * HEAD]
+                v = mixed[:, 2 * SLICE + h * HEAD : 2 * SLICE + (h + 1) * HEAD]
+                q_s[h, out, :] = jnp.concatenate([q.astype(bf16), jnp.zeros_like(ones)], axis=1)
+                k_s[h, out, :] = jnp.concatenate([k, ones], axis=1)
+                v_s[h, out, :] = jnp.concatenate([v, ones], axis=1)
+            return carry
+
+        lax.fori_loop(0, 2, some, 0)
+
+    own_x.wait()
+    norm(pos)
+    beside.wait()
+    norm(pos ^ 1)
+    own_w.wait()
+    for copy in slices:
+        copy.wait_recv()
+    w_s[...] = wg[:, :rows48, :].reshape(D, WIDE)
+    project_block(pos)
+    project_block(pos ^ 1)
+    passed = []
+    for part in range(parts):
+        across[part].wait_recv()
+        copy = x_part(xg.at[pos ^ 2], pos ^ 2, part, parts + part, near)
+        copy.start()
+        passed.append(copy)
+    for copy in passed:
+        copy.wait()
+    norm(pos ^ 2)
+    project_block(pos ^ 2)
+    norm(pos ^ 3)
+    project_block(pos ^ 3)
+    arrive(0)
+
+    outs = [
+        pltpu.make_async_copy(smg, smo_ref, out_sem.at[0]),
+        pltpu.make_async_copy(w_s, wq_ref, out_sem.at[1]),
+        pltpu.make_async_copy(xg, a_ref, out_sem.at[2]),
+        pltpu.make_async_copy(k_s, k_ref, out_sem.at[3]),
+        pltpu.make_async_copy(v_s, v_ref, out_sem.at[4]),
+    ]
+    for copy in outs:
+        copy.start()
+
+    lane = lanes(T)
+    causal = below(T, T, False)
+    half = lanes(PAIR) < HEAD
+    code = [smg[base + c, 1:2, 0:2].astype(f32) for c in range(GROUP)]
+    reaches = [c[:, 0:1] * 16.0 + c[:, 1:2] for c in code]
+    column = lax.broadcasted_iota(jnp.int32, (T, PROMPT), 1).astype(f32)
+
+    for h in range(OWN):
+
+        def tile(at, blocks):
+            q = q_s[h, pl.ds(at, T), :]
+            scores = []
+            for start, size, mask in blocks:
+                s = dot_nt(q, k_s[h, pl.ds(start, size), :])
+                scores.append(s if mask is None else jnp.where(mask, s, NEG))
+            peak = scores[0].max(axis=1, keepdims=True)
+            for s in scores[1:]:
+                peak = jnp.maximum(peak, s.max(axis=1, keepdims=True))
+            total = jnp.zeros((T, 2 * HEAD), f32)
+            for s, (start, size, _) in zip(scores, blocks):
+                total += dot(jnp.exp(s - peak).astype(bf16), v_s[h, pl.ds(start, size), :])
+            mass = total[:, HEAD : HEAD + 1]
+            f_s[h, pl.ds(at, T), :] = total / mass
+            lse = peak + jnp.log(mass)
+            q_s[h, pl.ds(at, T), :] = split_columns(q.astype(f32), lane, lse)
+
+        for p in range(GROUP):
+            past = [(i * TOK, PROMPT, None) for i in range(p)]
+            at = p * TOK
+            tile(at, past + [(at, T, causal)])
+            tile(at + T, past + [(at, T, None), (at + T, T, causal)])
+        if h < 2:
+            arrive(1 + h)
+        for c in range(GROUP):
+            at = c * TOK + PROMPT
+            blocks = [(i * TOK, PROMPT, column < reaches[c] - i * PROMPT) for i in range(GROUP)]
+            tile(at, blocks + [(at, T, causal)])
+        for p in range(GROUP):
+            top = f_s[h, p * TOK : p * TOK + PAIR, :]
+            low = f_s[h, p * TOK + PAIR : (p + 1) * TOK, :]
+            o_s[h, p] = jnp.where(half, top, pltpu.roll(low, HEAD, 1)).astype(bf16)
+        for i in range(1, GROUP):
+            copy = remote(
+                o_s.at[h, pos ^ i], o_ref.at[pos, h], o_send.at[h, i], o_recv.at[h, i], me ^ i
+            )
+            copy.start()
+            shared.append(copy)
+        for src, dst, i in (
+            (o_s.at[h, pos], o_ref.at[pos, h], 5 + h),
+            (f_s.at[h], f_ref.at[h], 8 + h),
+            (q_s.at[h], q_ref.at[h], 11 + h),
+        ):
+            copy = pltpu.make_async_copy(src, dst, out_sem.at[i])
+            copy.start()
+            outs.append(copy)
+
+    arrive(3)
+    for copy in across + smalls + slices + list(hops.values()):
+        copy.wait_send()
+    for copy in shared + outs:
+        copy.wait()
+
+
+def forward(x, small, pieces, wp, wo, wf):
+    dma = pltpu.SemaphoreType.DMA
+    n = BLOCKS
+    shape = jax.ShapeDtypeStruct
+    head = (OWN, ROWS, 2 * HEAD)
+    return pl.pallas_call(
+        forward_kernel,
+        name="forward",
+        out_shape=(
+            shape((n, UNIT, D), bf16),
+            shape((n,) + small.shape, bf16),
+            shape((D, WIDE), bf16),
+            shape((GROUP, TOK, D), bf16),
+            shape(head, bf16),
+            shape(head, bf16),
+            shape(head, bf16),
+            shape(head, f32),
+            shape((GROUP, OWN, PAIR, 2 * HEAD), bf16),
+        ),
+        in_specs=[ANY] * 6,
+        out_specs=(ANY,) * 9,
+        scratch_shapes=[
+            pltpu.VMEM((GROUP, TOK, D), bf16),
+            pltpu.VMEM((n,) + small.shape, bf16),
+            pltpu.VMEM((n,) + pieces.shape[1:], bf16),
+            pltpu.VMEM((D, WIDE), bf16),
+            pltpu.VMEM(head, bf16),
+            pltpu.VMEM(head, bf16),
+            pltpu.VMEM(head, bf16),
+            pltpu.VMEM(head, f32),
+            pltpu.VMEM((OWN, GROUP, PAIR, 2 * HEAD), bf16),
+            dma((9,)),
+            dma((n,)),
+            dma((n,)),
+            dma((n,)),
+            dma((n,)),
+            dma((9,)),
+            dma((9,)),
+            dma((7,)),
+            dma((7,)),
+            dma((8,)),
+            dma((8,)),
+            dma((OWN, GROUP)),
+            dma((OWN, GROUP)),
+            dma((14,)),
+        ],
+        compiler_params=params(60, collective_id=0, has_side_effects=True),
+    )(x, small, pieces, wp, wo, wf)
+
+
 def middle_kernel(
-    x_ref, o_ref, dy_ref, wo_ref, bo_ref, g_ref, s_ref, wf_ref, bf_ref, wp_ref, bp_ref,
+    x_ref, o_ref, dy_ref, wo_ref, wf_ref, wp_ref, bo_ref, g_ref, s_ref, bf_ref, bp_ref,
     y_ref, dwf_ref, dwp_ref, dbf_ref, dwo_ref, dh_ref, do_ref, small_ref,
     o_s, h_s, b_s, bt_s, y_s, dn_s,
 ):
     step = pl.program_id(0)
     half = lanes(PAIR) < HEAD
+    wf = wf_ref[...].reshape(D, CHUNK)
+    wp = wp_ref[...].reshape(CHUNK, D)
+    wo = wo_ref[...].reshape(D, D)
 
     @pl.when(step == 0)
     def _():
@@ -414,7 +729,7 @@
             at = slice(2 * t * HEAD, (2 * t + 2) * HEAD)
             o_s[:PAIR, at] = jnp.where(half, one, pltpu.roll(two, HEAD, 1)).astype(bf16)
             o_s[PAIR:, at] = jnp.where(half, pltpu.roll(one, HEAD, 1), two).astype(bf16)
-        h = x_ref[...].astype(f32) + dot(o_s[...], wo_ref[...]) + bo_ref[...]
+        h = x_ref[...].astype(f32) + dot(o_s[...], wo) + bo_ref[...]
         h_s[...] = h
         n, _ = moments(h)
         b_low = (n * g_ref[...] + s_ref[...]).astype(bf16)
@@ -424,15 +739,15 @@
         dn_s[...] = jnp.zeros_like(dn_s)
 
     dy = dy_ref[...]
-    u = dot(b_s[...], wf_ref[...]) + bf_ref[...]
+    u = dot(b_s[...], wf) + bf_ref[...]
     square = u * u
     t = jnp.tanh(GELU_A * (u + GELU_B * (square * u)))
     m_low = (0.5 * u * (1.0 + t)).astype(bf16)
     slope = 0.5 * (1.0 + t) + 0.5 * u * (1.0 - t * t) * (GELU_A * (1.0 + 3.0 * GELU_B * square))
-    y_s[...] += dot(m_low, wp_ref[...])
-    du = (dot_nt(dy, wp_ref[...]) * slope).astype(bf16)
+    y_s[...] += dot(m_low, wp)
+    du = (dot_nt(dy, wp) * slope).astype(bf16)
     dbf_ref[...] = jnp.sum(du.astype(f32), axis=0, keepdims=True)
-    dn_s[...] += dot_nt(du, wf_ref[...])
+    dn_s[...] += dot_nt(du, wf)
     dwf_ref[...] = dot(bt_s[...], du).astype(bf16)
     dwp_ref[...] = dot_tn(m_low, dy).astype(bf16)
 
@@ -454,7 +769,7 @@
         dh_low = dh.astype(bf16)
         small_ref[3:4, :] = jnp.sum(dh_low.astype(f32), axis=0, keepdims=True)
         dwo_ref[...] = dot_tn(o_s[...], dh_low).astype(bf16)
-        h_s[...] = dot_nt(dh_low, wo_ref[...])
+        h_s[...] = dot_nt(dh_low, wo)
         for t in range(HEADS // 2):
             at = slice(2 * t * HEAD, (2 * t + 2) * HEAD)
             top, low = h_s[:PAIR, at], h_s[PAIR:, at]
@@ -464,7 +779,7 @@
             do_ref[(2 * t + 1) // OWN, (2 * t + 1) % OWN] = two.astype(bf16)
 
 
-def middle(x, o, dy, wo, bo, gain, shift, wf, bf, wp, bp):
+def middle(x, o, dy, wall, bo, gain, shift, bf, bp):
     fixed2 = lambda i: (0, 0)
     fixed4 = lambda i: (0, 0, 0, 0)
     square = pl.BlockSpec((TOK, D), fixed2)
@@ -488,7 +803,13 @@
             shape((GROUP, OWN, PAIR, 2 * HEAD), bf16),
             shape((8, D), f32),
         ),
-        in_specs=[square, heads, square, square, row, row, row, columns, line, down, row],
+        in_specs=[
+            square, heads, square,
+            pl.BlockSpec((BLOCKS, 48, D), lambda i: (0, 4, 0)),
+            pl.BlockSpec((BLOCKS, 48, D), lambda i: (0, 5 + i, 0)),
+            pl.BlockSpec((BLOCKS // 4, 192, D), lambda i: (i, 0, 0)),
+            row, row, row, line, row,
+        ],
         out_specs=(
             square, columns, down, line, square, square, heads, pl.BlockSpec((8, D), fixed2),
         ),
@@ -501,7 +822,7 @@
             pltpu.VMEM((TOK, D), f32),
         ],
         compiler_params=params(60),
-    )(x, o, dy, wo, bo, gain, shift, wf, bf, wp, bp)
+    )(x, o, dy, wall, wall, wall, bo, gain, shift, bf, bp)
 
 
 def unproject_kernel(dq_ref, dk_ref, dv_ref, a_ref, w_ref, dn_ref, dw_ref, db_ref):
@@ -605,33 +926,44 @@
     reach = prefix_len[0]
     reach_row = jnp.concatenate([reach // 16, reach % 16]).astype(bf16)
     wq = chosen(w_qkv).reshape(rows, 3, GROUP, SLICE).transpose(2, 0, 1, 3).reshape(GROUP, rows, WIDE)
+    width = -(-WIDE // 128) * 128
     extra = jnp.stack(
-        [jnp.pad(small, (0, WIDE - count)), jnp.pad(reach_row, (0, WIDE - reach_row.shape[0]))]
+        [jnp.pad(small, (0, width - count)), jnp.pad(reach_row, (0, width - reach_row.shape[0]))]
     )
-    extra = jnp.pad(extra, ((0, high - rows - 2), (0, 0)))
-    pieces = jnp.concatenate([wq, jnp.broadcast_to(extra, (GROUP,) + extra.shape)], axis=1)
-
-    wo = lax.all_gather(chosen(w_out), "fsdp", axis=0, tiled=True)
-    wf = lax.all_gather(chosen(w_fc), "fsdp", axis=0, tiled=True)
-    wp = lax.all_gather(chosen(w_proj), "fsdp", axis=0, tiled=True)
-
-    xg, wg = gather_group(n, block_input, pieces)
-    wq = wg[:, :rows].reshape(D, WIDE)
-    smalls = wg[:, rows, :count].astype(f32)
-    group_rows = lax.dynamic_slice_in_dim(wg[:, rows + 1, :2], me - pos, GROUP, 0)
-    reaches = (group_rows[:, 0].astype(f32) * 16 + group_rows[:, 1].astype(f32)).astype(jnp.int32)
+    wo, wf, wp = chosen(w_out), chosen(w_fc), chosen(w_proj)
     cuts = [sum(sizes[:i]) for i in range(len(sizes) + 1)]
-    g1, s1, bqv, bo, g2, s2, bf, bp = (
-        smalls[:, cuts[i] : cuts[i + 1]].reshape(1, -1) for i in range(len(sizes))
-    )
-    own_bias = lax.dynamic_index_in_dim(bqv.reshape(2, GROUP, SLICE), pos, 1, keepdims=False)
-    bias = jnp.concatenate([own_bias[0], jnp.zeros((SLICE,), f32), own_bias[1]])[None]
-
-    a_low, q, k, v = project(xg.reshape(ROWS, D), wq, g1, s1, bias)
-    o_send, o_full, qx = attend(reaches, q, k, v)
-    o_recv = swap(o_send, 1, "swap_o")
+
+    def vectors_of(lines):
+        smalls = lines[:, 0, :count].astype(f32)
+        group_rows = lax.dynamic_slice_in_dim(lines[:, 1, :2], me - pos, GROUP, 0)
+        reaches = group_rows[:, 0].astype(f32) * 16 + group_rows[:, 1].astype(f32)
+        return [
+            smalls[:, cuts[i] : cuts[i + 1]].reshape(1, -1) for i in range(len(sizes))
+        ], reaches.astype(jnp.int32)
+
+    if n == BLOCKS:
+        wall, lines, wq, a_low, qx, k, v, o_full, o_recv = forward(block_input, extra, wq, wp, wo, wf)
+        a_low = a_low.reshape(ROWS, D)
+        (g1, s1, _, bo, g2, s2, bf, bp), reaches = vectors_of(lines)
+    else:
+        extra = jnp.pad(extra[:, :WIDE], ((0, high - rows - 2), (0, 0)))
+        pieces = jnp.concatenate([wq, jnp.broadcast_to(extra, (GROUP,) + extra.shape)], axis=1)
+        wo = lax.all_gather(wo, "fsdp", axis=0, tiled=True).reshape(BLOCKS, -1, D)
+        wf = lax.all_gather(wf, "fsdp", axis=0, tiled=True)
+        wf = wf.reshape(BLOCKS, D // BLOCKS, FF // D, D).transpose(0, 2, 1, 3)
+        wp = lax.all_gather(wp, "fsdp", axis=0, tiled=True).reshape(BLOCKS, -1, D)
+        wall = jnp.concatenate([wp, wo, wf.reshape(BLOCKS, -1, D)], axis=1)
+        xg, wg = gather_group(n, block_input, pieces)
+        wq = wg[:, :rows].reshape(D, WIDE)
+        (g1, s1, bqv, bo, g2, s2, bf, bp), reaches = vectors_of(wg[:, rows : rows + 2])
+        own_bias = lax.dynamic_index_in_dim(bqv.reshape(2, GROUP, SLICE), pos, 1, keepdims=False)
+        bias = jnp.concatenate([own_bias[0], jnp.zeros((SLICE,), f32), own_bias[1]])[None]
+        a_low, q, k, v = project(xg.reshape(ROWS, D), wq, g1, s1, bias)
+        o_send, o_full, qx = attend(reaches, q, k, v)
+        o_recv = swap(o_send, 1, "swap_o")
+
     y, dwf, dwp, dbf, dwo, dh, do_send, sums = middle(
-        block_input, o_recv, cotangent, wo, bo, g2, s2, wf, bf, wp, bp
+        block_input, o_recv, cotangent, wall, bo, g2, s2, bf, bp
     )
     dwf = lax.psum_scatter(dwf, "fsdp", scatter_dimension=0, tiled=True)
     dwp = lax.psum_scatter(dwp, "fsdp", scatter_dimension=0, tiled=True)

time: 476 us -> 450 us (0.945); the launches traced: 475 us -> 444 us
  waiting for transfers between devices: 107 us -> 76.1 us
    all_gather x3 -> x0, waiting for transfers between devices: 33.1 us -> none  [the longest x1 33.1 us: body(): wp = lax.all_gather(chosen(w_proj), 'fsdp', axis=0, tiled=True)]
    pallas_call x3 -> x1, Pallas kernels: 92.7 us -> 118 us  [forward(): pl.pallas_call(forward_kernel, name='forward', out_shape=(shape((n, UNIT,...]
    pallas_call x3 -> x2, Pallas kernels: 69 us -> 51.4 us  [swap(): pl.pallas_call(partial(swap_kernel, count), name=name, out_shape=jax.Shap...]
    unnamed x46 -> x28, local copies, waits for them, and re-layouts: 16.1 us -> 7.66 us
    pallas_call x1, Pallas kernels: 45.6 us -> 39.2 us  [middle(): pl.pallas_call(middle_kernel, name='middle', grid=(FF // CHUNK,), out_sha...]
    squeeze x4 -> x7, local copies, waits for them, and re-layouts: 2.8 us -> 8.29 us  [chosen(): return lax.dynamic_index_in_dim(bank, index, 0, keepdims=False)]
  transfers between devices with their start and end apart: 14 -> 11, of which waited for: 3 -> 2; matrix products, arithmetic and copies ran while one was open for 9% -> 6% of each run, Pallas kernels for 50% -> 28%
where the time goes in v2:
time: 450 us; the launch traced here: 444 us
  Pallas kernels  282 us (63%)
  waiting for transfers between devices  76.1 us (17%)
  local copies, waits for them, and re-layouts  46.2 us (10%)
  between operations  16 us (4%)
  other arithmetic  14.8 us (3%)
  starting transfers between devices  8.96 us (2%)
    pallas_call x1, Pallas kernels, forward(): pl.pallas_call(forward_kernel, name='forward', out_shape=(shape((n, UNIT,...  118 us
    reduce_scatter x1, waiting for transfers between devices, body(): dwf = lax.psum_scatter(dwf, 'fsdp', scatter_dimension=0, tiled=True)  71.2 us
    pallas_call x1, Pallas kernels, attend_back(): pl.pallas_call(attend_back_kernel, name='attend_back', grid=(OWN,), out_s...  57 us
    pallas_call x2, Pallas kernels, swap(): pl.pallas_call(partial(swap_kernel, count), name=name, out_shape=jax.Shap...  51.4 us
    pallas_call x1, Pallas kernels, middle(): pl.pallas_call(middle_kernel, name='middle', grid=(FF // CHUNK,), out_sha...  39.2 us
    pallas_call x1, Pallas kernels, unproject(): pl.pallas_call(unproject_kernel, name='unproject', grid=(ROWS // tile,),...  12.1 us
  transfers between devices with their start and end apart: 11, of which 2 were waited for; matrix products, arithmetic and copies ran while one was open for 6% of the time, Pallas kernels for 28%

profile of v2, /device:TPU:0, one launch (start us, length us, event | category | flops | bytes accessed | tf_op | source)
XLA Modules:
  0.0 444.3 jit_solution(526605800367036875)
XLA Ops:
  8.9 1.2 fusion.14
  10.1 1.2 fusion.11
  11.4 0.7 fusion.12
  12.1 1.2 fusion.15
  13.4 1.2 fusion.17
  14.6 4.1 concatenate.53
  18.7 1.5 dynamic-slice_bitcast_fusion.5.wo_ref
  20.2 1.6 constant_dynamic-slice_fusion.1
  21.8 2.0 reshape.447
  23.8 1.9 copy.42
  25.6 2.0 reshape.448.pc_ref
  27.6 0.7 dynamic-slice_bitcast_fusion.3.wf_ref
  28.4 1.7 dynamic-slice_bitcast_fusion.4.wp_ref
  30.6 117.5 %forward.1 = (bf16[16,432,768]{2,1,0:T(8,128)(2,1)}, bf16[16,2,640]{2,1,0:T(2,128)(2,1)}, bf16[768,576]{1,0:T(8,128)(2,1)}, bf16[4,768,768]{2,1,0:T(8,128)(2,1)}...) custom-call(bf16[768,768]{1,0:T(8,128)(2,1)} %x_ref.5, ...), custom_call_target="tpu_custom_call" | custom-call | tf_op jit(solution)/shard_map/forward/pallas_call | solution.py:668
  148.2 0.8 copy.43
  152.5 39.2 %middle.1 = (bf16[768,768]{1,0:T(8,128)(2,1)}, bf16[768,3072]{1,0:T(8,128)(2,1)}, bf16[3072,768]{1,0:T(8,128)(2,1)}, f32[1,3072]{1,0:T(1,128)}, bf16[768,768]{1,...) custom-call(bf16[768,768]{1,0:T(8,128)(2,1)} %x_ref.5, ...), custom_call_target="tpu_custom_call" | custom-call | tf_op jit(solution)/shard_map/middle/pallas_call | solution.py:792
  191.7 0.7 reduce-scatter.8.cloned.1.call-update
  193.2 0.7 slice.91
  194.0 15.9 %swap_do.1.g_ref = bf16[4,3,384,128]{3,2,1,0:T(8,128)(2,1)S(1)} custom-call(bf16[4,3,384,128]{3,2,1,0:T(8,128)(2,1)S(1)} %copy-done.7), custom_call_target="tpu_custom_call" | custom-call | tf_op jit(solution)/shard_map/swap_do/pallas_call | solution.py:177
  209.9 1.0 copy-done.3
  211.4 57.0 %attend_back.1 = (bf16[3,3072,64]{2,1,0:T(8,128)(2,1)}, bf16[3,3072,64]{2,1,0:T(8,128)(2,1)}, bf16[3,3072,64]{2,1,0:T(8,128)(2,1)}) custom-call(s32[4]{0:T(128)} %convert_bitcast_fusion.reach_ref, bf16[3,3072,128]{2,1,0:T(8,128)(2,1)} %get-tuple-element.42.q_ref, bf16[3,3072,128]{2,1,0:T(8,128)(2,1)} %get-tuple-element.43.k_ref, ...), custom_call_target="tpu_custom_call" | custom-call | tf_op jit(solution)/shard_map/attend_back/pallas_call | solution.py:384
  268.5 1.8 copy-done.6
  270.3 12.1 %unproject.1 = (bf16[3072,768]{1,0:T(8,128)(2,1)}, f32[768,576]{1,0:T(8,128)S(1)}, f32[1,576]{1,0:T(1,128)S(1)}) custom-call(bf16[3,3072,64]{2,1,0:T(8,128)(2,1)S(1)} %copy-done.6, bf16[3,3072,64]{2,1,0:T(8,128)(2,1)} %get-tuple-element.48.dk_ref, bf16[3,3072,64]{2,1,0:T(8,128)(2,1)} %get-tuple-element.49.dv_ref, bf16[3072,768]{1,0:T(8,128)(2,1)} %bitcast.55, ...), custom_call_target="tpu_custom_call" | custom-call | tf_op jit(solution)/shard_map/unproject/pallas_call | solution.py:853
  282.4 3.9 dynamic-slice_bitcast_fusion
  286.9 1.9 fusion.2
  291.5 1.4 pad_maximum_fusion.x_ref
  292.9 35.5 %swap_grad.1 = bf16[16,64,576]{2,1,0:T(8,128)(2,1)S(1)} custom-call(bf16[16,64,576]{2,1,0:T(8,128)(2,1)S(1)} %pad_maximum_fusion.x_ref), custom_call_target="tpu_custom_call" | custom-call | tf_op jit(solution)/shard_map/swap_grad/pallas_call | solution.py:177
  328.4 2.9 fusion
  331.3 2.7 collective-permute-start.2
  334.0 1.3 collective-permute-start.3
  335.4 1.1 slice.105
  336.5 3.2 reshape.458
  339.7 1.3 reduce.1
  341.5 0.8 collective-permute-start.4
  344.3 1.3 collective-permute-start.5
  345.5 0.8 collective-permute-start.7
  346.3 3.6 collective-permute-done.4
  349.9 0.8 convert_add_fusion.3
  350.7 71.2 %reduce-scatter.6.cloned.1.call-done = bf16[48,3072]{1,0:T(8,128)(2,1)} async-done(((bf16[768,3072]{1,0:T(8,128)(2,1)}), bf16[48,3072]{1,0:T(8,128)(2,1)}) %reduce-scatter.6.cloned.1.call-update) | async-done | bytes 294928 | tf_op jit(solution)/shard_map/reduce_scatter | solution.py:968
  421.8 1.5 collective-permute-start.6
  423.3 1.6 convert_add_fusion.4
  424.9 1.0 copy-done.8
  425.9 1.3 copy-done.2
  427.2 1.3 copy-done.4
  428.5 1.3 copy-done.9
  429.7 5.0 %finish.1 = f32[768,768]{1,0:T(8,128)} custom-call(bf16[768,768]{1,0:T(8,128)(2,1)S(1)} %copy-done.2, f32[768,768]{1,0:T(8,128)} %get-tuple-element.41.dh_ref, f32[1,768]{1,0:T(1,128)S(1)} %reshape.454.g_ref, bf16[768,768]{1,0:T(8,128)(2,1)S(1)} %copy-done.4, bf16[768,768]{1,0:T(8,128)(2,1)} %collective-permute-done.two_ref, bf16[768,768]{1,0:T(8,128)(2,1)S(1)} %copy-done.9), custom_call_target="tpu_custom_call" | custom-call | tf_op jit(solution)/shard_map/finish/pallas_call | solution.py:883
  434.8 1.8 convert_add_fusion.1
  436.6 0.9 convert_add_fusion.2
  (88 shorter events, 11.5 us)
Async XLA Ops:
  7.2 20.4 %copy-start = (bf16[12,48,3072]{2,1,0:T(8,128)(2,1)S(1)}, bf16[12,48,3072]{2,1,0:T(8,128)(2,1)}, u32[]{:S(2)}) copy-start(bf16[12,48,3072]{2,1,0:T(8,128)(2,1)} %param.28) | copy-start | bytes 10616836
  7.2 337.1 %reduce-scatter.4.cloned.1.call-start = ((), (), s32[]{:S(2)}) async-start(), calls=%async_computation.3 | async-start | bytes 1253376 | tf_op jit(solution)/shard_map/reduce_scatter | solution.py:970
  191.7 153.8 %reduce-scatter.8.cloned.1.call-start = ((), (), s32[]{:S(2)}) async-start(), calls=%async_computation.5 | async-start | bytes 5013504 | tf_op jit(solution)/shard_map/reduce_scatter | solution.py:969
  192.4 229.4 %reduce-scatter.6.cloned.1.call-start = ((), (), s32[]{:S(2)}) async-start(), calls=%async_computation.4 | async-start | bytes 5013504 | tf_op jit(solution)/shard_map/reduce_scatter | solution.py:968
  192.5 1.6 copy-start.7
  209.9 1.0 copy-start.3
  211.4 57.0 %copy-start.5 = (bf16[768,576]{1,0:T(8,128)(2,1)S(1)}, bf16[768,576]{1,0:T(8,128)(2,1)}, u32[]{:S(2)}) copy-start(bf16[768,576]{1,0:T(8,128)(2,1)} %get-tuple-element.51.w_ref) | copy-start | bytes 2654212
  268.5 1.8 copy-start.6
  282.4 4.5 %copy-start.13 = (f32[8,768]{1,0:T(8,128)S(1)}, f32[8,768]{1,0:T(8,128)}, u32[]{:S(2)}) copy-start(f32[8,768]{1,0:T(8,128)} %get-tuple-element.55) | copy-start | bytes 73732
  286.3 42.1 %collective-permute-start.1 = (bf16[768,768]{1,0:T(8,128)(2,1)}, bf16[768,768]{1,0:T(8,128)(2,1)}, u32[]{:S(2)}, u32[]{:S(2)}) collective-permute-start(bf16[768,768]{1,0:T(8,128)(2,1)} %get-tuple-element.68), channel_id=1, source_target_pairs={{0,1},{1,0},{2,3},{3,2},{4,5},{5,4},{6,7},{7,6},{8,9},{9,8},{10,11... | collective-permute-start | bytes 3538952 | tf_op jit(solution)/shard_map/ppermute | solution.py:896
  286.6 138.3 %collective-permute-start = (bf16[768,768]{1,0:T(8,128)(2,1)}, bf16[768,768]{1,0:T(8,128)(2,1)}, u32[]{:S(2)}, u32[]{:S(2)}) collective-permute-start(bf16[768,768]{1,0:T(8,128)(2,1)} %get-tuple-element.69), channel_id=1, source_target_pairs={{0,1},{1,0},{2,3},{3,2},{4,5},{5,4},{6,7},{7,6},{8,9},{9,8},{10,11... | collective-permute-start | bytes 3538952 | tf_op jit(solution)/shard_map/ppermute | solution.py:896
  286.9 2.5 copy-start.12
  331.3 93.6 %collective-permute-start.2 = (bf16[768,768]{1,0:T(8,128)(2,1)}, bf16[768,768]{1,0:T(8,128)(2,1)S(1)}, u32[]{:S(2)}, u32[]{:S(2)}) collective-permute-start(bf16[768,768]{1,0:T(8,128)(2,1)} %fusion), channel_id=1, source_target_pairs={{0,2},{1,3},{2,0},{3,1},{4,6},{5,7},{6,4},{7,5},{8,10},{9,11},{10,... | collective-permute-start | bytes 3538952 | tf_op jit(solution)/shard_map/ppermute | solution.py:896
  334.0 8.4 %collective-permute-start.3 = (f32[576]{0:T(1024)S(1)}, f32[576]{0:T(1024)S(1)}, u32[]{:S(2)}, u32[]{:S(2)}) collective-permute-start(f32[576]{0:T(1024)S(1)} %add_reduce_fusion), channel_id=1, source_target_pairs={{0,16},{16,0},{1,17},{17,1},{2,18},{18,2},{3,19},{19,3},{4,20},{20... | collective-permute-start | bytes 6920 | tf_op jit(solution)/shard_map/ppermute | solution.py:903
  341.5 8.3 %collective-permute-start.4 = (bf16[48,2304]{1,0:T(8,128)(2,1)S(1)}, bf16[48,2304]{1,0:T(8,128)(2,1)S(1)}, u32[]{:S(2)}, u32[]{:S(2)}) collective-permute-start(bf16[48,2304]{1,0:T(8,128)(2,1)S(1)} %convert_element_type.132), channel_id=1, source_target_pairs={{0,16},{16,0},{1,17},{17,1},{2,18},{18,2},{3,19},{19,3},{4,20},{20... | collective-permute-start | bytes 663560 | tf_op jit(solution)/shard_map/ppermute | solution.py:903
  344.3 79.1 %collective-permute-start.5 = (bf16[48,768]{1,0:T(8,128)(2,1)}, bf16[48,768]{1,0:T(8,128)(2,1)S(1)}, u32[]{:S(2)}, u32[]{:S(2)}) collective-permute-start(bf16[48,768]{1,0:T(8,128)(2,1)} %reduce-scatter.4.cloned.1.call-done), channel_id=1, source_target_pairs={{0,16},{16,0},{1,17},{17,1},{2,18},{18,2},{3,19},{19,3},{4,20},{20... | collective-permute-start | bytes 221192 | tf_op jit(solution)/shard_map/ppermute | solution.py:903
  345.5 89.2 %collective-permute-start.7 = (bf16[192,768]{1,0:T(8,128)(2,1)}, bf16[192,768]{1,0:T(8,128)(2,1)}, u32[]{:S(2)}, u32[]{:S(2)}) collective-permute-start(bf16[192,768]{1,0:T(8,128)(2,1)} %reduce-scatter.8.cloned.1.call-done), channel_id=1, source_target_pairs={{0,16},{16,0},{1,17},{17,1},{2,18},{18,2},{3,19},{19,3},{4,20},{20... | collective-permute-start | bytes 884744 | tf_op jit(solution)/shard_map/ppermute | solution.py:903
  421.8 14.8 %collective-permute-start.6 = (bf16[48,3072]{1,0:T(8,128)(2,1)}, bf16[48,3072]{1,0:T(8,128)(2,1)S(1)}, u32[]{:S(2)}, u32[]{:S(2)}) collective-permute-start(bf16[48,3072]{1,0:T(8,128)(2,1)} %reduce-scatter.6.cloned.1.call-done), channel_id=1, source_target_pairs={{0,16},{16,0},{1,17},{17,1},{2,18},{18,2},{3,19},{19,3},{4,20},{20... | collective-permute-start | bytes 884744 | tf_op jit(solution)/shard_map/ppermute | solution.py:903
  424.9 1.0 copy-start.8
  425.9 1.3 copy-start.2
  427.2 1.3 copy-start.4
  428.5 1.3 copy-start.9
  429.7 5.0 %copy-start.10 = (bf16[192,768]{1,0:T(8,128)(2,1)S(1)}, bf16[192,768]{1,0:T(8,128)(2,1)}, u32[]{:S(2)}) copy-start(bf16[192,768]{1,0:T(8,128)(2,1)} %reduce-scatter.8.cloned.1.call-done) | copy-start | bytes 884740
  429.7 6.9 %copy-start.11 = (bf16[48,3072]{1,0:T(8,128)(2,1)S(1)}, bf16[48,3072]{1,0:T(8,128)(2,1)}, u32[]{:S(2)}) copy-start(bf16[48,3072]{1,0:T(8,128)(2,1)} %reduce-scatter.6.cloned.1.call-done) | copy-start | bytes 884740
  429.7 7.7 %copy-start.1 = (bf16[12,48,3072]{2,1,0:T(8,128)(2,1)S(1)}, bf16[12,48,3072]{2,1,0:T(8,128)(2,1)}, u32[]{:S(2)}) copy-start(bf16[12,48,3072]{2,1,0:T(8,128)(2,1)} %param.28) | copy-start | bytes 10616836
Sparse Core Ops, SparseCore 0:
  191.8 56.5 reduce-scatter.3
  252.2 91.0 reduce-scatter.7
  347.7 74.1 reduce-scatter.5

commit v3 on v2

--- a/solution.py
+++ b/solution.py
@@ -56,11 +56,13 @@
     return center * scale, scale
 
 
-def greet(peers):
+def greet(peers, replica=None):
     sem = pltpu.get_barrier_semaphore()
     for peer in peers:
         pl.semaphore_signal(sem, inc=1, device_id={"fsdp": peer}, device_id_type=MESH)
-    pl.semaphore_wait(sem, len(peers))
+    if replica is not None:
+        pl.semaphore_signal(sem, inc=1, device_id={"rep": replica}, device_id_type=MESH)
+    pl.semaphore_wait(sem, len(peers) + (replica is not None))
 
 
 def gather_kernel(n, parts, x_ref, w_ref, xg_ref, wg_ref, xs, xr, ws, wr, local):
@@ -400,6 +402,60 @@
     )(reach, q, k, v, f, g)
 
 
+def pick_kernel(index_ref, reach_ref, *refs):
+    vectors, (wq_ref, wo_ref, wf_ref, wp_ref), (small_ref, piece_ref, shard_ref) = (
+        refs[:8], refs[8:12], refs[12:],
+    )
+    index = index_ref[0]
+    rows = []
+    for ref in vectors:
+        bank = ref[...].astype(f32)
+        chosen = lax.broadcasted_iota(jnp.int32, bank.shape, 0) == index
+        rows.append(jnp.sum(jnp.where(chosen, bank, 0.0), axis=0, keepdims=True))
+    width = sum(row.shape[1] for row in rows)
+    rest = small_ref.shape[1] - width
+    small_ref[0:1, :] = jnp.concatenate(rows + [jnp.zeros((1, rest), f32)], axis=1).astype(bf16)
+    reach = reach_ref[0, 0]
+    lane = lax.broadcasted_iota(jnp.int32, (1, small_ref.shape[1]), 1)
+    code = jnp.where(lane == 0, reach // 16, jnp.where(lane == 1, lax.rem(reach, 16), 0))
+    small_ref[1:2, :] = code.astype(f32).astype(bf16)
+    for j in range(GROUP):
+        for part in range(3):
+            at = part * D + j * SLICE
+            piece_ref[j, :, part * SLICE : (part + 1) * SLICE] = wq_ref[0, :, at : at + SLICE]
+    shard_ref[:192, :] = wp_ref[0]
+    shard_ref[192:240, :] = wo_ref[0]
+    for c in range(FF // D):
+        shard_ref[240 + 48 * c : 288 + 48 * c, :] = wf_ref[0, :, c * D : (c + 1) * D]
+
+
+def pick(index, reach, vectors, wq, wo, wf, wp):
+    shape = jax.ShapeDtypeStruct
+    chosen = lambda bank: pl.BlockSpec((1,) + bank.shape[1:], lambda i, at: (at[0], 0, 0))
+    whole = lambda bank: pl.BlockSpec(bank.shape, lambda i, at: (0, 0))
+    fixed3 = lambda i, at: (0, 0, 0)
+    return pl.pallas_call(
+        pick_kernel,
+        name="pick",
+        out_shape=(
+            shape((2, 640), bf16), shape((GROUP, D // BLOCKS, WIDE), bf16), shape((UNIT, D), bf16),
+        ),
+        grid_spec=pltpu.PrefetchScalarGridSpec(
+            num_scalar_prefetch=1,
+            grid=(1,),
+            in_specs=[pl.BlockSpec(memory_space=pltpu.SMEM)]
+            + [whole(bank) for bank in vectors]
+            + [chosen(bank) for bank in (wq, wo, wf, wp)],
+            out_specs=(
+                pl.BlockSpec((2, 640), lambda i, at: (0, 0)),
+                pl.BlockSpec((GROUP, D // BLOCKS, WIDE), fixed3),
+                pl.BlockSpec((UNIT, D), lambda i, at: (0, 0)),
+            ),
+        ),
+        compiler_params=params(60),
+    )(index, reach, *vectors, wq, wo, wf, wp)
+
+
 def ring_of(me):
     chip, core = me // 2, lax.rem(me, 2)
     z, x = chip // 2, lax.rem(chip, 2)
@@ -417,14 +473,15 @@
 
 
 def forward_kernel(
-    x_ref, sm_ref, pc_ref, wp_ref, wo_ref, wf_ref,
+    x_ref, sm_ref, pc_ref, sh_ref,
     wall_ref, smo_ref, wq_ref, a_ref, q_ref, k_ref, v_ref, f_ref, o_ref,
     xg, smg, wg, w_s, q_s, k_s, v_s, f_s, o_s,
     local, sm_send, sm_recv, w_send, w_recv, x_send, x_recv, r_send, r_recv, n_send, n_recv,
-    o_send, o_recv, out_sem,
+    y_send, y_recv, o_send, o_recv, out_sem,
 ):
     n = BLOCKS
     me = lax.axis_index("fsdp")
+    rep = lax.axis_index("rep")
     pos = lax.rem(me, GROUP)
     base = me - pos
     near, far = me ^ 1, me ^ 2
@@ -439,40 +496,31 @@
             dst_ref=dst,
             send_sem=send,
             recv_sem=recv,
-            device_id={"fsdp": peer},
+            device_id=peer if isinstance(peer, dict) else {"fsdp": peer},
             device_id_type=MESH,
         )
 
-    greet([me ^ i for i in range(1, n)])
-
-    shard = [
-        pltpu.make_async_copy(wp_ref, wall_ref.at[me, pl.ds(0, 192)], local.at[0]),
-        pltpu.make_async_copy(wo_ref, wall_ref.at[me, pl.ds(192, 48)], local.at[1]),
-    ]
-    for c in range(4):
-        shard.append(
-            pltpu.make_async_copy(
-                wf_ref.at[:, pl.ds(c * D, D)], wall_ref.at[me, pl.ds(240 + 48 * c, 48)], local.at[2 + c]
-            )
-        )
-    own_x = pltpu.make_async_copy(x_ref, xg.at[pos], local.at[6])
-    own_w = pltpu.make_async_copy(pc_ref.at[pos], wg.at[me], local.at[7])
-    own_s = pltpu.make_async_copy(sm_ref, smg.at[me], local.at[8])
-    for copy in [own_s, own_x, own_w] + shard:
+    greet([me ^ i for i in range(1, n)], 1 - rep)
+
+    own_block = pltpu.make_async_copy(sh_ref, wall_ref.at[me], local.at[0])
+    own_x = pltpu.make_async_copy(x_ref, xg.at[pos], local.at[1])
+    own_w = pltpu.make_async_copy(pc_ref.at[pos], wg.at[me], local.at[2])
+    own_s = pltpu.make_async_copy(sm_ref, smg.at[me], local.at[3])
+    for copy in (own_s, own_w, own_x, own_block):
         copy.start()
 
-    smalls, slices = [], []
+    slices = []
+    for i in range(1, GROUP):
+        copy = remote(pc_ref.at[pos ^ i], wg.at[me], w_send.at[i], w_recv.at[i], me ^ i)
+        copy.start()
+        slices.append(copy)
+    smalls = []
     for i in range(1, n):
         copy = remote(sm_ref, smg.at[me], sm_send.at[i], sm_recv.at[i], me ^ i)
         copy.start()
         smalls.append(copy)
     beside = remote(x_ref, xg.at[pos], x_send.at[2 * parts], x_recv.at[2 * parts], near)
     beside.start()
-    for i in range(1, n):
-        peer = me ^ i
-        copy = remote(pc_ref.at[lax.rem(peer, GROUP)], wg.at[me], w_send.at[i], w_recv.at[i], peer)
-        copy.start()
-        slices.append(copy)
 
     def x_part(src, slot, part, i, peer):
         at = pl.ds(part * part_rows, part_rows)
@@ -482,44 +530,61 @@
     for copy in across:
         copy.start()
 
+    mine = pl.ds(pl.multiple_of(rep * (D // 2), D // 2), D // 2)
+    other = pl.ds(pl.multiple_of((1 - rep) * (D // 2), D // 2), D // 2)
+    sides = lambda t: (True, False) if t < 3 else (True,)
+    key = lambda t, right: t if right else 4 + t
+
+    def came(t, right):
+        return device(place - 1 - t if right else place + 1 + t)
+
     def hop(t, right):
-        at = place - t if right else place + t
-        block = wall_ref.at[device(at)]
-        i = t if right else 4 + t
-        return remote(block, block, r_send.at[i], r_recv.at[i], device(place + 1 if right else place - 1))
-
-    def beside_hop(t, right):
-        at = place - 1 - t if right else place + 1 + t
-        block = wall_ref.at[device(at)]
-        i = 1 + (t if right else 4 + t)
+        block = wall_ref.at[device(place - t if right else place + t), :, mine]
+        src = sh_ref.at[:, mine] if t == 0 else block
+        i = key(t, right)
+        return remote(src, block, r_send.at[i], r_recv.at[i], device(place + 1 if right else place - 1))
+
+    def to_near(t, right, columns, i):
+        block = wall_ref.at[came(t, right), :, columns]
         return remote(block, block, n_send.at[i], n_recv.at[i], near)
 
-    hops, shared = {}, []
+    def to_replica(t, right):
+        block = wall_ref.at[came(t, right), :, mine]
+        i = key(t, right)
+        return remote(block, block, y_send.at[i], y_recv.at[i], {"rep": 1 - rep})
+
+    def from_replica(t, right):
+        block = wall_ref.at[came(t, right), :, other]
+        i = key(t, right)
+        return remote(block, block, y_send.at[i], y_recv.at[i], {"rep": 1 - rep})
+
+    hops, sent, shared = {}, [], []
+
+    def begin(copy, keep):
+        copy.start()
+        keep.append(copy)
 
     def launch(t):
-        for right in (True, False):
-            if t < (4 if right else 3):
-                hops[t, right] = hop(t, right)
-                hops[t, right].start()
+        for right in sides(t):
+            hops[t, right] = hop(t, right)
+            hops[t, right].start()
 
     def arrive(t):
-        for right in (True, False):
-            if t < (4 if right else 3):
-                hops[t, right].wait_recv()
+        for right in sides(t):
+            hops[t, right].wait_recv()
         if t < 3:
             launch(t + 1)
-        for right in (True, False):
-            if t < (4 if right else 3):
-                copy = beside_hop(t, right)
-                copy.start()
-                shared.append(copy)
-
-    for copy in shard:
-        copy.wait()
+        for right in sides(t):
+            begin(to_replica(t, right), sent)
+            begin(to_near(t, right, mine, 1 + key(t, right)), shared)
+
+    def settle(t):
+        for right in sides(t):
+            from_replica(t, right).wait_recv()
+            begin(to_near(t, right, other, 8 + key(t, right)), shared)
+
     launch(0)
-    own_block = remote(wall_ref.at[me], wall_ref.at[me], n_send.at[0], n_recv.at[0], near)
-    own_block.start()
-    shared.append(own_block)
+    begin(remote(sh_ref, wall_ref.at[me], n_send.at[0], n_recv.at[0], near), shared)
 
     own_s.wait()
     for copy in smalls:
@@ -563,13 +628,23 @@
 
         lax.fori_loop(0, 2, some, 0)
 
+    own_w.wait()
+    for copy in slices:
+        copy.wait_recv()
+    group = pl.ds(base, GROUP)
+    wide = []
+    for i in range(1, n // GROUP):
+        begin(
+            remote(wg.at[group], wg.at[group], w_send.at[GROUP + i], w_recv.at[GROUP + i], me ^ (GROUP * i)),
+            wide,
+        )
     own_x.wait()
     norm(pos)
     beside.wait()
     norm(pos ^ 1)
-    own_w.wait()
-    for copy in slices:
+    for copy in wide:
         copy.wait_recv()
+    arrive(0)
     w_s[...] = wg[:, :rows48, :].reshape(D, WIDE)
     project_block(pos)
     project_block(pos ^ 1)
@@ -585,7 +660,7 @@
     project_block(pos ^ 2)
     norm(pos ^ 3)
     project_block(pos ^ 3)
-    arrive(0)
+    arrive(1)
 
     outs = [
         pltpu.make_async_copy(smg, smo_ref, out_sem.at[0]),
@@ -628,8 +703,13 @@
             at = p * TOK
             tile(at, past + [(at, T, causal)])
             tile(at + T, past + [(at, T, None), (at + T, T, causal)])
-        if h < 2:
-            arrive(1 + h)
+        if h == 0:
+            arrive(2)
+        if h == 1:
+            arrive(3)
+            settle(0)
+        if h == 2:
+            settle(1)
         for c in range(GROUP):
             at = c * TOK + PROMPT
             blocks = [(i * TOK, PROMPT, column < reaches[c] - i * PROMPT) for i in range(GROUP)]
@@ -653,14 +733,16 @@
             copy.start()
             outs.append(copy)
 
-    arrive(3)
-    for copy in across + smalls + slices + list(hops.values()):
+    settle(2)
+    settle(3)
+    for copy in across + smalls + slices + wide + list(hops.values()) + sent:
         copy.wait_send()
+    own_block.wait()
     for copy in shared + outs:
         copy.wait()
 
 
-def forward(x, small, pieces, wp, wo, wf):
+def forward(x, small, pieces, shard):
     dma = pltpu.SemaphoreType.DMA
     n = BLOCKS
     shape = jax.ShapeDtypeStruct
@@ -679,7 +761,7 @@
             shape(head, f32),
             shape((GROUP, OWN, PAIR, 2 * HEAD), bf16),
         ),
-        in_specs=[ANY] * 6,
+        in_specs=[ANY] * 4,
         out_specs=(ANY,) * 9,
         scratch_shapes=[
             pltpu.VMEM((GROUP, TOK, D), bf16),
@@ -691,23 +773,25 @@
             pltpu.VMEM(head, bf16),
             pltpu.VMEM(head, f32),
             pltpu.VMEM((OWN, GROUP, PAIR, 2 * HEAD), bf16),
-            dma((9,)),
+            dma((4,)),
             dma((n,)),
             dma((n,)),
-            dma((n,)),
-            dma((n,)),
+            dma((2 * GROUP,)),
+            dma((2 * GROUP,)),
             dma((9,)),
             dma((9,)),
             dma((7,)),
             dma((7,)),
-            dma((8,)),
-            dma((8,)),
+            dma((15,)),
+            dma((15,)),
+            dma((7,)),
+            dma((7,)),
             dma((OWN, GROUP)),
             dma((OWN, GROUP)),
             dma((14,)),
         ],
         compiler_params=params(60, collective_id=0, has_side_effects=True),
-    )(x, small, pieces, wp, wo, wf)
+    )(x, small, pieces, shard)
 
 
 def middle_kernel(
@@ -748,7 +832,7 @@
     du = (dot_nt(dy, wp) * slope).astype(bf16)
     dbf_ref[...] = jnp.sum(du.astype(f32), axis=0, keepdims=True)
     dn_s[...] += dot_nt(du, wf)
-    dwf_ref[...] = dot(bt_s[...], du).astype(bf16)
+    dwf_ref[...] = dot(bt_s[...], du).astype(bf16).reshape(dwf_ref.shape)
     dwp_ref[...] = dot_tn(m_low, dy).astype(bf16)
 
     @pl.when(step == pl.num_programs(0) - 1)
@@ -785,7 +869,7 @@
     square = pl.BlockSpec((TOK, D), fixed2)
     row = pl.BlockSpec((1, D), fixed2)
     heads = pl.BlockSpec((GROUP, OWN, PAIR, 2 * HEAD), fixed4)
-    columns = pl.BlockSpec((D, CHUNK), lambda i: (0, i))
+    columns = pl.BlockSpec((BLOCKS, 1, D // BLOCKS, D), lambda i: (0, i, 0, 0))
     down = pl.BlockSpec((CHUNK, D), lambda i: (i, 0))
     line = pl.BlockSpec((1, CHUNK), lambda i: (0, i))
     shape = jax.ShapeDtypeStruct
@@ -795,7 +879,7 @@
         grid=(FF // CHUNK,),
         out_shape=(
             shape((TOK, D), bf16),
-            shape((D, FF), bf16),
+            shape((BLOCKS, FF // D, D // BLOCKS, D), bf16),
             shape((FF, D), bf16),
             shape((1, FF), f32),
             shape((D, D), bf16),
@@ -825,6 +909,588 @@
     )(x, o, dy, wall, wall, wall, bo, gain, shift, bf, bp)
 
 
+ORDER = (4, -3, 3, -2, 2, -1, 1, 0)
+SMALL = 16
+
+
+def backward_kernel(
+    do_ref, q_ref, k_ref, v_ref, f_ref, a_ref, w_ref, x_ref, dh_ref, lines_ref, sums_ref, dbf_ref,
+    dwp_ref, dwo_ref, dwf_ref,
+    grad_ref, gq_ref, gp_ref, go_ref, gf_ref, small_ref,
+    g_b, q_s, k_s, v_s, f_b, a_s, w_s, x_s, dh_s, lines_s, sums_s, dbf_s,
+    near_b, mine_b, ring_b, fin_b, fin_r, fin_o,
+    g_s, dq_s, kt_s, dk_s, dv_s, dm_s, w_h, acc_s, db_s,
+    dw_b, z_b, j_b, j_r, rep_b, rep_r, gq_o,
+    dn_a, dn_b, dn_c, dn_ra, dn_rb, dn_rc, dn_o, sm_b, sm_r,
+    load, mine_sem, g_send, g_recv, n_send, n_recv, r_send, r_recv, fin_send, fin_recv,
+    z_send, z_recv, j_send, j_recv, rep_send, rep_recv, d_send, d_recv, s_send, s_recv, out_sem,
+):
+    n = BLOCKS
+    me = lax.axis_index("fsdp")
+    rep = lax.axis_index("rep")
+    pos = lax.rem(me, GROUP)
+    base = me - pos
+    level = me // GROUP
+    near, far = me ^ 1, me ^ 2
+    place, device = ring_of(me)
+    T = CONT
+    W3 = 3 * HEAD
+    other = {"rep": 1 - rep}
+
+    def remote(src, dst, send, recv, peer):
+        return pltpu.make_async_remote_copy(
+            src_ref=src,
+            dst_ref=dst,
+            send_sem=send,
+            recv_sem=recv,
+            device_id=peer if isinstance(peer, dict) else {"fsdp": peer},
+            device_id_type=MESH,
+        )
+
+    greet([me ^ i for i in range(1, n)], 1 - rep)
+
+    def do_copy(h, i):
+        return remote(do_ref.at[pos ^ i, h], g_b.at[pos, h], g_send.at[h, i], g_recv.at[h, i], me ^ i)
+
+    own_do = pltpu.make_async_copy(do_ref.at[pos], g_b.at[pos], load.at[0])
+    own_do.start()
+    for h in range(OWN):
+        for i in range(1, GROUP):
+            do_copy(h, i).start()
+
+    def f_copy(h):
+        return pltpu.make_async_copy(f_ref.at[h], f_b, load.at[1])
+
+    first = [
+        pltpu.make_async_copy(src, dst, load.at[2 + i])
+        for i, (src, dst) in enumerate(
+            ((q_ref, q_s), (k_ref, k_s), (v_ref, v_s), (lines_ref, lines_s), (w_ref, w_s))
+        )
+    ]
+    later = [
+        pltpu.make_async_copy(src, dst, load.at[7 + i])
+        for i, (src, dst) in enumerate(
+            ((a_ref, a_s), (x_ref, x_s), (dh_ref, dh_s), (sums_ref, sums_s), (dbf_ref, dbf_s))
+        )
+    ]
+    f_copy(0).start()
+    for copy in first:
+        copy.start()
+
+    cut = ((0, 192), (192, 48), (240, 192))
+
+    def near_copies(i):
+        d = device(place + ORDER[i]) ^ 1
+        return [
+            remote(ref.at[d], near_b.at[i, pl.ds(at, size)], n_send.at[i, k], n_recv.at[i, k], near)
+            for k, (ref, (at, size)) in enumerate(zip((dwp_ref, dwo_ref, dwf_ref), cut))
+        ]
+
+    def mine_copies(i):
+        d = device(place + ORDER[i])
+        return [
+            pltpu.make_async_copy(ref.at[d], mine_b.at[i % 4, pl.ds(at, size)], mine_sem.at[i, k])
+            for k, (ref, (at, size)) in enumerate(zip((dwp_ref, dwo_ref, dwf_ref), cut))
+        ]
+
+    for i in range(8):
+        for copy in near_copies(i):
+            copy.start()
+    for i in range(4):
+        for copy in mine_copies(i):
+            copy.start()
+    for copy in later:
+        copy.start()
+
+    def ready(i):
+        for copy in near_copies(i):
+            copy.wait_recv()
+        for copy in mine_copies(i):
+            copy.wait()
+
+    def ring_copy(t, right):
+        i = 2 * t if right else 2 * t + 1
+        slot = t if right else 4 + t
+        peer = device(place + 1 if right else place - 1)
+        return remote(near_b.at[i], ring_b.at[slot], r_send.at[slot], r_recv.at[slot], peer)
+
+    def rounds(some):
+        def chunk(c, carry):
+            some(pl.ds(pl.multiple_of(c * 144, 144), 144))
+            return carry
+
+        lax.fori_loop(0, UNIT // 144, chunk, 0)
+
+    def ring_step(t):
+        for right in (True, False) if t < 3 else (True,):
+            i = 2 * t if right else 2 * t + 1
+            ready(i)
+            if t > 0:
+                ring_copy(t - 1, right).wait_recv()
+            slot = (t if right else 4 + t) - 1
+
+            def some(at):
+                total = near_b[i, at, :].astype(f32) + mine_b[i % 4, at, :].astype(f32)
+                if t > 0:
+                    total = total + ring_b[slot, at, :].astype(f32)
+                near_b[i, at, :] = total.astype(bf16)
+
+            rounds(some)
+            ring_copy(t, right).start()
+            if i + 4 < 8:
+                for copy in mine_copies(i + 4):
+                    copy.start()
+
+    fin_copy = remote(fin_b, fin_r, fin_send, fin_recv, other)
+
+    def ring_end():
+        ready(7)
+        ring_copy(3, True).wait_recv()
+        ring_copy(2, False).wait_recv()
+
+        def some(at):
+            total = near_b[7, at, :].astype(f32) + mine_b[3, at, :].astype(f32)
+            fin_b[at, :] = (total + ring_b[3, at, :].astype(f32) + ring_b[6, at, :].astype(f32)).astype(bf16)
+
+        rounds(some)
+        fin_copy.start()
+
+    def z_copy(h, i):
+        return remote(
+            dw_b.at[h, level ^ i], z_b.at[h, i], z_send.at[h, i], z_recv.at[h, i], me ^ (GROUP * i)
+        )
+
+    def j_copy(h, i):
+        return remote(j_b.at[h, pos ^ i], j_r.at[pos, h], j_send.at[h, i], j_recv.at[h, i], me ^ i)
+
+    def gather_rows(h):
+        for i in range(1, GROUP):
+            z_copy(h, i).wait_recv()
+        total = dw_b[h, level].astype(f32)
+        for i in range(1, GROUP):
+            total = total + z_b[h, i].astype(f32)
+        total = total.astype(bf16).reshape(GROUP, D // n, W3)
+        j_b[h] = total
+        j_r[pos, h] = j_b[h, pos]
+        for i in range(1, GROUP):
+            j_copy(h, i).start()
+
+    half = lanes(PAIR) < HEAD
+    lane = lanes(PAIR)
+    causal = below(T, T, True)
+    key_row = lax.broadcasted_iota(jnp.int32, (PROMPT, T), 0).astype(f32)
+    narrow = lanes(T) < HEAD
+
+    first[3].wait()
+    first[4].wait()
+    for h in range(OWN):
+        w_h[h] = jnp.concatenate(
+            [
+                w_s[:, part * SLICE + h * HEAD : part * SLICE + (h + 1) * HEAD]
+                for part in (1, 2, 0)
+            ],
+            axis=1,
+        )
+    for copy in first[:3]:
+        copy.wait()
+    own_do.wait()
+
+    def one_head(h, carry):
+        for i in range(1, GROUP):
+            do_copy(h, i).wait_recv()
+        f_copy(h).wait()
+        for p in range(GROUP):
+            packed = g_b[p, h].astype(f32)
+            for i, block in enumerate((packed, pltpu.roll(packed, HEAD, 1))):
+                at = p * TOK + i * PAIR
+                prod = jnp.where(half, block * f_b[at : at + PAIR, :], 0.0)
+                inner = jnp.sum(prod, axis=1, keepdims=True)
+                g_s[at : at + PAIR, :] = split_columns(block, lane, inner)
+            kt_s[:, p * TOK : (p + 1) * TOK] = k_s[h, p * TOK : (p + 1) * TOK, :].T[:HEAD]
+
+        @pl.when(h + 1 < OWN)
+        def _():
+            f_copy(h + 1).start()
+
+        @pl.when(h == 0)
+        def _():
+            ring_step(0)
+
+        dq_s[...] = jnp.zeros_like(dq_s)
+
+        def block(keys, size, rows, count, mask, first, key_at):
+            kb = k_s[h, pl.ds(keys, size), :]
+            vb = v_s[h, pl.ds(keys, size), :]
+            q = q_s[h, pl.ds(rows, count), :]
+            g = g_s[pl.ds(rows, count), :]
+            probs = jnp.exp(dot_nt(kb, q))
+            if mask is not None:
+                probs = jnp.where(mask, probs, 0.0)
+            ds = (probs * dot_nt(vb, g)).astype(bf16)
+            dv = dot(probs.astype(bf16), g)
+            dk = dot(ds, q)
+            at = pl.ds(key_at, size)
+            dv_s[at, :] = dv if first else dv_s[at, :] + dv
+            dk_s[at, :] = dk if first else dk_s[at, :] + dk
+            dq_s[:, pl.ds(rows, count)] += dot(kt_s[:, pl.ds(keys, size)], ds)
+
+        def flush(at, size):
+            for i in range(size // T):
+                part = slice(i * T, (i + 1) * T)
+                pair = jnp.where(narrow, dk_s[part, :], pltpu.roll(dv_s[part, :], HEAD, 1))
+                dm_s[h, pl.ds(at + i * T, T), : 2 * HEAD] = pair.astype(bf16)
+
+        for p in range(GROUP):
+            base_row = p * TOK
+            block(base_row, T, base_row, T, causal, True, 0)
+            block(base_row + T, T, base_row + T, T, causal, True, T)
+            block(base_row, T, base_row + T, T, None, False, 0)
+
+            def past(i, carry):
+                rows = pl.multiple_of(i * TOK, CONT)
+                block(base_row, PROMPT, rows, PROMPT, None, False, 0)
+                return carry
+
+            lax.fori_loop(p + 1, GROUP, past, 0)
+
+            def cont(c, carry):
+                rows = pl.multiple_of(c * TOK + PROMPT, CONT)
+                code = lines_s[base + c, 1:2, 0:128].astype(f32)
+                reach = code[:, 0:1] * 16.0 + code[:, 1:2] - p * PROMPT
+                block(base_row, PROMPT, rows, T, key_row < reach, False, 0)
+                return carry
+
+            lax.fori_loop(0, GROUP, cont, 0)
+            flush(base_row, PROMPT)
+            if p == 1:
+
+                @pl.when(h > 0)
+                def _():
+                    gather_rows(h - 1)
+
+        def own(c, carry):
+            at = pl.multiple_of(c * TOK + PROMPT, CONT)
+            block(at, T, at, T, causal, True, 0)
+            flush(at, T)
+            return carry
+
+        lax.fori_loop(0, GROUP, own, 0)
+        for i in range(ROWS // PROMPT):
+            at = i * PROMPT
+            dm_s[h, at : at + PROMPT, 2 * HEAD :] = (dq_s[:, at : at + PROMPT].T * 0.125).astype(bf16)
+
+        @pl.when(h == 0)
+        def _():
+            later[0].wait()
+
+        def weight():
+            dw_t = jnp.zeros((W3, D), f32)
+            for i in range(GROUP):
+                rows = slice(i * TOK, (i + 1) * TOK)
+                dw_t = dw_t + dot_tn(dm_s[h, rows, :], a_s[rows, :])
+            acc_s[...] = dw_t
+            dw = acc_s[...].T
+            dw_b[h] = dw.astype(bf16).reshape(GROUP, D // GROUP, W3)
+            for i in range(1, GROUP):
+                z_copy(h, i).start()
+            db = jnp.zeros((1, W3), f32)
+            for i in range(GROUP):
+                db = db + jnp.sum(dm_s[h, i * TOK : (i + 1) * TOK, :].astype(f32), axis=0, keepdims=True)
+            hi = db.astype(bf16)
+            mid = (db - hi.astype(f32)).astype(bf16)
+            low = (db - hi.astype(f32) - mid.astype(f32)).astype(bf16)
+            split = jnp.concatenate([hi, mid, low, jnp.zeros((13, W3), bf16)], axis=0)
+            shift_rows = dot_nt(split, w_h[h])
+            shift_part = jnp.sum(shift_rows, axis=0, keepdims=True)
+            ones = jnp.ones((8, W3), f32)
+            gain_rows = lax.dot_general(
+                ones,
+                w_h[h].astype(f32) * dw,
+                (((1,), (1,)), ((), ())),
+                precision=lax.Precision.HIGHEST,
+                preferred_element_type=f32,
+            )
+            db_s[h, 0:1, :W3] = db
+            db_s[h, 1:2, W3 : W3 + D] = shift_part
+            db_s[h, 2:3, W3 : W3 + D] = gain_rows[0:1]
+
+        @pl.when(h < OWN - 1)
+        def _():
+            weight()
+            ring_step_at(h)
+
+        @pl.when(h == OWN - 1)
+        def _():
+            ring_step(3)
+            send_rows()
+            weight()
+
+        return carry
+
+    def ring_step_at(h):
+        @pl.when(h == 0)
+        def _():
+            ring_step(1)
+
+        @pl.when(h == 1)
+        def _():
+            ring_step(2)
+
+    def dn_rows(block, part):
+        rows = pl.ds(pl.multiple_of((pos ^ block) * TOK + part * PAIR, PAIR), PAIR)
+        total = dot_nt(dm_s[0, rows, :], w_h[0])
+        for h in range(1, OWN):
+            total = total + dot_nt(dm_s[h, rows, :], w_h[h])
+        return total
+
+    def dn_copy(kind, part):
+        at = pl.ds(part * PAIR, PAIR)
+        src, dst, peer = ((dn_a, dn_ra, near), (dn_b, dn_rb, far), (dn_c, dn_rc, near))[kind]
+        i = 2 * kind + part
+        return remote(src.at[at], dst.at[at], d_send.at[i], d_recv.at[i], peer)
+
+    def send_rows():
+        for part in range(2):
+            dn_a[part * PAIR : (part + 1) * PAIR, :] = dn_rows(3, part).astype(bf16)
+            dn_copy(0, part).start()
+        for part in range(2):
+            at = slice(part * PAIR, (part + 1) * PAIR)
+            rows = dn_rows(2, part)
+            dn_copy(0, part).wait_recv()
+            dn_b[at, :] = (rows + dn_ra[at, :].astype(f32)).astype(bf16)
+            dn_copy(1, part).start()
+        for part in range(2):
+            dn_c[part * PAIR : (part + 1) * PAIR, :] = dn_rows(1, part).astype(bf16)
+            dn_copy(2, part).start()
+
+    lax.fori_loop(0, OWN, one_head, 0)
+
+    for copy in later[1:]:
+        copy.wait()
+    for part in range(2):
+        dn_o[part * PAIR : (part + 1) * PAIR, :] = dn_rows(0, part)
+
+    rows48 = D // n
+    gain = jnp.concatenate([lines_s[d, 0:1, 0:rows48] for d in range(n)], axis=1).astype(f32)
+    shift = jnp.concatenate([lines_s[d, 0:1, rows48 : 2 * rows48] for d in range(n)], axis=1).astype(f32)
+    d_shift = db_s[0, 1:2, W3 : W3 + D] + db_s[1, 1:2, W3 : W3 + D] + db_s[2, 1:2, W3 : W3 + D]
+    d_gain = db_s[0, 2:3, W3 : W3 + D] + db_s[1, 2:3, W3 : W3 + D] + db_s[2, 2:3, W3 : W3 + D]
+    blank = jnp.zeros((1, D - SLICE), f32)
+
+    def biases(lo):
+        row = jnp.concatenate([db_s[h, 0:1, lo : lo + HEAD] for h in range(OWN)] + [blank], axis=1)
+        return pltpu.roll(jnp.broadcast_to(row, (8, D)), pos * SLICE, 1)[0:1]
+
+    sm_b[0] = jnp.concatenate(
+        [
+            (d_gain - shift * d_shift) / gain,
+            d_shift,
+            biases(2 * HEAD),
+            biases(HEAD),
+            sums_s[3:4, :],
+            sums_s[1:2, :],
+            sums_s[2:3, :],
+            sums_s[0:1, :],
+        ]
+        + [dbf_s[0:1, c * D : (c + 1) * D] for c in range(FF // D)]
+        + [jnp.zeros((SMALL - 12, D), f32)],
+        axis=0,
+    )
+    peers = [me ^ 1, me ^ 2, me ^ 4, me ^ 8, other]
+
+    def small_copy(i):
+        return remote(sm_b.at[i], sm_r.at[i], s_send.at[i], s_recv.at[i], peers[i])
+
+    def small_step(i):
+        small_copy(i).wait_recv()
+        sm_b[i + 1] = sm_b[i] + sm_r[i]
+        if i < 4:
+            small_copy(i + 1).start()
+
+    small_copy(0).start()
+    small_step(0)
+    gather_rows(OWN - 1)
+    small_step(1)
+    small_step(2)
+    for h in range(OWN):
+        for i in range(1, GROUP):
+            j_copy(h, i).wait_recv()
+    rep_b[...] = j_r[...]
+    rep_copy = remote(rep_b, rep_r, rep_send, rep_recv, other)
+    rep_copy.start()
+    ring_end()
+    small_step(3)
+
+    outs = []
+    for part in range(2):
+        at = slice(part * PAIR, (part + 1) * PAIR)
+        dn_copy(2, part).wait_recv()
+        dn_copy(1, part).wait_recv()
+        n_rows, r = moments(x_s[at, :].astype(f32))
+        e = (dn_o[at, :] + dn_rb[at, :].astype(f32) + dn_rc[at, :].astype(f32)) * gain
+        lean = jnp.mean(e, axis=-1, keepdims=True) + n_rows * jnp.mean(e * n_rows, axis=-1, keepdims=True)
+        dh_s[at, :] = dh_s[at, :] + r * (e - lean)
+        copy = pltpu.make_async_copy(dh_s.at[at], grad_ref.at[at], out_sem.at[part])
+        copy.start()
+        outs.append(copy)
+
+    small_step(4)
+    total = sm_b[5]
+    turned = pltpu.roll(total, lax.rem(n - me, n) * rows48, 1)
+    eighth = lax.rem(me, 8)
+    biased = pltpu.roll(total, lax.rem(8 - eighth, 8) * (2 * rows48), 1)
+    quarter = lax.rem(me, 4)
+    wide = pltpu.roll(total, lax.rem(4 - quarter, 4) * (4 * rows48), 1)
+    row = lax.broadcasted_iota(jnp.int32, (SMALL, D), 0)
+    bias_row = jnp.sum(jnp.where(row == 2 + me // 8, biased, 0.0), axis=0, keepdims=True)
+    wide_row = jnp.sum(jnp.where(row == 8 + me // 4, wide, 0.0), axis=0, keepdims=True)
+    small_copy(0).wait_send()
+    sm_b[0] = jnp.where(row == 2, bias_row, jnp.where(row == 3, wide_row, turned))
+    copy = pltpu.make_async_copy(sm_b.at[0], small_ref, out_sem.at[2])
+    copy.start()
+    outs.append(copy)
+
+    rep_copy.wait_recv()
+    for part, (at, piece) in enumerate(((2 * HEAD, 0), (0, 1), (HEAD, 2))):
+        row = jnp.concatenate(
+            [
+                rep_b[j, h, :, at : at + HEAD].astype(f32) + rep_r[j, h, :, at : at + HEAD].astype(f32)
+                for j in range(GROUP)
+                for h in range(OWN)
+            ],
+            axis=1,
+        )
+        gq_o[:, piece * D : (piece + 1) * D] = row
+    copy = pltpu.make_async_copy(gq_o, gq_ref, out_sem.at[3])
+    copy.start()
+    outs.append(copy)
+
+    fin_copy.wait_recv()
+
+    def some(at):
+        fin_o[at, :] = fin_b[at, :].astype(f32) + fin_r[at, :].astype(f32)
+
+    rounds(some)
+    targets = [(gp_ref, 0, 192), (go_ref, 192, 48)]
+    targets += [(gf_ref.at[:, pl.ds(c * D, D)], 240 + 48 * c, 48) for c in range(FF // D)]
+    for i, (ref, at, size) in enumerate(targets):
+        copy = pltpu.make_async_copy(fin_o.at[pl.ds(at, size)], ref, out_sem.at[4 + i])
+        copy.start()
+        outs.append(copy)
+
+    for h in range(OWN):
+        for i in range(1, GROUP):
+            for copy in (do_copy(h, i), z_copy(h, i), j_copy(h, i)):
+                copy.wait_send()
+    for i in range(8):
+        for copy in near_copies(i):
+            copy.wait_send()
+    for t in range(4):
+        for right in (True, False) if t < 3 else (True,):
+            ring_copy(t, right).wait_send()
+    for kind in range(3):
+        for part in range(2):
+            dn_copy(kind, part).wait_send()
+    for i in range(1, 5):
+        small_copy(i).wait_send()
+    rep_copy.wait_send()
+    fin_copy.wait_send()
+    for copy in outs:
+        copy.wait()
+
+
+def backward(do, q, k, v, f, a, w, x, dh, lines, sums, dbf, dwp, dwo, dwf):
+    dma = pltpu.SemaphoreType.DMA
+    n = BLOCKS
+    shape = jax.ShapeDtypeStruct
+    vmem = pltpu.VMEM
+    rows = D // n
+    head = (OWN, ROWS, 2 * HEAD)
+    W3 = 3 * HEAD
+    pairs = (OWN, GROUP)
+    return pl.pallas_call(
+        backward_kernel,
+        name="backward",
+        out_shape=(
+            shape((TOK, D), f32),
+            shape((rows, 3 * D), f32),
+            shape((FF // n, D), f32),
+            shape((rows, D), f32),
+            shape((rows, FF), f32),
+            shape((SMALL, D), f32),
+        ),
+        in_specs=[ANY] * 15,
+        out_specs=(ANY,) * 6,
+        scratch_shapes=[
+            vmem((GROUP, OWN, PAIR, 2 * HEAD), bf16),
+            vmem(head, bf16),
+            vmem(head, bf16),
+            vmem(head, bf16),
+            vmem(head[1:], f32),
+            vmem((ROWS, D), bf16),
+            vmem((D, WIDE), bf16),
+            vmem((TOK, D), bf16),
+            vmem((TOK, D), f32),
+            vmem(lines.shape, bf16),
+            vmem(sums.shape, f32),
+            vmem(dbf.shape, f32),
+            vmem((8, UNIT, D), bf16),
+            vmem((4, UNIT, D), bf16),
+            vmem((7, UNIT, D), bf16),
+            vmem((UNIT, D), bf16),
+            vmem((UNIT, D), bf16),
+            vmem((UNIT, D), f32),
+            vmem((ROWS, 2 * HEAD), bf16),
+            vmem((HEAD, ROWS), f32),
+            vmem((HEAD, ROWS), bf16),
+            vmem((PROMPT, 2 * HEAD), f32),
+            vmem((PROMPT, 2 * HEAD), f32),
+            vmem((OWN, ROWS, W3), bf16),
+            vmem((OWN, D, W3), bf16),
+            vmem((W3, D), f32),
+            vmem((OWN, 8, W3 + D), f32),
+            vmem((OWN, GROUP, D // GROUP, W3), bf16),
+            vmem((OWN, GROUP, D // GROUP, W3), bf16),
+            vmem((OWN, GROUP, rows, W3), bf16),
+            vmem((GROUP, OWN, rows, W3), bf16),
+            vmem((GROUP, OWN, rows, W3), bf16),
+            vmem((GROUP, OWN, rows, W3), bf16),
+            vmem((rows, 3 * D), f32),
+            vmem((TOK, D), bf16),
+            vmem((TOK, D), bf16),
+            vmem((TOK, D), bf16),
+            vmem((TOK, D), bf16),
+            vmem((TOK, D), bf16),
+            vmem((TOK, D), bf16),
+            vmem((TOK, D), f32),
+            vmem((6, SMALL, D), f32),
+            vmem((5, SMALL, D), f32),
+            dma((12,)),
+            dma((8, 3)),
+            dma(pairs),
+            dma(pairs),
+            dma((8, 3)),
+            dma((8, 3)),
+            dma((7,)),
+            dma((7,)),
+            dma,
+            dma,
+            dma(pairs),
+            dma(pairs),
+            dma(pairs),
+            dma(pairs),
+            dma,
+            dma,
+            dma((6,)),
+            dma((6,)),
+            dma((5,)),
+            dma((5,)),
+            dma((10,)),
+        ],
+        compiler_params=params(63, collective_id=4, has_side_effects=True),
+    )(do, q, k, v, f, a, w, x, dh, lines, sums, dbf, dwp, dwo, dwf)
+
+
 def unproject_kernel(dq_ref, dk_ref, dv_ref, a_ref, w_ref, dn_ref, dw_ref, db_ref):
     step = pl.program_id(0)
     mixed = jnp.concatenate(
@@ -921,16 +1587,7 @@
     vectors = (pre_gain, pre_shift, b_qv, b_out, mid_gain, mid_shift, b_fc, b_proj)
     sizes = [bank.shape[1] for bank in vectors]
     count = sum(sizes)
-    small = jnp.concatenate([chosen(bank) for bank in vectors])
     high = -(-(rows + 2) // 16) * 16
-    reach = prefix_len[0]
-    reach_row = jnp.concatenate([reach // 16, reach % 16]).astype(bf16)
-    wq = chosen(w_qkv).reshape(rows, 3, GROUP, SLICE).transpose(2, 0, 1, 3).reshape(GROUP, rows, WIDE)
-    width = -(-WIDE // 128) * 128
-    extra = jnp.stack(
-        [jnp.pad(small, (0, width - count)), jnp.pad(reach_row, (0, width - reach_row.shape[0]))]
-    )
-    wo, wf, wp = chosen(w_out), chosen(w_fc), chosen(w_proj)
     cuts = [sum(sizes[:i]) for i in range(len(sizes) + 1)]
 
     def vectors_of(lines):
@@ -941,12 +1598,21 @@
             smalls[:, cuts[i] : cuts[i + 1]].reshape(1, -1) for i in range(len(sizes))
         ], reaches.astype(jnp.int32)
 
-    if n == BLOCKS:
-        wall, lines, wq, a_low, qx, k, v, o_full, o_recv = forward(block_input, extra, wq, wp, wo, wf)
+    fused = n == BLOCKS and lax.axis_size("rep") == 2
+    if fused:
+        small, pieces, shard = pick(tie_index, prefix_len, vectors, w_qkv, w_out, w_fc, w_proj)
+        wall, lines, wq, a_low, qx, k, v, o_full, o_recv = forward(block_input, small, pieces, shard)
         a_low = a_low.reshape(ROWS, D)
         (g1, s1, _, bo, g2, s2, bf, bp), reaches = vectors_of(lines)
     else:
-        extra = jnp.pad(extra[:, :WIDE], ((0, high - rows - 2), (0, 0)))
+        small = jnp.concatenate([chosen(bank) for bank in vectors])
+        reach = prefix_len[0]
+        reach_row = jnp.concatenate([reach // 16, reach % 16]).astype(bf16)
+        wq = chosen(w_qkv).reshape(rows, 3, GROUP, SLICE).transpose(2, 0, 1, 3)
+        wq = wq.reshape(GROUP, rows, WIDE)
+        extra = jnp.stack([jnp.pad(line, (0, WIDE - line.shape[0])) for line in (small, reach_row)])
+        wo, wf, wp = chosen(w_out), chosen(w_fc), chosen(w_proj)
+        extra = jnp.pad(extra, ((0, high - rows - 2), (0, 0)))
         pieces = jnp.concatenate([wq, jnp.broadcast_to(extra, (GROUP,) + extra.shape)], axis=1)
         wo = lax.all_gather(wo, "fsdp", axis=0, tiled=True).reshape(BLOCKS, -1, D)
         wf = lax.all_gather(wf, "fsdp", axis=0, tiled=True)
@@ -965,6 +1631,16 @@
     y, dwf, dwp, dbf, dwo, dh, do_send, sums = middle(
         block_input, o_recv, cotangent, wall, bo, g2, s2, bf, bp
     )
+    if fused:
+        grad, dwq, dwp, dwo, dwf, sums = backward(
+            do_send, qx, k, v, o_full, a_low, wq, block_input, dh, lines, sums, dbf,
+            dwp.reshape(BLOCKS, -1, D), dwo.reshape(BLOCKS, -1, D), dwf.reshape(BLOCKS, -1, D),
+        )
+        rows48 = D // n
+        dg1, ds1, dbo, dg2, ds2, dbp = (sums[i, :rows48] for i in (0, 1, 4, 5, 6, 7))
+        dbqv, dbf = sums[2, : 2 * rows48], sums[3, : 4 * rows48]
+        return (y, grad, dg1, ds1, dwq, dbqv, dwo, dbo, dg2, ds2, dwf, dbf, dwp, dbp)
+    dwf = dwf.transpose(0, 2, 1, 3).reshape(D, FF)
     dwf = lax.psum_scatter(dwf, "fsdp", scatter_dimension=0, tiled=True)
     dwp = lax.psum_scatter(dwp, "fsdp", scatter_dimension=0, tiled=True)
     dwo = lax.psum_scatter(dwo, "fsdp", scatter_dimension=0, tiled=True)

time: 450 us -> 306 us (0.68)
  waiting for transfers between devices: 76.1 us -> 0 us
  local copies, waits for them, and re-layouts: 46.2 us -> 13.8 us
  other arithmetic: 14.8 us -> 0.81 us
  between operations: 16 us -> 2.44 us
  starting transfers between devices: 8.96 us -> 0 us
    reduce_scatter x3 -> x0, waiting for transfers between devices: 71.2 us -> none  [the longest x1 71.2 us: body(): dwf = lax.psum_scatter(dwf, 'fsdp', scatter_dimension=0, tiled=True)]
    pallas_call x5 -> x2, Pallas kernels: 125 us -> 147 us  [the longest x1 144 us: backward(): pl.pallas_call(backward_kernel, name='backward', out_shape=(shape((TOK, D...]
    pallas_call x1, Pallas kernels: 118 us -> 98.7 us  [forward(): pl.pallas_call(forward_kernel, name='forward', out_shape=(shape((n, UNIT,...]
    squeeze x8 -> x2, local copies, waits for them, and re-layouts: 12.2 us -> 2.62 us  [the longest x1 1.43 us: body(): sums[i, :rows48]]
    ppermute x8 -> x0, starting transfers between devices: 8.84 us -> none  [the longest x5 5.67 us: over_replicas(): other = lax.ppermute(held, 'rep', [(0, 1), (1, 0)])]
    reshape x3 -> x0, local copies, waits for them, and re-layouts: 7.13 us -> none  [the longest x2 3.94 us: body(): chosen(w_qkv).reshape(rows, 3, GROUP, SLICE).transpose(2, 0, 1, 3)]
    add x5 -> x0, other arithmetic: 5.09 us -> none  [over_replicas(): return held.astype(f32) + other.astype(f32)]
    concatenate x8 -> x0, local copies, waits for them, and re-layouts: 4.86 us -> none  [the longest x1 4.09 us: body(): small = jnp.concatenate([chosen(bank) for bank in vectors])]
  transfers between devices with their start and end apart: 11 -> 0, of which waited for: 2 -> 0; matrix products, arithmetic and copies ran while one was open for 6% -> 0% of each run, Pallas kernels for 28% -> 0%
where the time goes in v3:
time: 306 us; the launch traced here: 302 us
  Pallas kernels  285 us (93%)
  local copies, waits for them, and re-layouts  13.8 us (5%)
    pallas_call x1, Pallas kernels, backward(): pl.pallas_call(backward_kernel, name='backward', out_shape=(shape((TOK, D...  144 us
    pallas_call x1, Pallas kernels, forward(): pl.pallas_call(forward_kernel, name='forward', out_shape=(shape((n, UNIT,...  98.7 us
    pallas_call x1, Pallas kernels, middle(): pl.pallas_call(middle_kernel, name='middle', grid=(FF // CHUNK,), out_sha...  39.3 us
    unnamed x14, local copies, waits for them, and re-layouts  6.39 us

profile of v3, /device:TPU:0, one launch (start us, length us, event | category | flops | bytes accessed | tf_op | source)
XLA Modules:
  0.0 301.9 jit_solution(13836048747825617038)
XLA Ops:
  1.9 2.4 pick.1
  4.3 98.7 %forward.1 = (bf16[16,432,768]{2,1,0:T(8,128)(2,1)}, bf16[16,2,640]{2,1,0:T(2,128)(2,1)}, bf16[768,576]{1,0:T(8,128)(2,1)}, bf16[4,768,768]{2,1,0:T(8,128)(2,1)}...) custom-call(bf16[768,768]{1,0:T(8,128)(2,1)} %x_ref.5, ...), custom_call_target="tpu_custom_call" | custom-call | tf_op jit(solution)/shard_map/forward/pallas_call | solution.py:750
  103.0 0.8 slice_convert_fusion
  103.8 0.1 slice.59
  103.9 0.1 fusion
  104.0 0.7 reshape.60.bf_ref
  104.7 0.7 reshape.61.bp_ref
  105.3 0.7 reshape.59.s_ref
  106.0 0.7 reshape.58.g_ref
  106.7 0.7 reshape.57.bo_ref
  107.4 39.3 %middle.1 = (bf16[768,768]{1,0:T(8,128)(2,1)}, bf16[16,4,48,768]{3,2,1,0:T(8,128)(2,1)}, bf16[3072,768]{1,0:T(8,128)(2,1)}, f32[1,3072]{1,0:T(1,128)}, bf16[768,...) custom-call(bf16[768,768]{1,0:T(8,128)(2,1)} %x_ref.5, ...), custom_call_target="tpu_custom_call" | custom-call | tf_op jit(solution)/shard_map/middle/pallas_call | solution.py:876
  146.7 144.5 %backward.1 = (f32[768,768]{1,0:T(8,128)}, f32[48,2304]{1,0:T(8,128)}, f32[192,768]{1,0:T(8,128)}, f32[48,768]{1,0:T(8,128)}, f32[48,3072]{1,0:T(8,128)}, /*index=5*/f32[16,768]{1,0:T(8,128)}) custom-call(bf16[4,3,384,128]{3,2,1,0:T(8,128)(2,1)} %get-tuple-element.47.do_ref, bf16[3,3072,128]{2,1,0:T(8,128)(2,1)} %get-tuple-element.48.q_ref, ...), custom_call_target="tpu_custom_call" | custom-call | tf_op jit(solution)/shard_map/backward/pallas_call | solution.py:1411
  291.2 1.2 slice_bitcast_fusion.4
  292.4 1.3 slice.54
  293.7 1.4 slice_bitcast_fusion
  295.1 0.0 copy-start.2
  295.1 0.0 copy-start.3
  295.1 0.0 copy-start.1
  295.1 3.3 %copy.40 = f32[768,768]{1,0:T(8,128)} copy(f32[768,768]{1,0:T(8,128)} %get-tuple-element.91) | data formatting | bytes 4718592
  298.4 0.0 copy-done.2
  298.4 0.0 copy-start
  298.4 0.8 copy.41
  299.2 0.0 copy-done.3
  299.2 0.7 copy.42
  299.9 0.0 copy-done.1
  299.9 0.8 copy.43
  300.7 0.0 copy-done
  300.7 0.8 copy.44
  (1 shorter events, 0.0 us)
Async XLA Ops:
  295.1 3.3 %copy-start.2 = (f32[48,2304]{1,0:T(8,128)S(1)}, f32[48,2304]{1,0:T(8,128)}, u32[]{:S(2)}) copy-start(f32[48,2304]{1,0:T(8,128)} %get-tuple-element.94) | copy-start | bytes 1327108
  295.1 4.1 %copy-start.3 = (f32[48,768]{1,0:T(8,128)S(1)}, f32[48,768]{1,0:T(8,128)}, u32[]{:S(2)}) copy-start(f32[48,768]{1,0:T(8,128)} %get-tuple-element.96) | copy-start | bytes 442372
  295.1 4.8 %copy-start.1 = (f32[48,3072]{1,0:T(8,128)S(1)}, f32[48,3072]{1,0:T(8,128)}, u32[]{:S(2)}) copy-start(f32[48,3072]{1,0:T(8,128)} %get-tuple-element.100) | copy-start | bytes 1769476
  298.4 2.2 copy-start

commit v4 on v3

--- a/solution.py
+++ b/solution.py
@@ -25,6 +25,7 @@
 UNIT = 432
 NEG = -1e30
 EPS = 1e-5
+PACK = ((512, 640, 128, 0), (0, 256, 256, 128))
 GELU_A = 0.7978845608028654
 GELU_B = 0.044715
 
@@ -623,7 +624,7 @@
                 v = mixed[:, 2 * SLICE + h * HEAD : 2 * SLICE + (h + 1) * HEAD]
                 q_s[h, out, :] = jnp.concatenate([q.astype(bf16), jnp.zeros_like(ones)], axis=1)
                 k_s[h, out, :] = jnp.concatenate([k, ones], axis=1)
-                v_s[h, out, :] = jnp.concatenate([v, ones], axis=1)
+                v_s[h, out, :] = jnp.concatenate([ones, v], axis=1)
             return carry
 
         lax.fori_loop(0, 2, some, 0)
@@ -674,7 +675,6 @@
 
     lane = lanes(T)
     causal = below(T, T, False)
-    half = lanes(PAIR) < HEAD
     code = [smg[base + c, 1:2, 0:2].astype(f32) for c in range(GROUP)]
     reaches = [c[:, 0:1] * 16.0 + c[:, 1:2] for c in code]
     column = lax.broadcasted_iota(jnp.int32, (T, PROMPT), 1).astype(f32)
@@ -693,7 +693,7 @@
             total = jnp.zeros((T, 2 * HEAD), f32)
             for s, (start, size, _) in zip(scores, blocks):
                 total += dot(jnp.exp(s - peak).astype(bf16), v_s[h, pl.ds(start, size), :])
-            mass = total[:, HEAD : HEAD + 1]
+            mass = total[:, 0:1]
             f_s[h, pl.ds(at, T), :] = total / mass
             lse = peak + jnp.log(mass)
             q_s[h, pl.ds(at, T), :] = split_columns(q.astype(f32), lane, lse)
@@ -715,9 +715,11 @@
             blocks = [(i * TOK, PROMPT, column < reaches[c] - i * PROMPT) for i in range(GROUP)]
             tile(at, blocks + [(at, T, causal)])
         for p in range(GROUP):
-            top = f_s[h, p * TOK : p * TOK + PAIR, :]
-            low = f_s[h, p * TOK + PAIR : (p + 1) * TOK, :]
-            o_s[h, p] = jnp.where(half, top, pltpu.roll(low, HEAD, 1)).astype(bf16)
+            for left, right, size, to in PACK:
+                top = f_s[h, p * TOK + left : p * TOK + left + size, :]
+                low = f_s[h, p * TOK + right : p * TOK + right + size, :]
+                pair = jnp.where(lanes(size) < HEAD, pltpu.roll(top, HEAD, 1), low)
+                o_s[h, p, to : to + size, :] = pair.astype(bf16)
         for i in range(1, GROUP):
             copy = remote(
                 o_s.at[h, pos ^ i], o_ref.at[pos, h], o_send.at[h, i], o_recv.at[h, i], me ^ i
@@ -811,8 +813,11 @@
             one = o_ref[2 * t // OWN, 2 * t % OWN].astype(f32)
             two = o_ref[(2 * t + 1) // OWN, (2 * t + 1) % OWN].astype(f32)
             at = slice(2 * t * HEAD, (2 * t + 2) * HEAD)
-            o_s[:PAIR, at] = jnp.where(half, one, pltpu.roll(two, HEAD, 1)).astype(bf16)
-            o_s[PAIR:, at] = jnp.where(half, pltpu.roll(one, HEAD, 1), two).astype(bf16)
+            first = jnp.where(half, one, pltpu.roll(two, HEAD, 1)).astype(bf16)
+            second = jnp.where(half, pltpu.roll(one, HEAD, 1), two).astype(bf16)
+            for left, right, size, to in PACK:
+                o_s[left : left + size, at] = first[to : to + size]
+                o_s[right : right + size, at] = second[to : to + size]
         h = x_ref[...].astype(f32) + dot(o_s[...], wo) + bo_ref[...]
         h_s[...] = h
         n, _ = moments(h)
@@ -856,11 +861,13 @@
         h_s[...] = dot_nt(dh_low, wo)
         for t in range(HEADS // 2):
             at = slice(2 * t * HEAD, (2 * t + 2) * HEAD)
-            top, low = h_s[:PAIR, at], h_s[PAIR:, at]
-            one = jnp.where(half, top, pltpu.roll(low, HEAD, 1))
-            two = jnp.where(half, pltpu.roll(top, HEAD, 1), low)
-            do_ref[2 * t // OWN, 2 * t % OWN] = one.astype(bf16)
-            do_ref[(2 * t + 1) // OWN, (2 * t + 1) % OWN] = two.astype(bf16)
+            for left, right, size, to in PACK:
+                top, low = h_s[left : left + size, at], h_s[right : right + size, at]
+                side = lanes(size) < HEAD
+                one = jnp.where(side, top, pltpu.roll(low, HEAD, 1))
+                two = jnp.where(side, pltpu.roll(top, HEAD, 1), low)
+                do_ref[2 * t // OWN, 2 * t % OWN, to : to + size] = one.astype(bf16)
+                do_ref[(2 * t + 1) // OWN, (2 * t + 1) % OWN, to : to + size] = two.astype(bf16)
 
 
 def middle(x, o, dy, wall, bo, gain, shift, bf, bp):
@@ -917,13 +924,13 @@
     do_ref, q_ref, k_ref, v_ref, f_ref, a_ref, w_ref, x_ref, dh_ref, lines_ref, sums_ref, dbf_ref,
     dwp_ref, dwo_ref, dwf_ref,
     grad_ref, gq_ref, gp_ref, go_ref, gf_ref, small_ref,
-    g_b, q_s, k_s, v_s, f_b, a_s, w_s, x_s, dh_s, lines_s, sums_s, dbf_s,
-    near_b, mine_b, ring_b, fin_b, fin_r, fin_o,
-    g_s, dq_s, kt_s, dk_s, dv_s, dm_s, w_h, acc_s, db_s,
+    g_b, q_s, k_s, v_s, f_b, a_b, w_s, x_s, dh_s, lines_s, sums_s, dbf_s,
+    near_b, mine_b, y_b, ring_b, fin_b, fin_r, fin_o,
+    g_s, dq_s, kt_s, dkv_s, dm_s, w_h, dw_s, db_s,
     dw_b, z_b, j_b, j_r, rep_b, rep_r, gq_o,
-    dn_a, dn_b, dn_c, dn_ra, dn_rb, dn_rc, dn_o, sm_b, sm_r,
-    load, mine_sem, g_send, g_recv, n_send, n_recv, r_send, r_recv, fin_send, fin_recv,
-    z_send, z_recv, j_send, j_recv, rep_send, rep_recv, d_send, d_recv, s_send, s_recv, out_sem,
+    dn_a, dn_b, dn_c, dn_ra, dn_rb, dn_rc, sm_b, sm_r,
+    load, f_sem, a_sem, mine_sem, g_send, g_recv, n_send, n_recv, y_send, y_recv, r_send, r_recv, fin_send,
+    fin_recv, z_send, z_recv, j_send, j_recv, rep_send, rep_recv, d_send, d_recv, s_send, s_recv, out_sem,
 ):
     n = BLOCKS
     me = lax.axis_index("fsdp")
@@ -949,32 +956,53 @@
 
     greet([me ^ i for i in range(1, n)], 1 - rep)
 
-    def do_copy(h, i):
-        return remote(do_ref.at[pos ^ i, h], g_b.at[pos, h], g_send.at[h, i], g_recv.at[h, i], me ^ i)
+    def do_copy(kind, i):
+        at = pl.ds(*((0, 128), (128, 256))[kind])
+        src, dst = do_ref.at[pos ^ i, :, at], g_b.at[pos, :, at]
+        return remote(src, dst, g_send.at[kind, i], g_recv.at[kind, i], me ^ i)
 
     own_do = pltpu.make_async_copy(do_ref.at[pos], g_b.at[pos], load.at[0])
     own_do.start()
-    for h in range(OWN):
-        for i in range(1, GROUP):
-            do_copy(h, i).start()
-
-    def f_copy(h):
-        return pltpu.make_async_copy(f_ref.at[h], f_b, load.at[1])
+    for i in range(1, GROUP):
+        do_copy(0, i).start()
+
+    stages = (
+        tuple((c * TOK + PROMPT, CONT) for c in range(GROUP)),
+        ((3 * TOK, PROMPT),),
+        ((0, PROMPT),),
+        ((TOK, PROMPT), (2 * TOK, PROMPT)),
+    )
+    loads = (stages[0], ((3 * TOK, PROMPT), (2 * TOK, PROMPT)), ((0, PROMPT), (TOK, PROMPT)))
+
+    def f_copies(part):
+        at, found = 0, []
+        for i, (row, size) in enumerate(loads[part]):
+            src, dst = f_ref.at[:, pl.ds(row, size)], f_b.at[:, pl.ds(at, size)]
+            found.append(pltpu.make_async_copy(src, dst, f_sem.at[part, i]))
+            at += size
+        return found
+
+    def a_copies(stage):
+        at, found = 0, []
+        for i, (row, size) in enumerate(stages[stage]):
+            src, dst = a_ref.at[pl.ds(row, size)], a_b.at[pl.ds(at, size)]
+            found.append(pltpu.make_async_copy(src, dst, a_sem.at[stage, i]))
+            at += size
+        return found
 
     first = [
-        pltpu.make_async_copy(src, dst, load.at[2 + i])
+        pltpu.make_async_copy(src, dst, load.at[1 + i])
         for i, (src, dst) in enumerate(
-            ((q_ref, q_s), (k_ref, k_s), (v_ref, v_s), (lines_ref, lines_s), (w_ref, w_s))
+            ((k_ref, k_s), (v_ref, v_s), (q_ref, q_s), (lines_ref, lines_s), (w_ref, w_s))
         )
     ]
     later = [
-        pltpu.make_async_copy(src, dst, load.at[7 + i])
+        pltpu.make_async_copy(src, dst, load.at[6 + i])
         for i, (src, dst) in enumerate(
-            ((a_ref, a_s), (x_ref, x_s), (dh_ref, dh_s), (sums_ref, sums_s), (dbf_ref, dbf_s))
+            ((x_ref, x_s), (dh_ref, dh_s), (sums_ref, sums_s), (dbf_ref, dbf_s))
         )
     ]
-    f_copy(0).start()
-    for copy in first:
+    for copy in f_copies(0) + first:
         copy.start()
 
     cut = ((0, 192), (192, 48), (240, 192))
@@ -993,13 +1021,15 @@
             for k, (ref, (at, size)) in enumerate(zip((dwp_ref, dwo_ref, dwf_ref), cut))
         ]
 
-    for i in range(8):
+    for i in range(2):
+        for copy in near_copies(i) + mine_copies(i):
+            copy.start()
+    for i in range(1, GROUP):
+        do_copy(1, i).start()
+    for i in range(2, 8):
         for copy in near_copies(i):
             copy.start()
-    for i in range(4):
-        for copy in mine_copies(i):
-            copy.start()
-    for copy in later:
+    for copy in a_copies(0) + mine_copies(2) + mine_copies(3) + later:
         copy.start()
 
     def ready(i):
@@ -1008,48 +1038,64 @@
         for copy in mine_copies(i):
             copy.wait()
 
+    mine = pl.ds(pl.multiple_of(rep * (D // 2), D // 2), D // 2)
+    rest = pl.ds(pl.multiple_of((1 - rep) * (D // 2), D // 2), D // 2)
+
+    def rounds(some):
+        def chunk(c, carry):
+            some(pl.ds(pl.multiple_of(c * 144, 144), 144))
+            return carry
+
+        lax.fori_loop(0, UNIT // 144, chunk, 0)
+
+    def y_copy(i):
+        return remote(near_b.at[i, :, rest], y_b.at[i], y_send.at[i], y_recv.at[i], other)
+
+    def chip_sum(i):
+        ready(i)
+
+        def some(at):
+            total = near_b[i, at, :].astype(f32) + mine_b[i % 4, at, :].astype(f32)
+            near_b[i, at, :] = total.astype(bf16)
+
+        rounds(some)
+        y_copy(i).start()
+        if i + 4 < 8:
+            for copy in mine_copies(i + 4):
+                copy.start()
+
     def ring_copy(t, right):
         i = 2 * t if right else 2 * t + 1
         slot = t if right else 4 + t
         peer = device(place + 1 if right else place - 1)
-        return remote(near_b.at[i], ring_b.at[slot], r_send.at[slot], r_recv.at[slot], peer)
-
-    def rounds(some):
-        def chunk(c, carry):
-            some(pl.ds(pl.multiple_of(c * 144, 144), 144))
-            return carry
-
-        lax.fori_loop(0, UNIT // 144, chunk, 0)
+        return remote(near_b.at[i, :, mine], ring_b.at[slot], r_send.at[slot], r_recv.at[slot], peer)
 
     def ring_step(t):
         for right in (True, False) if t < 3 else (True,):
             i = 2 * t if right else 2 * t + 1
-            ready(i)
+            y_copy(i).wait_recv()
             if t > 0:
                 ring_copy(t - 1, right).wait_recv()
             slot = (t if right else 4 + t) - 1
 
             def some(at):
-                total = near_b[i, at, :].astype(f32) + mine_b[i % 4, at, :].astype(f32)
+                total = near_b[i, at, mine].astype(f32) + y_b[i, at, :].astype(f32)
                 if t > 0:
                     total = total + ring_b[slot, at, :].astype(f32)
-                near_b[i, at, :] = total.astype(bf16)
+                near_b[i, at, mine] = total.astype(bf16)
 
             rounds(some)
             ring_copy(t, right).start()
-            if i + 4 < 8:
-                for copy in mine_copies(i + 4):
-                    copy.start()
 
     fin_copy = remote(fin_b, fin_r, fin_send, fin_recv, other)
 
     def ring_end():
-        ready(7)
+        y_copy(7).wait_recv()
         ring_copy(3, True).wait_recv()
         ring_copy(2, False).wait_recv()
 
         def some(at):
-            total = near_b[7, at, :].astype(f32) + mine_b[3, at, :].astype(f32)
+            total = near_b[7, at, mine].astype(f32) + y_b[7, at, :].astype(f32)
             fin_b[at, :] = (total + ring_b[3, at, :].astype(f32) + ring_b[6, at, :].astype(f32)).astype(bf16)
 
         rounds(some)
@@ -1069,206 +1115,260 @@
         total = dw_b[h, level].astype(f32)
         for i in range(1, GROUP):
             total = total + z_b[h, i].astype(f32)
-        total = total.astype(bf16).reshape(GROUP, D // n, W3)
-        j_b[h] = total
+        j_b[h] = total.astype(bf16).reshape(GROUP, D // n, W3)
         j_r[pos, h] = j_b[h, pos]
         for i in range(1, GROUP):
             j_copy(h, i).start()
 
-    half = lanes(PAIR) < HEAD
-    lane = lanes(PAIR)
     causal = below(T, T, True)
     key_row = lax.broadcasted_iota(jnp.int32, (PROMPT, T), 0).astype(f32)
-    narrow = lanes(T) < HEAD
+
+    def prepare(part, h):
+        at = 0
+        for row, size in loads[part]:
+            p = row // TOK
+            left, right, count, to = PACK[0 if size == CONT else 1]
+            packed = g_b[p, h, to : to + count, :].astype(f32)
+            lane = lanes(count)
+            for start, block in ((left, pltpu.roll(packed, HEAD, 1)), (right, packed)):
+                off = at + start - (row - p * TOK)
+                prod = jnp.where(lane >= HEAD, block * f_b[h, off : off + count, :], 0.0)
+                inner = jnp.sum(prod, axis=1, keepdims=True)
+                hi = inner.astype(bf16).astype(f32)
+                mid = (inner - hi).astype(bf16).astype(f32)
+                low = inner - hi - mid
+                tail = jnp.where(lane == 0, -hi, jnp.where(lane == 1, -mid, -low))
+                value = jnp.where(lane >= HEAD, block, jnp.where(lane < 3, tail, 0.0))
+                g_s[h, p * TOK + start : p * TOK + start + count, :] = value.astype(bf16)
+            at += size
+
+    def block(h, keys, size, rows, count, mask, target):
+        kb = k_s[h, pl.ds(keys, size), :]
+        vb = v_s[h, pl.ds(keys, size), :]
+        q = q_s[h, pl.ds(rows, count), :]
+        g = g_s[h, pl.ds(rows, count), :]
+        probs = jnp.exp(dot_nt(kb, q))
+        if mask is not None:
+            probs = jnp.where(mask, probs, 0.0)
+        ds = (probs * dot_nt(vb, g)).astype(bf16)
+        lane = lanes(count)
+        none = jnp.zeros_like(q)
+        pair = dot(ds, jnp.where(lane < HEAD, q, none))
+        pair = pair + dot(probs.astype(bf16), jnp.where(lane < HEAD, none, g))
+        dq_s[h, :, pl.ds(rows, count)] += dot(kt_s[h, :, pl.ds(keys, size)], ds)
+        if target is None:
+            return pair
+        dkv_s[h, pl.ds(target, size), :] += pair
+
+    def diagonal(h, p):
+        row, at = p * TOK, p * PROMPT
+        block(h, row, T, row, T, causal, at)
+        block(h, row, T, row + T, T, None, at)
+        block(h, row + T, T, row + T, T, causal, at + T)
+
+    def flush_q(h, row, size):
+        at = pl.ds(row, size)
+        dm_s[h, at, 2 * HEAD :] = (dq_s[h, :, at].T * 0.125).astype(bf16)
+
+    def flush(h, p):
+        dm_s[h, p * TOK : p * TOK + PROMPT, : 2 * HEAD] = dkv_s[
+            h, p * PROMPT : (p + 1) * PROMPT, :
+        ].astype(bf16)
+        flush_q(h, p * TOK, PROMPT)
+
+    def add_weight(stage, h):
+        at = 0
+        total = jnp.zeros((W3, D), f32)
+        for row, size in stages[stage]:
+            total = total + dot_tn(dm_s[h, row : row + size, :], a_b[at : at + size, :])
+            at += size
+        if stage == 0:
+            dw_s[h] = total
+        else:
+            dw_s[h] += total
+
+    def dn_rows(owner, seg):
+        rows = pl.ds(pl.multiple_of(owner * TOK + seg * T, T), T)
+        total = dot_nt(dm_s[0, rows, :], w_h[0])
+        for h in range(1, OWN):
+            total = total + dot_nt(dm_s[h, rows, :], w_h[h])
+        return total
+
+    def dn_copy(kind, seg):
+        at = pl.ds(seg * T, T)
+        src, dst, peer = ((dn_a, dn_ra, near), (dn_b, dn_rb, far), (dn_c, dn_rc, near))[kind]
+        return remote(src.at[at], dst.at[at], d_send.at[kind, seg], d_recv.at[kind, seg], peer)
+
+    def put(kind, seg):
+        at = slice(seg * T, (seg + 1) * T)
+        rows = dn_rows(pos ^ (3, 2, 1)[kind], seg)
+        if kind == 1:
+            dn_copy(0, seg).wait_recv()
+            rows = rows + dn_ra[at, :].astype(f32)
+        (dn_a, dn_b, dn_c)[kind][at, :] = rows.astype(bf16)
+        dn_copy(kind, seg).start()
+
+    def put_prompt(p, kinds):
+        for kind in kinds:
+
+            @pl.when((pos ^ (3, 2, 1)[kind]) == p)
+            def _():
+                for seg in range(2):
+                    put(kind, seg)
 
     first[3].wait()
     first[4].wait()
     for h in range(OWN):
         w_h[h] = jnp.concatenate(
-            [
-                w_s[:, part * SLICE + h * HEAD : part * SLICE + (h + 1) * HEAD]
-                for part in (1, 2, 0)
-            ],
+            [w_s[:, part * SLICE + h * HEAD : part * SLICE + (h + 1) * HEAD] for part in (1, 2, 0)],
             axis=1,
         )
+    dq_s[...] = jnp.zeros_like(dq_s)
+    dkv_s[...] = jnp.zeros_like(dkv_s)
     for copy in first[:3]:
         copy.wait()
+
+    def turn(h, carry):
+        for p in range(GROUP):
+            kt_s[h, :, p * TOK : (p + 1) * TOK] = k_s[h, p * TOK : (p + 1) * TOK, :].T[:HEAD]
+        return carry
+
+    lax.fori_loop(0, OWN, turn, 0)
     own_do.wait()
-
-    def one_head(h, carry):
+    for i in range(1, GROUP):
+        do_copy(0, i).wait_recv()
+    for copy in f_copies(0):
+        copy.wait()
+    chip_sum(0)
+    chip_sum(1)
+
+    def stage_cont(h, carry):
+        prepare(0, h)
+
+        def cont(c, carry):
+            rows = pl.multiple_of(c * TOK + PROMPT, CONT)
+            code = lines_s[base + c, 1:2, 0:128].astype(f32)
+            reach = code[:, 0:1] * 16.0 + code[:, 1:2]
+            for p in range(GROUP):
+                block(h, p * TOK, PROMPT, rows, T, key_row < reach - p * PROMPT, p * PROMPT)
+            pair = block(h, rows, T, rows, T, causal, None)
+            dm_s[h, pl.ds(rows, T), : 2 * HEAD] = pair.astype(bf16)
+            flush_q(h, rows, T)
+            return carry
+
+        lax.fori_loop(0, GROUP, cont, 0)
+
+        for k in range(OWN):
+
+            @pl.when(h == k)
+            def _():
+                chip_sum(2 + 2 * k)
+                chip_sum(3 + 2 * k)
+
+        return carry
+
+    lax.fori_loop(0, OWN, stage_cont, 0)
+    ring_step(0)
+    for copy in f_copies(1):
+        copy.start()
+    for copy in a_copies(0):
+        copy.wait()
+    for kind in (0, 2, 1):
+        put(kind, 2)
+    lax.fori_loop(0, OWN, lambda h, carry: (add_weight(0, h), carry)[1], 0)
+    for copy in a_copies(1):
+        copy.start()
+    for i in range(1, GROUP):
+        do_copy(1, i).wait_recv()
+    for copy in f_copies(1):
+        copy.wait()
+
+    def stage_last(h, carry):
+        prepare(1, h)
+        for p in range(3):
+            block(h, p * TOK, PROMPT, 3 * TOK, PROMPT, None, p * PROMPT)
+        diagonal(h, 3)
+        flush(h, 3)
+
+        return carry
+
+    lax.fori_loop(0, OWN, stage_last, 0)
+    ring_step(1)
+    for copy in f_copies(2):
+        copy.start()
+    for copy in a_copies(1):
+        copy.wait()
+    put_prompt(3, (0, 2))
+    lax.fori_loop(0, OWN, lambda h, carry: (add_weight(1, h), carry)[1], 0)
+    for copy in a_copies(2):
+        copy.start()
+    put_prompt(3, (1,))
+    for copy in f_copies(2):
+        copy.wait()
+
+    def stage_first(h, carry):
+        prepare(2, h)
+        diagonal(h, 0)
+        for p in range(1, 3):
+            block(h, 0, PROMPT, p * TOK, PROMPT, None, 0)
+        flush(h, 0)
+
+        return carry
+
+    lax.fori_loop(0, OWN, stage_first, 0)
+    for copy in a_copies(2):
+        copy.wait()
+    put_prompt(0, (0, 2))
+    lax.fori_loop(0, OWN, lambda h, carry: (add_weight(2, h), carry)[1], 0)
+    for copy in a_copies(3):
+        copy.start()
+    put_prompt(0, (1,))
+    for copy in a_copies(3):
+        copy.wait()
+
+    def stage_middle(h, carry):
+        block(h, TOK, PROMPT, 2 * TOK, PROMPT, None, PROMPT)
+        diagonal(h, 1)
+        flush(h, 1)
+        diagonal(h, 2)
+        flush(h, 2)
+        add_weight(3, h)
+        dw = dw_s[h].T
+        dw_b[h] = dw.astype(bf16).reshape(GROUP, D // GROUP, W3)
         for i in range(1, GROUP):
-            do_copy(h, i).wait_recv()
-        f_copy(h).wait()
-        for p in range(GROUP):
-            packed = g_b[p, h].astype(f32)
-            for i, block in enumerate((packed, pltpu.roll(packed, HEAD, 1))):
-                at = p * TOK + i * PAIR
-                prod = jnp.where(half, block * f_b[at : at + PAIR, :], 0.0)
-                inner = jnp.sum(prod, axis=1, keepdims=True)
-                g_s[at : at + PAIR, :] = split_columns(block, lane, inner)
-            kt_s[:, p * TOK : (p + 1) * TOK] = k_s[h, p * TOK : (p + 1) * TOK, :].T[:HEAD]
-
-        @pl.when(h + 1 < OWN)
+            z_copy(h, i).start()
+        db = jnp.zeros((1, W3), f32)
+        for i in range(GROUP):
+            db = db + jnp.sum(dm_s[h, i * TOK : (i + 1) * TOK, :].astype(f32), axis=0, keepdims=True)
+        hi = db.astype(bf16)
+        mid = (db - hi.astype(f32)).astype(bf16)
+        low = (db - hi.astype(f32) - mid.astype(f32)).astype(bf16)
+        split = jnp.concatenate([hi, mid, low, jnp.zeros((13, W3), bf16)], axis=0)
+        ones = jnp.ones((8, W3), f32)
+        gain_rows = lax.dot_general(
+            ones,
+            w_h[h].astype(f32) * dw,
+            (((1,), (1,)), ((), ())),
+            precision=lax.Precision.HIGHEST,
+            preferred_element_type=f32,
+        )
+        db_s[h, 0:1, :W3] = db
+        db_s[h, 1:2, W3 : W3 + D] = jnp.sum(dot_nt(split, w_h[h]), axis=0, keepdims=True)
+        db_s[h, 2:3, W3 : W3 + D] = gain_rows[0:1]
+        return carry
+
+    lax.fori_loop(0, OWN, stage_middle, 0)
+    for kind, owners in ((2, (0, 3)), (0, (1, 2)), (1, (0, 3))):
+        inner = lax.rem(pos + 1, GROUP) // 2
+
+        @pl.when(inner == (0 if owners == (0, 3) else 1))
         def _():
-            f_copy(h + 1).start()
-
-        @pl.when(h == 0)
-        def _():
-            ring_step(0)
-
-        dq_s[...] = jnp.zeros_like(dq_s)
-
-        def block(keys, size, rows, count, mask, first, key_at):
-            kb = k_s[h, pl.ds(keys, size), :]
-            vb = v_s[h, pl.ds(keys, size), :]
-            q = q_s[h, pl.ds(rows, count), :]
-            g = g_s[pl.ds(rows, count), :]
-            probs = jnp.exp(dot_nt(kb, q))
-            if mask is not None:
-                probs = jnp.where(mask, probs, 0.0)
-            ds = (probs * dot_nt(vb, g)).astype(bf16)
-            dv = dot(probs.astype(bf16), g)
-            dk = dot(ds, q)
-            at = pl.ds(key_at, size)
-            dv_s[at, :] = dv if first else dv_s[at, :] + dv
-            dk_s[at, :] = dk if first else dk_s[at, :] + dk
-            dq_s[:, pl.ds(rows, count)] += dot(kt_s[:, pl.ds(keys, size)], ds)
-
-        def flush(at, size):
-            for i in range(size // T):
-                part = slice(i * T, (i + 1) * T)
-                pair = jnp.where(narrow, dk_s[part, :], pltpu.roll(dv_s[part, :], HEAD, 1))
-                dm_s[h, pl.ds(at + i * T, T), : 2 * HEAD] = pair.astype(bf16)
-
-        for p in range(GROUP):
-            base_row = p * TOK
-            block(base_row, T, base_row, T, causal, True, 0)
-            block(base_row + T, T, base_row + T, T, causal, True, T)
-            block(base_row, T, base_row + T, T, None, False, 0)
-
-            def past(i, carry):
-                rows = pl.multiple_of(i * TOK, CONT)
-                block(base_row, PROMPT, rows, PROMPT, None, False, 0)
-                return carry
-
-            lax.fori_loop(p + 1, GROUP, past, 0)
-
-            def cont(c, carry):
-                rows = pl.multiple_of(c * TOK + PROMPT, CONT)
-                code = lines_s[base + c, 1:2, 0:128].astype(f32)
-                reach = code[:, 0:1] * 16.0 + code[:, 1:2] - p * PROMPT
-                block(base_row, PROMPT, rows, T, key_row < reach, False, 0)
-                return carry
-
-            lax.fori_loop(0, GROUP, cont, 0)
-            flush(base_row, PROMPT)
-            if p == 1:
-
-                @pl.when(h > 0)
-                def _():
-                    gather_rows(h - 1)
-
-        def own(c, carry):
-            at = pl.multiple_of(c * TOK + PROMPT, CONT)
-            block(at, T, at, T, causal, True, 0)
-            flush(at, T)
-            return carry
-
-        lax.fori_loop(0, GROUP, own, 0)
-        for i in range(ROWS // PROMPT):
-            at = i * PROMPT
-            dm_s[h, at : at + PROMPT, 2 * HEAD :] = (dq_s[:, at : at + PROMPT].T * 0.125).astype(bf16)
-
-        @pl.when(h == 0)
-        def _():
-            later[0].wait()
-
-        def weight():
-            dw_t = jnp.zeros((W3, D), f32)
-            for i in range(GROUP):
-                rows = slice(i * TOK, (i + 1) * TOK)
-                dw_t = dw_t + dot_tn(dm_s[h, rows, :], a_s[rows, :])
-            acc_s[...] = dw_t
-            dw = acc_s[...].T
-            dw_b[h] = dw.astype(bf16).reshape(GROUP, D // GROUP, W3)
-            for i in range(1, GROUP):
-                z_copy(h, i).start()
-            db = jnp.zeros((1, W3), f32)
-            for i in range(GROUP):
-                db = db + jnp.sum(dm_s[h, i * TOK : (i + 1) * TOK, :].astype(f32), axis=0, keepdims=True)
-            hi = db.astype(bf16)
-            mid = (db - hi.astype(f32)).astype(bf16)
-            low = (db - hi.astype(f32) - mid.astype(f32)).astype(bf16)
-            split = jnp.concatenate([hi, mid, low, jnp.zeros((13, W3), bf16)], axis=0)
-            shift_rows = dot_nt(split, w_h[h])
-            shift_part = jnp.sum(shift_rows, axis=0, keepdims=True)
-            ones = jnp.ones((8, W3), f32)
-            gain_rows = lax.dot_general(
-                ones,
-                w_h[h].astype(f32) * dw,
-                (((1,), (1,)), ((), ())),
-                precision=lax.Precision.HIGHEST,
-                preferred_element_type=f32,
-            )
-            db_s[h, 0:1, :W3] = db
-            db_s[h, 1:2, W3 : W3 + D] = shift_part
-            db_s[h, 2:3, W3 : W3 + D] = gain_rows[0:1]
-
-        @pl.when(h < OWN - 1)
-        def _():
-            weight()
-            ring_step_at(h)
-
-        @pl.when(h == OWN - 1)
-        def _():
-            ring_step(3)
-            send_rows()
-            weight()
-
-        return carry
-
-    def ring_step_at(h):
-        @pl.when(h == 0)
-        def _():
-            ring_step(1)
-
-        @pl.when(h == 1)
-        def _():
-            ring_step(2)
-
-    def dn_rows(block, part):
-        rows = pl.ds(pl.multiple_of((pos ^ block) * TOK + part * PAIR, PAIR), PAIR)
-        total = dot_nt(dm_s[0, rows, :], w_h[0])
-        for h in range(1, OWN):
-            total = total + dot_nt(dm_s[h, rows, :], w_h[h])
-        return total
-
-    def dn_copy(kind, part):
-        at = pl.ds(part * PAIR, PAIR)
-        src, dst, peer = ((dn_a, dn_ra, near), (dn_b, dn_rb, far), (dn_c, dn_rc, near))[kind]
-        i = 2 * kind + part
-        return remote(src.at[at], dst.at[at], d_send.at[i], d_recv.at[i], peer)
-
-    def send_rows():
-        for part in range(2):
-            dn_a[part * PAIR : (part + 1) * PAIR, :] = dn_rows(3, part).astype(bf16)
-            dn_copy(0, part).start()
-        for part in range(2):
-            at = slice(part * PAIR, (part + 1) * PAIR)
-            rows = dn_rows(2, part)
-            dn_copy(0, part).wait_recv()
-            dn_b[at, :] = (rows + dn_ra[at, :].astype(f32)).astype(bf16)
-            dn_copy(1, part).start()
-        for part in range(2):
-            dn_c[part * PAIR : (part + 1) * PAIR, :] = dn_rows(1, part).astype(bf16)
-            dn_copy(2, part).start()
-
-    lax.fori_loop(0, OWN, one_head, 0)
-
-    for copy in later[1:]:
+            for seg in range(2):
+                put(kind, seg)
+
+    ring_step(2)
+    for copy in later:
         copy.wait()
-    for part in range(2):
-        dn_o[part * PAIR : (part + 1) * PAIR, :] = dn_rows(0, part)
 
     rows48 = D // n
     gain = jnp.concatenate([lines_s[d, 0:1, 0:rows48] for d in range(n)], axis=1).astype(f32)
@@ -1308,9 +1408,12 @@
             small_copy(i + 1).start()
 
     small_copy(0).start()
+    gather_rows(0)
     small_step(0)
-    gather_rows(OWN - 1)
+    gather_rows(1)
     small_step(1)
+    ring_step(3)
+    gather_rows(2)
     small_step(2)
     for h in range(OWN):
         for i in range(1, GROUP):
@@ -1318,19 +1421,20 @@
     rep_b[...] = j_r[...]
     rep_copy = remote(rep_b, rep_r, rep_send, rep_recv, other)
     rep_copy.start()
+    small_step(3)
     ring_end()
-    small_step(3)
 
     outs = []
-    for part in range(2):
-        at = slice(part * PAIR, (part + 1) * PAIR)
-        dn_copy(2, part).wait_recv()
-        dn_copy(1, part).wait_recv()
+    for seg in (2, 0, 1):
+        at = slice(seg * T, (seg + 1) * T)
+        rows = dn_rows(pos, seg)
+        dn_copy(2, seg).wait_recv()
+        dn_copy(1, seg).wait_recv()
         n_rows, r = moments(x_s[at, :].astype(f32))
-        e = (dn_o[at, :] + dn_rb[at, :].astype(f32) + dn_rc[at, :].astype(f32)) * gain
+        e = (rows + dn_rb[at, :].astype(f32) + dn_rc[at, :].astype(f32)) * gain
         lean = jnp.mean(e, axis=-1, keepdims=True) + n_rows * jnp.mean(e * n_rows, axis=-1, keepdims=True)
         dh_s[at, :] = dh_s[at, :] + r * (e - lean)
-        copy = pltpu.make_async_copy(dh_s.at[at], grad_ref.at[at], out_sem.at[part])
+        copy = pltpu.make_async_copy(dh_s.at[at], grad_ref.at[at], out_sem.at[10 + seg])
         copy.start()
         outs.append(copy)
 
@@ -1368,7 +1472,8 @@
     fin_copy.wait_recv()
 
     def some(at):
-        fin_o[at, :] = fin_b[at, :].astype(f32) + fin_r[at, :].astype(f32)
+        fin_o[at, mine] = fin_b[at, :].astype(f32)
+        fin_o[at, rest] = fin_r[at, :].astype(f32)
 
     rounds(some)
     targets = [(gp_ref, 0, 192), (go_ref, 192, 48)]
@@ -1380,17 +1485,21 @@
 
     for h in range(OWN):
         for i in range(1, GROUP):
-            for copy in (do_copy(h, i), z_copy(h, i), j_copy(h, i)):
+            for copy in (z_copy(h, i), j_copy(h, i)):
                 copy.wait_send()
+    for kind in range(2):
+        for i in range(1, GROUP):
+            do_copy(kind, i).wait_send()
     for i in range(8):
+        y_copy(i).wait_send()
         for copy in near_copies(i):
             copy.wait_send()
     for t in range(4):
         for right in (True, False) if t < 3 else (True,):
             ring_copy(t, right).wait_send()
     for kind in range(3):
-        for part in range(2):
-            dn_copy(kind, part).wait_send()
+        for seg in range(3):
+            dn_copy(kind, seg).wait_send()
     for i in range(1, 5):
         small_copy(i).wait_send()
     rep_copy.wait_send()
@@ -1426,8 +1535,8 @@
             vmem(head, bf16),
             vmem(head, bf16),
             vmem(head, bf16),
-            vmem(head[1:], f32),
-            vmem((ROWS, D), bf16),
+            vmem((OWN, GROUP * CONT, 2 * HEAD), f32),
+            vmem((GROUP * CONT, D), bf16),
             vmem((D, WIDE), bf16),
             vmem((TOK, D), bf16),
             vmem((TOK, D), f32),
@@ -1436,18 +1545,18 @@
             vmem(dbf.shape, f32),
             vmem((8, UNIT, D), bf16),
             vmem((4, UNIT, D), bf16),
-            vmem((7, UNIT, D), bf16),
-            vmem((UNIT, D), bf16),
-            vmem((UNIT, D), bf16),
+            vmem((8, UNIT, D // 2), bf16),
+            vmem((7, UNIT, D // 2), bf16),
+            vmem((UNIT, D // 2), bf16),
+            vmem((UNIT, D // 2), bf16),
             vmem((UNIT, D), f32),
-            vmem((ROWS, 2 * HEAD), bf16),
-            vmem((HEAD, ROWS), f32),
-            vmem((HEAD, ROWS), bf16),
-            vmem((PROMPT, 2 * HEAD), f32),
-            vmem((PROMPT, 2 * HEAD), f32),
+            vmem(head, bf16),
+            vmem((OWN, HEAD, ROWS), f32),
+            vmem((OWN, HEAD, ROWS), bf16),
+            vmem((OWN, GROUP * PROMPT, 2 * HEAD), f32),
             vmem((OWN, ROWS, W3), bf16),
             vmem((OWN, D, W3), bf16),
-            vmem((W3, D), f32),
+            vmem((OWN, W3, D), f32),
             vmem((OWN, 8, W3 + D), f32),
             vmem((OWN, GROUP, D // GROUP, W3), bf16),
             vmem((OWN, GROUP, D // GROUP, W3), bf16),
@@ -1462,15 +1571,18 @@
             vmem((TOK, D), bf16),
             vmem((TOK, D), bf16),
             vmem((TOK, D), bf16),
-            vmem((TOK, D), f32),
             vmem((6, SMALL, D), f32),
             vmem((5, SMALL, D), f32),
-            dma((12,)),
+            dma((10,)),
+            dma((3, GROUP)),
+            dma((4, GROUP)),
             dma((8, 3)),
-            dma(pairs),
-            dma(pairs),
+            dma((2, GROUP)),
+            dma((2, GROUP)),
             dma((8, 3)),
             dma((8, 3)),
+            dma((8,)),
+            dma((8,)),
             dma((7,)),
             dma((7,)),
             dma,
@@ -1481,11 +1593,11 @@
             dma(pairs),
             dma,
             dma,
-            dma((6,)),
-            dma((6,)),
+            dma((3, 3)),
+            dma((3, 3)),
             dma((5,)),
             dma((5,)),
-            dma((10,)),
+            dma((13,)),
         ],
         compiler_params=params(63, collective_id=4, has_side_effects=True),
     )(do, q, k, v, f, a, w, x, dh, lines, sums, dbf, dwp, dwo, dwf)
@@ -1560,6 +1672,19 @@
 def flip(block, bit):
     count = lax.axis_size("fsdp")
     return lax.ppermute(block, "fsdp", [(i, i ^ bit) for i in range(count)])
+
+
+def repack(packed, old, new):
+    rows = []
+    for left, right, size, at in old:
+        rows.append((left, packed[:, :, at : at + size, :HEAD]))
+        rows.append((right, packed[:, :, at : at + size, HEAD:]))
+    rows = jnp.concatenate([part for _, part in sorted(rows, key=lambda entry: entry[0])], axis=2)
+    parts = [
+        jnp.concatenate([rows[:, :, left : left + size], rows[:, :, right : right + size]], axis=3)
+        for left, right, size, _ in sorted(new, key=lambda entry: entry[3])
+    ]
+    return jnp.concatenate(parts, axis=2)
 
 
 def over_replicas(block):
@@ -1626,7 +1751,7 @@
         bias = jnp.concatenate([own_bias[0], jnp.zeros((SLICE,), f32), own_bias[1]])[None]
         a_low, q, k, v = project(xg.reshape(ROWS, D), wq, g1, s1, bias)
         o_send, o_full, qx = attend(reaches, q, k, v)
-        o_recv = swap(o_send, 1, "swap_o")
+        o_recv = repack(swap(o_send, 1, "swap_o"), ((0, 384, 384, 0),), PACK)
 
     y, dwf, dwp, dbf, dwo, dh, do_send, sums = middle(
         block_input, o_recv, cotangent, wall, bo, g2, s2, bf, bp
@@ -1644,7 +1769,7 @@
     dwf = lax.psum_scatter(dwf, "fsdp", scatter_dimension=0, tiled=True)
     dwp = lax.psum_scatter(dwp, "fsdp", scatter_dimension=0, tiled=True)
     dwo = lax.psum_scatter(dwo, "fsdp", scatter_dimension=0, tiled=True)
-    do_recv = swap(do_send, 2, "swap_do")
+    do_recv = repack(swap(do_send, 2, "swap_do"), PACK, ((0, 384, 384, 0),))
     dq, dk, dv = attend_back(reaches, qx, k, v, o_full, do_recv)
     dn, dwq, db = unproject(dq, dk, dv, a_low, wq)
 

time: 306 us -> 284 us (0.928)
  Pallas kernels: 285 us -> 263 us
    pallas_call x1, Pallas kernels: 144 us -> 122 us  [backward(): pl.pallas_call(backward_kernel, name='backward', out_shape=(shape((TOK, D...]
where the time goes in v4:
time: 284 us; the launch traced here: 279 us
  Pallas kernels  263 us (93%)
  local copies, waits for them, and re-layouts  13.8 us (5%)
    pallas_call x1, Pallas kernels, backward(): pl.pallas_call(backward_kernel, name='backward', out_shape=(shape((TOK, D...  122 us
    pallas_call x1, Pallas kernels, forward(): pl.pallas_call(forward_kernel, name='forward', out_shape=(shape((n, UNIT,...  98.7 us
    pallas_call x1, Pallas kernels, middle(): pl.pallas_call(middle_kernel, name='middle', grid=(FF // CHUNK,), out_sha...  39.4 us
    unnamed x14, local copies, waits for them, and re-layouts  6.39 us

profile of v4, /device:TPU:0, one launch (start us, length us, event | category | flops | bytes accessed | tf_op | source)
XLA Modules:
  0.0 279.4 jit_solution(17955668771979500669)
XLA Ops:
  1.9 2.4 pick.1
  4.3 98.7 %forward.1 = (bf16[16,432,768]{2,1,0:T(8,128)(2,1)}, bf16[16,2,640]{2,1,0:T(2,128)(2,1)}, bf16[768,576]{1,0:T(8,128)(2,1)}, bf16[4,768,768]{2,1,0:T(8,128)(2,1)}...) custom-call(bf16[768,768]{1,0:T(8,128)(2,1)} %x_ref.5, ...), custom_call_target="tpu_custom_call" | custom-call | tf_op jit(solution)/shard_map/forward/pallas_call | solution.py:752
  103.0 0.8 slice_convert_fusion
  103.8 0.1 slice.59
  103.9 0.1 fusion
  104.0 0.7 reshape.60.bf_ref
  104.7 0.7 reshape.61.bp_ref
  105.3 0.7 reshape.59.s_ref
  106.0 0.7 reshape.58.g_ref
  106.7 0.7 reshape.57.bo_ref
  107.4 39.4 %middle.1 = (bf16[768,768]{1,0:T(8,128)(2,1)}, bf16[16,4,48,768]{3,2,1,0:T(8,128)(2,1)}, bf16[3072,768]{1,0:T(8,128)(2,1)}, f32[1,3072]{1,0:T(1,128)}, bf16[768,...) custom-call(bf16[768,768]{1,0:T(8,128)(2,1)} %x_ref.5, ...), custom_call_target="tpu_custom_call" | custom-call | tf_op jit(solution)/shard_map/middle/pallas_call | solution.py:883
  146.7 122.2 %backward.1 = (f32[768,768]{1,0:T(8,128)}, f32[48,2304]{1,0:T(8,128)}, f32[192,768]{1,0:T(8,128)}, f32[48,768]{1,0:T(8,128)}, f32[48,3072]{1,0:T(8,128)}, /*index=5*/f32[16,768]{1,0:T(8,128)}) custom-call(bf16[4,3,384,128]{3,2,1,0:T(8,128)(2,1)} %get-tuple-element.47.do_ref, bf16[3,3072,128]{2,1,0:T(8,128)(2,1)} %get-tuple-element.48.q_ref, ...), custom_call_target="tpu_custom_call" | custom-call | tf_op jit(solution)/shard_map/backward/pallas_call | solution.py:1520
  268.9 1.2 slice_bitcast_fusion.4
  270.1 1.3 slice.54
  271.4 1.4 slice_bitcast_fusion
  272.8 0.0 copy-start.2
  272.8 0.0 copy-start.3
  272.8 0.0 copy-start.1
  272.8 3.3 %copy.40 = f32[768,768]{1,0:T(8,128)} copy(f32[768,768]{1,0:T(8,128)} %get-tuple-element.91) | data formatting | bytes 4718592
  276.1 0.0 copy-done.2
  276.1 0.0 copy-start
  276.1 0.8 copy.41
  276.9 0.0 copy-done.3
  276.9 0.7 copy.42
  277.6 0.0 copy-done.1
  277.6 0.8 copy.43
  278.4 0.0 copy-done
  278.4 0.8 copy.44
  (1 shorter events, 0.0 us)
Async XLA Ops:
  272.8 3.3 %copy-start.2 = (f32[48,2304]{1,0:T(8,128)S(1)}, f32[48,2304]{1,0:T(8,128)}, u32[]{:S(2)}) copy-start(f32[48,2304]{1,0:T(8,128)} %get-tuple-element.94) | copy-start | bytes 1327108
  272.8 4.1 %copy-start.3 = (f32[48,768]{1,0:T(8,128)S(1)}, f32[48,768]{1,0:T(8,128)}, u32[]{:S(2)}) copy-start(f32[48,768]{1,0:T(8,128)} %get-tuple-element.96) | copy-start | bytes 442372
  272.8 4.8 %copy-start.1 = (f32[48,3072]{1,0:T(8,128)S(1)}, f32[48,3072]{1,0:T(8,128)}, u32[]{:S(2)}) copy-start(f32[48,3072]{1,0:T(8,128)} %get-tuple-element.100) | copy-start | bytes 1769476
  276.1 2.2 copy-start

commit v5 on v4

--- a/solution.py
+++ b/solution.py
@@ -797,11 +797,12 @@
 
 
 def middle_kernel(
-    x_ref, o_ref, dy_ref, wo_ref, wf_ref, wp_ref, bo_ref, g_ref, s_ref, bf_ref, bp_ref,
+    x_ref, o_ref, dy_ref, wo_ref, wf_ref, wp_ref, line_ref,
     y_ref, dwf_ref, dwp_ref, dbf_ref, dwo_ref, dh_ref, do_ref, small_ref,
-    o_s, h_s, b_s, bt_s, y_s, dn_s,
+    o_s, h_s, b_s, bt_s, y_s, dn_s, row_s,
 ):
     step = pl.program_id(0)
+    part = D // BLOCKS
     half = lanes(PAIR) < HEAD
     wf = wf_ref[...].reshape(D, CHUNK)
     wp = wp_ref[...].reshape(CHUNK, D)
@@ -818,17 +819,21 @@
             for left, right, size, to in PACK:
                 o_s[left : left + size, at] = first[to : to + size]
                 o_s[right : right + size, at] = second[to : to + size]
-        h = x_ref[...].astype(f32) + dot(o_s[...], wo) + bo_ref[...]
+        for i, at in enumerate((4 * part, 5 * part, 6 * part, 11 * part)):
+            pieces = [line_ref[d, 0:1, at : at + part] for d in range(BLOCKS)]
+            row_s[i : i + 1, :] = jnp.concatenate(pieces, axis=1).astype(f32)
+        h = x_ref[...].astype(f32) + dot(o_s[...], wo) + row_s[0:1, :]
         h_s[...] = h
         n, _ = moments(h)
-        b_low = (n * g_ref[...] + s_ref[...]).astype(bf16)
+        b_low = (n * row_s[1:2, :] + row_s[2:3, :]).astype(bf16)
         b_s[...] = b_low
         bt_s[...] = b_low.T
         y_s[...] = jnp.zeros_like(y_s)
         dn_s[...] = jnp.zeros_like(dn_s)
 
     dy = dy_ref[...]
-    u = dot(b_s[...], wf) + bf_ref[...]
+    pieces = [line_ref[4 * step + i, 0:1, 7 * part : 11 * part] for i in range(4)]
+    u = dot(b_s[...], wf) + jnp.concatenate(pieces, axis=1).astype(f32)
     square = u * u
     t = jnp.tanh(GELU_A * (u + GELU_B * (square * u)))
     m_low = (0.5 * u * (1.0 + t)).astype(bf16)
@@ -843,7 +848,7 @@
     @pl.when(step == pl.num_programs(0) - 1)
     def _():
         h = h_s[...]
-        y_ref[...] = (h + y_s[...] + bp_ref[...]).astype(bf16)
+        y_ref[...] = (h + y_s[...] + row_s[3:4, :]).astype(bf16)
         n, r = moments(h)
         dn = dn_s[...]
         grad = dy_ref[...].astype(f32)
@@ -851,7 +856,7 @@
         small_ref[0:1, :] = jnp.sum(grad, axis=0, keepdims=True)
         small_ref[1:2, :] = jnp.sum(dn * n, axis=0, keepdims=True)
         small_ref[2:3, :] = jnp.sum(dn, axis=0, keepdims=True)
-        e = dn * g_ref[...]
+        e = dn * row_s[1:2, :]
         lean = jnp.mean(e, axis=-1, keepdims=True) + n * jnp.mean(e * n, axis=-1, keepdims=True)
         dh = grad + r * (e - lean)
         dh_ref[...] = dh
@@ -870,11 +875,10 @@
                 do_ref[(2 * t + 1) // OWN, (2 * t + 1) % OWN, to : to + size] = two.astype(bf16)
 
 
-def middle(x, o, dy, wall, bo, gain, shift, bf, bp):
+def middle(x, o, dy, wall, lines):
     fixed2 = lambda i: (0, 0)
     fixed4 = lambda i: (0, 0, 0, 0)
     square = pl.BlockSpec((TOK, D), fixed2)
-    row = pl.BlockSpec((1, D), fixed2)
     heads = pl.BlockSpec((GROUP, OWN, PAIR, 2 * HEAD), fixed4)
     columns = pl.BlockSpec((BLOCKS, 1, D // BLOCKS, D), lambda i: (0, i, 0, 0))
     down = pl.BlockSpec((CHUNK, D), lambda i: (i, 0))
@@ -899,7 +903,7 @@
             pl.BlockSpec((BLOCKS, 48, D), lambda i: (0, 4, 0)),
             pl.BlockSpec((BLOCKS, 48, D), lambda i: (0, 5 + i, 0)),
             pl.BlockSpec((BLOCKS // 4, 192, D), lambda i: (i, 0, 0)),
-            row, row, row, line, row,
+            pl.BlockSpec(lines.shape, lambda i: (0, 0, 0)),
         ],
         out_specs=(
             square, columns, down, line, square, square, heads, pl.BlockSpec((8, D), fixed2),
@@ -911,9 +915,10 @@
             pltpu.VMEM((D, TOK), bf16),
             pltpu.VMEM((TOK, D), f32),
             pltpu.VMEM((TOK, D), f32),
+            pltpu.VMEM((8, D), f32),
         ],
         compiler_params=params(60),
-    )(x, o, dy, wall, wall, wall, bo, gain, shift, bf, bp)
+    )(x, o, dy, wall, wall, wall, lines)
 
 
 ORDER = (4, -3, 3, -2, 2, -1, 1, 0)
@@ -927,7 +932,7 @@
     g_b, q_s, k_s, v_s, f_b, a_b, w_s, x_s, dh_s, lines_s, sums_s, dbf_s,
     near_b, mine_b, y_b, ring_b, fin_b, fin_r, fin_o,
     g_s, dq_s, kt_s, dkv_s, dm_s, w_h, dw_s, db_s,
-    dw_b, z_b, j_b, j_r, rep_b, rep_r, gq_o,
+    dw_b, z_b, j_b, j_r, rep_r, gq_o,
     dn_a, dn_b, dn_c, dn_ra, dn_rb, dn_rc, sm_b, sm_r,
     load, f_sem, a_sem, mine_sem, g_send, g_recv, n_send, n_recv, y_send, y_recv, r_send, r_recv, fin_send,
     fin_recv, z_send, z_recv, j_send, j_recv, rep_send, rep_recv, d_send, d_recv, s_send, s_recv, out_sem,
@@ -1107,7 +1112,7 @@
         )
 
     def j_copy(h, i):
-        return remote(j_b.at[h, pos ^ i], j_r.at[pos, h], j_send.at[h, i], j_recv.at[h, i], me ^ i)
+        return remote(j_b.at[h, pos ^ i], j_r.at[h, pos], j_send.at[h, i], j_recv.at[h, i], me ^ i)
 
     def gather_rows(h):
         for i in range(1, GROUP):
@@ -1116,9 +1121,17 @@
         for i in range(1, GROUP):
             total = total + z_b[h, i].astype(f32)
         j_b[h] = total.astype(bf16).reshape(GROUP, D // n, W3)
-        j_r[pos, h] = j_b[h, pos]
+        j_r[h, pos] = j_b[h, pos]
         for i in range(1, GROUP):
             j_copy(h, i).start()
+
+    def rep_copy(h):
+        return remote(j_r.at[h], rep_r.at[h], rep_send.at[h], rep_recv.at[h], other)
+
+    def trade_rows(h):
+        for i in range(1, GROUP):
+            j_copy(h, i).wait_recv()
+        rep_copy(h).start()
 
     causal = below(T, T, True)
     key_row = lax.broadcasted_iota(jnp.int32, (PROMPT, T), 0).astype(f32)
@@ -1290,10 +1303,13 @@
         diagonal(h, 3)
         flush(h, 3)
 
+        @pl.when(h == 1)
+        def _():
+            ring_step(1)
+
         return carry
 
     lax.fori_loop(0, OWN, stage_last, 0)
-    ring_step(1)
     for copy in f_copies(2):
         copy.start()
     for copy in a_copies(1):
@@ -1312,6 +1328,10 @@
         for p in range(1, 3):
             block(h, 0, PROMPT, p * TOK, PROMPT, None, 0)
         flush(h, 0)
+
+        @pl.when(h == 1)
+        def _():
+            ring_step(2)
 
         return carry
 
@@ -1355,18 +1375,27 @@
         db_s[h, 0:1, :W3] = db
         db_s[h, 1:2, W3 : W3 + D] = jnp.sum(dot_nt(split, w_h[h]), axis=0, keepdims=True)
         db_s[h, 2:3, W3 : W3 + D] = gain_rows[0:1]
+
+        @pl.when(h == 0)
+        def _():
+            ring_step(3)
+
         return carry
 
     lax.fori_loop(0, OWN, stage_middle, 0)
-    for kind, owners in ((2, (0, 3)), (0, (1, 2)), (1, (0, 3))):
-        inner = lax.rem(pos + 1, GROUP) // 2
-
-        @pl.when(inner == (0 if owners == (0, 3) else 1))
+    inner = lax.rem(pos + 1, GROUP) // 2
+
+    def put_last(kind, side):
+        @pl.when(inner == side)
         def _():
             for seg in range(2):
                 put(kind, seg)
 
-    ring_step(2)
+    put_last(2, 0)
+    put_last(0, 1)
+    gather_rows(0)
+    put_last(1, 0)
+    ring_end()
     for copy in later:
         copy.wait()
 
@@ -1408,24 +1437,10 @@
             small_copy(i + 1).start()
 
     small_copy(0).start()
-    gather_rows(0)
-    small_step(0)
-    gather_rows(1)
-    small_step(1)
-    ring_step(3)
-    gather_rows(2)
-    small_step(2)
-    for h in range(OWN):
-        for i in range(1, GROUP):
-            j_copy(h, i).wait_recv()
-    rep_b[...] = j_r[...]
-    rep_copy = remote(rep_b, rep_r, rep_send, rep_recv, other)
-    rep_copy.start()
-    small_step(3)
-    ring_end()
 
     outs = []
-    for seg in (2, 0, 1):
+
+    def finish_rows(seg):
         at = slice(seg * T, (seg + 1) * T)
         rows = dn_rows(pos, seg)
         dn_copy(2, seg).wait_recv()
@@ -1437,6 +1452,19 @@
         copy = pltpu.make_async_copy(dh_s.at[at], grad_ref.at[at], out_sem.at[10 + seg])
         copy.start()
         outs.append(copy)
+
+    finish_rows(2)
+    gather_rows(1)
+    small_step(0)
+    trade_rows(0)
+    small_step(1)
+    gather_rows(2)
+    trade_rows(1)
+    small_step(2)
+    finish_rows(0)
+    finish_rows(1)
+    trade_rows(2)
+    small_step(3)
 
     small_step(4)
     total = sm_b[5]
@@ -1454,11 +1482,12 @@
     copy.start()
     outs.append(copy)
 
-    rep_copy.wait_recv()
+    for h in range(OWN):
+        rep_copy(h).wait_recv()
     for part, (at, piece) in enumerate(((2 * HEAD, 0), (0, 1), (HEAD, 2))):
         row = jnp.concatenate(
             [
-                rep_b[j, h, :, at : at + HEAD].astype(f32) + rep_r[j, h, :, at : at + HEAD].astype(f32)
+                j_r[h, j, :, at : at + HEAD].astype(f32) + rep_r[h, j, :, at : at + HEAD].astype(f32)
                 for j in range(GROUP)
                 for h in range(OWN)
             ],
@@ -1502,7 +1531,8 @@
             dn_copy(kind, seg).wait_send()
     for i in range(1, 5):
         small_copy(i).wait_send()
-    rep_copy.wait_send()
+    for h in range(OWN):
+        rep_copy(h).wait_send()
     fin_copy.wait_send()
     for copy in outs:
         copy.wait()
@@ -1561,9 +1591,8 @@
             vmem((OWN, GROUP, D // GROUP, W3), bf16),
             vmem((OWN, GROUP, D // GROUP, W3), bf16),
             vmem((OWN, GROUP, rows, W3), bf16),
-            vmem((GROUP, OWN, rows, W3), bf16),
-            vmem((GROUP, OWN, rows, W3), bf16),
-            vmem((GROUP, OWN, rows, W3), bf16),
+            vmem((OWN, GROUP, rows, W3), bf16),
+            vmem((OWN, GROUP, rows, W3), bf16),
             vmem((rows, 3 * D), f32),
             vmem((TOK, D), bf16),
             vmem((TOK, D), bf16),
@@ -1591,8 +1620,8 @@
             dma(pairs),
             dma(pairs),
             dma(pairs),
-            dma,
-            dma,
+            dma((OWN,)),
+            dma((OWN,)),
             dma((3, 3)),
             dma((3, 3)),
             dma((5,)),
@@ -1601,6 +1630,50 @@
         ],
         compiler_params=params(63, collective_id=4, has_side_effects=True),
     )(do, q, k, v, f, a, w, x, dh, lines, sums, dbf, dwp, dwo, dwf)
+
+
+def land_kernel(sums_ref, *refs):
+    sources, targets, rows, held, sem = refs[:5], refs[5:10], refs[10:18], refs[18:23], refs[23]
+    parts = []
+    for i, ref in enumerate(held):
+        count = 4 if i == 0 else 1
+        size = ref.shape[0] // count
+        parts += [(i, pl.ds(k * size, size)) for k in range(count)]
+
+    def inward(k):
+        i, at = parts[k]
+        return pltpu.make_async_copy(sources[i].at[at], held[i].at[at], sem.at[0, k])
+
+    def outward(k):
+        i, at = parts[k]
+        return pltpu.make_async_copy(held[i].at[at], targets[i].at[at], sem.at[1, k])
+
+    for k in range(len(parts)):
+        inward(k).start()
+    for i, ref in zip((0, 1, 2, 4, 5, 6, 3, 7), rows):
+        ref[...] = sums_ref[i, : ref.shape[0]]
+    for k in range(len(parts)):
+        inward(k).wait()
+        outward(k).start()
+    for k in range(len(parts)):
+        outward(k).wait()
+
+
+def land(sums, matrices):
+    part = D // BLOCKS
+    shape = jax.ShapeDtypeStruct
+    vector = pl.BlockSpec(memory_space=pltpu.VMEM)
+    return pl.pallas_call(
+        land_kernel,
+        name="land",
+        out_shape=tuple(shape(m.shape, f32) for m in matrices)
+        + tuple(shape((k * part,), f32) for k in (1, 1, 2, 1, 1, 1, 4, 1)),
+        in_specs=[vector] + [ANY] * 5,
+        out_specs=(ANY,) * 5 + (vector,) * 8,
+        scratch_shapes=[pltpu.VMEM(m.shape, f32) for m in matrices]
+        + [pltpu.SemaphoreType.DMA((2, 8))],
+        compiler_params=params(60),
+    )(sums, *matrices)
 
 
 def unproject_kernel(dq_ref, dk_ref, dv_ref, a_ref, w_ref, dn_ref, dw_ref, db_ref):
@@ -1728,7 +1801,6 @@
         small, pieces, shard = pick(tie_index, prefix_len, vectors, w_qkv, w_out, w_fc, w_proj)
         wall, lines, wq, a_low, qx, k, v, o_full, o_recv = forward(block_input, small, pieces, shard)
         a_low = a_low.reshape(ROWS, D)
-        (g1, s1, _, bo, g2, s2, bf, bp), reaches = vectors_of(lines)
     else:
         small = jnp.concatenate([chosen(bank) for bank in vectors])
         reach = prefix_len[0]
@@ -1746,7 +1818,10 @@
         wall = jnp.concatenate([wp, wo, wf.reshape(BLOCKS, -1, D)], axis=1)
         xg, wg = gather_group(n, block_input, pieces)
         wq = wg[:, :rows].reshape(D, WIDE)
-        (g1, s1, bqv, bo, g2, s2, bf, bp), reaches = vectors_of(wg[:, rows : rows + 2])
+        found, reaches = vectors_of(wg[:, rows : rows + 2])
+        g1, s1, bqv = found[:3]
+        lines = jnp.concatenate([row.reshape(BLOCKS, -1) for row in found], axis=1).astype(bf16)
+        lines = jnp.pad(lines[:, None], ((0, 0), (0, 1), (0, 640 - lines.shape[1])))
         own_bias = lax.dynamic_index_in_dim(bqv.reshape(2, GROUP, SLICE), pos, 1, keepdims=False)
         bias = jnp.concatenate([own_bias[0], jnp.zeros((SLICE,), f32), own_bias[1]])[None]
         a_low, q, k, v = project(xg.reshape(ROWS, D), wq, g1, s1, bias)
@@ -1754,16 +1829,15 @@
         o_recv = repack(swap(o_send, 1, "swap_o"), ((0, 384, 384, 0),), PACK)
 
     y, dwf, dwp, dbf, dwo, dh, do_send, sums = middle(
-        block_input, o_recv, cotangent, wall, bo, g2, s2, bf, bp
+        block_input, o_recv, cotangent, wall, lines
     )
     if fused:
         grad, dwq, dwp, dwo, dwf, sums = backward(
             do_send, qx, k, v, o_full, a_low, wq, block_input, dh, lines, sums, dbf,
             dwp.reshape(BLOCKS, -1, D), dwo.reshape(BLOCKS, -1, D), dwf.reshape(BLOCKS, -1, D),
         )
-        rows48 = D // n
-        dg1, ds1, dbo, dg2, ds2, dbp = (sums[i, :rows48] for i in (0, 1, 4, 5, 6, 7))
-        dbqv, dbf = sums[2, : 2 * rows48], sums[3, : 4 * rows48]
+        landed = land(sums, (grad, dwq, dwo, dwf, dwp))
+        grad, dwq, dwo, dwf, dwp, dg1, ds1, dbqv, dbo, dg2, ds2, dbf, dbp = landed
         return (y, grad, dg1, ds1, dwq, dbqv, dwo, dbo, dg2, ds2, dwf, dbf, dwp, dbp)
     dwf = dwf.transpose(0, 2, 1, 3).reshape(D, FF)
     dwf = lax.psum_scatter(dwf, "fsdp", scatter_dimension=0, tiled=True)

time: 284 us -> 263 us (0.926)
  the two profiles are of different devices: /device:TPU:0 before, /device:TPU:1 now
where the time goes in v5:
time: 263 us; the launch traced here: 259 us
  Pallas kernels  256 us (97%)
    pallas_call x1, Pallas kernels, backward(): pl.pallas_call(backward_kernel, name='backward', out_shape=(shape((TOK, D...  111 us
    pallas_call x1, Pallas kernels, forward(): pl.pallas_call(forward_kernel, name='forward', out_shape=(shape((n, UNIT,...  98.6 us
    pallas_call x1, Pallas kernels, middle(): pl.pallas_call(middle_kernel, name='middle', grid=(FF // CHUNK,), out_sha...  39.3 us

profile of v5, /device:TPU:1, one launch (start us, length us, event | category | flops | bytes accessed | tf_op | source)
XLA Modules:
  0.0 258.6 jit_solution(3882908462947728858)
XLA Ops:
  1.9 2.4 pick.1
  4.3 98.6 %forward.1 = (bf16[16,432,768]{2,1,0:T(8,128)(2,1)}, bf16[16,2,640]{2,1,0:T(2,128)(2,1)}, bf16[768,576]{1,0:T(8,128)(2,1)}, bf16[4,768,768]{2,1,0:T(8,128)(2,1)}...) custom-call(bf16[768,768]{1,0:T(8,128)(2,1)} %x_ref.5, ...), custom_call_target="tpu_custom_call" | custom-call | tf_op jit(solution)/shard_map/forward/pallas_call | solution.py:752
  102.9 39.3 %middle.1 = (bf16[768,768]{1,0:T(8,128)(2,1)}, bf16[16,4,48,768]{3,2,1,0:T(8,128)(2,1)}, bf16[3072,768]{1,0:T(8,128)(2,1)}, f32[1,3072]{1,0:T(1,128)}, bf16[768,...) custom-call(bf16[768,768]{1,0:T(8,128)(2,1)} %x_ref.5, ...), custom_call_target="tpu_custom_call" | custom-call | tf_op jit(solution)/shard_map/middle/pallas_call | solution.py:887
  142.3 111.2 %backward.1 = (f32[768,768]{1,0:T(8,128)}, f32[48,2304]{1,0:T(8,128)}, f32[192,768]{1,0:T(8,128)}, f32[48,768]{1,0:T(8,128)}, f32[48,3072]{1,0:T(8,128)}, /*index=5*/f32[16,768]{1,0:T(8,128)}) custom-call(bf16[4,3,384,128]{3,2,1,0:T(8,128)(2,1)} %get-tuple-element.60.do_ref, bf16[3,3072,128]{2,1,0:T(8,128)(2,1)} %get-tuple-element.61.q_ref, ...), custom_call_target="tpu_custom_call" | custom-call | tf_op jit(solution)/shard_map/backward/pallas_call | solution.py:1550
  253.5 4.9 %land.1 = (f32[768,768]{1,0:T(8,128)}, f32[48,2304]{1,0:T(8,128)}, f32[48,768]{1,0:T(8,128)}, f32[48,3072]{1,0:T(8,128)}, f32[192,768]{1,0:T(8,128)}, /*index=5*...) custom-call(f32[16,768]{1,0:T(8,128)} %get-tuple-element.73.sums_ref, ...), custom_call_target="tpu_custom_call" | custom-call | tf_op jit(solution)/shard_map/land/pallas_call | solution.py:1666

commit v6 on v5

--- a/solution.py
+++ b/solution.py
@@ -476,7 +476,7 @@
 def forward_kernel(
     x_ref, sm_ref, pc_ref, sh_ref,
     wall_ref, smo_ref, wq_ref, a_ref, q_ref, k_ref, v_ref, f_ref, o_ref,
-    xg, smg, wg, w_s, q_s, k_s, v_s, f_s, o_s,
+    xg, smg, wg, w_s, q_s, k_s, v_s, f_s, o_s, sh_s,
     local, sm_send, sm_recv, w_send, w_recv, x_send, x_recv, r_send, r_recv, n_send, n_recv,
     y_send, y_recv, o_send, o_recv, out_sem,
 ):
@@ -486,9 +486,11 @@
     pos = lax.rem(me, GROUP)
     base = me - pos
     near, far = me ^ 1, me ^ 2
-    place, device = ring_of(me)
-    parts = 4
-    part_rows = TOK // parts
+    level, xside = me // GROUP, lax.rem(me, GROUP) // 2
+    core = lax.rem(me, 2)
+    levels = n // GROUP
+    parts = TOK // CONT
+    part_rows = CONT
     T = CONT
 
     def remote(src, dst, send, recv, peer):
@@ -503,7 +505,8 @@
 
     greet([me ^ i for i in range(1, n)], 1 - rep)
 
-    own_block = pltpu.make_async_copy(sh_ref, wall_ref.at[me], local.at[0])
+    own_block = pltpu.make_async_copy(sh_ref, sh_s, local.at[0])
+    own_store = pltpu.make_async_copy(sh_s, wall_ref.at[me], local.at[4])
     own_x = pltpu.make_async_copy(x_ref, xg.at[pos], local.at[1])
     own_w = pltpu.make_async_copy(pc_ref.at[pos], wg.at[me], local.at[2])
     own_s = pltpu.make_async_copy(sm_ref, smg.at[me], local.at[3])
@@ -528,64 +531,114 @@
         return remote(src.at[at], xg.at[slot, at], x_send.at[i], x_recv.at[i], peer)
 
     across = [x_part(x_ref, pos, part, part, far) for part in range(parts)]
+    own_block.wait()
+    own_store.start()
+    mine = pl.ds(pl.multiple_of(rep * (D // 2), D // 2), D // 2)
+    other = pl.ds(pl.multiple_of((1 - rep) * (D // 2), D // 2), D // 2)
+    hops, sent, shared = [], [], []
+
+    def begin(copy, keep):
+        copy.start()
+        keep.append((None, copy))
+
+    def block_of(stream, at):
+        side = xside if stream == 0 else 1 - xside
+        return (at * 2 + side) * 2 + core
+
+    def slot(stream, t, up):
+        return 6 * stream + 2 * t + (0 if up else 1)
+
+    def sends(t, up):
+        return (level >= t) & (level < levels - 1) if up else (level + t < levels) & (level > 0)
+
+    def comes(t, up):
+        return level > t if up else level + t < levels - 1
+
+    def when(cond, keep, copies):
+        @pl.when(cond)
+        def _():
+            for copy in copies:
+                copy.start()
+
+        keep.extend((cond, copy) for copy in copies)
+
+    def hop(stream, t, up):
+        at = block_of(stream, level - t if up else level + t)
+        block = wall_ref.at[at, :, mine]
+        src = sh_s.at[:, mine] if stream == 0 and t == 0 else block
+        i = slot(stream, t, up)
+        return remote(src, block, r_send.at[i], r_recv.at[i], me + GROUP if up else me - GROUP)
+
+    def to_near(d, columns, i):
+        block = wall_ref.at[d, :, columns]
+        return remote(block, block, n_send.at[i], n_recv.at[i], near)
+
+    def to_replica(d, columns, i):
+        block = wall_ref.at[d, :, columns]
+        return remote(block, block, y_send.at[i], y_recv.at[i], {"rep": 1 - rep})
+
+    def launch(stream, t):
+        for up in (True, False):
+            when(sends(t, up), hops, [hop(stream, t, up)])
+
+    def came(stream, t, up):
+        return block_of(stream, level - 1 - t if up else level + 1 + t)
+
+    def arrive(stream, t):
+        for up in (True, False):
+            copy = hop(stream, t, up)
+
+            @pl.when(comes(t, up))
+            def _():
+                copy.wait_recv()
+
+        if t < levels - 2:
+            launch(stream, t + 1)
+        for up in (True, False):
+            d, i = came(stream, t, up), slot(stream, t, up)
+            when(comes(t, up), sent, [to_replica(d, mine, i)])
+            when(comes(t, up), shared, [to_near(d, mine, 1 + i)])
+
+    def settle(stream, t):
+        for up in (True, False):
+            d, i = came(stream, t, up), slot(stream, t, up)
+            copy = to_replica(d, other, i)
+
+            @pl.when(comes(t, up))
+            def _():
+                copy.wait_recv()
+
+            when(comes(t, up), shared, [to_near(d, other, 14 + i)])
+
+    facing = block_of(1, level)
+    cross = remote(sh_s.at[:, mine], wall_ref.at[me, :, mine], r_send.at[12], r_recv.at[12], far)
+    crossed = remote(wall_ref.at[facing, :, mine], wall_ref.at[facing, :, mine], r_send.at[12], r_recv.at[12], far)
+
+    def arrive_across():
+        crossed.wait_recv()
+        launch(1, 0)
+        begin(to_replica(facing, mine, 12), sent)
+        begin(to_near(facing, mine, 13), shared)
+
+    def settle_across():
+        to_replica(facing, other, 12).wait_recv()
+        begin(to_near(facing, other, 26), shared)
+
+    def drain(kept, both):
+        for cond, copy in kept:
+            if cond is None:
+                copy.wait() if both else copy.wait_send()
+            else:
+
+                @pl.when(cond)
+                def _():
+                    copy.wait() if both else copy.wait_send()
+
+    cross.start()
     for copy in across:
         copy.start()
-
-    mine = pl.ds(pl.multiple_of(rep * (D // 2), D // 2), D // 2)
-    other = pl.ds(pl.multiple_of((1 - rep) * (D // 2), D // 2), D // 2)
-    sides = lambda t: (True, False) if t < 3 else (True,)
-    key = lambda t, right: t if right else 4 + t
-
-    def came(t, right):
-        return device(place - 1 - t if right else place + 1 + t)
-
-    def hop(t, right):
-        block = wall_ref.at[device(place - t if right else place + t), :, mine]
-        src = sh_ref.at[:, mine] if t == 0 else block
-        i = key(t, right)
-        return remote(src, block, r_send.at[i], r_recv.at[i], device(place + 1 if right else place - 1))
-
-    def to_near(t, right, columns, i):
-        block = wall_ref.at[came(t, right), :, columns]
-        return remote(block, block, n_send.at[i], n_recv.at[i], near)
-
-    def to_replica(t, right):
-        block = wall_ref.at[came(t, right), :, mine]
-        i = key(t, right)
-        return remote(block, block, y_send.at[i], y_recv.at[i], {"rep": 1 - rep})
-
-    def from_replica(t, right):
-        block = wall_ref.at[came(t, right), :, other]
-        i = key(t, right)
-        return remote(block, block, y_send.at[i], y_recv.at[i], {"rep": 1 - rep})
-
-    hops, sent, shared = {}, [], []
-
-    def begin(copy, keep):
-        copy.start()
-        keep.append(copy)
-
-    def launch(t):
-        for right in sides(t):
-            hops[t, right] = hop(t, right)
-            hops[t, right].start()
-
-    def arrive(t):
-        for right in sides(t):
-            hops[t, right].wait_recv()
-        if t < 3:
-            launch(t + 1)
-        for right in sides(t):
-            begin(to_replica(t, right), sent)
-            begin(to_near(t, right, mine, 1 + key(t, right)), shared)
-
-    def settle(t):
-        for right in sides(t):
-            from_replica(t, right).wait_recv()
-            begin(to_near(t, right, other, 8 + key(t, right)), shared)
-
-    launch(0)
-    begin(remote(sh_ref, wall_ref.at[me], n_send.at[0], n_recv.at[0], near), shared)
+    launch(0, 0)
+    begin(remote(sh_s, wall_ref.at[me], n_send.at[0], n_recv.at[0], near), shared)
 
     own_s.wait()
     for copy in smalls:
@@ -603,21 +656,21 @@
         axis=1,
     ).astype(f32)
 
-    def norm(slot):
+    def norm(slot, lo, hi):
         def some(i, carry):
-            at = pl.ds(pl.multiple_of(i * PAIR, PAIR), PAIR)
+            at = pl.ds(pl.multiple_of(i * T, T), T)
             n_rows, _ = moments(xg[slot, at, :].astype(f32))
             xg[slot, at, :] = (n_rows * gain + shift).astype(bf16)
             return carry
 
-        lax.fori_loop(0, 2, some, 0)
-
-    def project_block(slot):
+        lax.fori_loop(lo, hi, some, 0)
+
+    def project_block(slot, lo, hi):
         def some(i, carry):
-            at = pl.ds(pl.multiple_of(i * PAIR, PAIR), PAIR)
-            out = pl.ds(pl.multiple_of(slot * TOK + i * PAIR, PAIR), PAIR)
+            at = pl.ds(pl.multiple_of(i * T, T), T)
+            out = pl.ds(pl.multiple_of(slot * TOK + i * T, T), T)
             mixed = (dot(xg[slot, at, :], w_s[...]) + bias).astype(bf16)
-            ones = jnp.ones((PAIR, HEAD), bf16)
+            ones = jnp.ones((T, HEAD), bf16)
             for h in range(OWN):
                 q = mixed[:, h * HEAD : (h + 1) * HEAD] * 0.125
                 k = mixed[:, SLICE + h * HEAD : SLICE + (h + 1) * HEAD]
@@ -627,7 +680,7 @@
                 v_s[h, out, :] = jnp.concatenate([ones, v], axis=1)
             return carry
 
-        lax.fori_loop(0, 2, some, 0)
+        lax.fori_loop(lo, hi, some, 0)
 
     own_w.wait()
     for copy in slices:
@@ -640,38 +693,42 @@
             wide,
         )
     own_x.wait()
-    norm(pos)
+    norm(pos, 0, 3)
     beside.wait()
-    norm(pos ^ 1)
-    for copy in wide:
+    norm(pos ^ 1, 0, 3)
+    arrive(0, 0)
+    arrive_across()
+    for _, copy in wide:
         copy.wait_recv()
-    arrive(0)
     w_s[...] = wg[:, :rows48, :].reshape(D, WIDE)
-    project_block(pos)
-    project_block(pos ^ 1)
+    project_block(pos, 0, 3)
+    project_block(pos ^ 1, 0, 3)
     passed = []
-    for part in range(parts):
+
+    def take(part):
         across[part].wait_recv()
-        copy = x_part(xg.at[pos ^ 2], pos ^ 2, part, parts + part, near)
-        copy.start()
-        passed.append(copy)
-    for copy in passed:
+        begin(x_part(xg.at[pos ^ 2], pos ^ 2, part, parts + part, near), passed)
+
+    take(0)
+    take(1)
+    arrive(0, 1)
+    for _, copy in passed:
         copy.wait()
-    norm(pos ^ 2)
-    project_block(pos ^ 2)
-    norm(pos ^ 3)
-    project_block(pos ^ 3)
-    arrive(1)
-
-    outs = [
-        pltpu.make_async_copy(smg, smo_ref, out_sem.at[0]),
-        pltpu.make_async_copy(w_s, wq_ref, out_sem.at[1]),
-        pltpu.make_async_copy(xg, a_ref, out_sem.at[2]),
-        pltpu.make_async_copy(k_s, k_ref, out_sem.at[3]),
-        pltpu.make_async_copy(v_s, v_ref, out_sem.at[4]),
-    ]
-    for copy in outs:
-        copy.start()
+    for i in (2, 3):
+        norm(pos ^ i, 0, 2)
+        project_block(pos ^ i, 0, 2)
+    outs = []
+
+    def last_rows():
+        take(2)
+        passed[2][1].wait()
+        for i in (2, 3):
+            norm(pos ^ i, 2, 3)
+            project_block(pos ^ i, 2, 3)
+        for i, (src, dst) in enumerate(
+            ((smg, smo_ref), (w_s, wq_ref), (xg, a_ref), (k_s, k_ref), (v_s, v_ref))
+        ):
+            begin(pltpu.make_async_copy(src, dst, out_sem.at[i]), outs)
 
     lane = lanes(T)
     causal = below(T, T, False)
@@ -704,12 +761,14 @@
             tile(at, past + [(at, T, causal)])
             tile(at + T, past + [(at, T, None), (at + T, T, causal)])
         if h == 0:
-            arrive(2)
+            arrive(0, 2)
+            arrive(1, 0)
+            last_rows()
         if h == 1:
-            arrive(3)
-            settle(0)
+            arrive(1, 2)
         if h == 2:
-            settle(1)
+            settle_across()
+            settle(1, 0)
         for c in range(GROUP):
             at = c * TOK + PROMPT
             blocks = [(i * TOK, PROMPT, column < reaches[c] - i * PROMPT) for i in range(GROUP)]
@@ -720,28 +779,32 @@
                 low = f_s[h, p * TOK + right : p * TOK + right + size, :]
                 pair = jnp.where(lanes(size) < HEAD, pltpu.roll(top, HEAD, 1), low)
                 o_s[h, p, to : to + size, :] = pair.astype(bf16)
+        if h == 0:
+            arrive(1, 1)
+        if h == 1:
+            settle(0, 0)
+            settle(0, 1)
+            settle(0, 2)
         for i in range(1, GROUP):
             copy = remote(
                 o_s.at[h, pos ^ i], o_ref.at[pos, h], o_send.at[h, i], o_recv.at[h, i], me ^ i
             )
-            copy.start()
-            shared.append(copy)
+            begin(copy, shared)
         for src, dst, i in (
             (o_s.at[h, pos], o_ref.at[pos, h], 5 + h),
             (f_s.at[h], f_ref.at[h], 8 + h),
             (q_s.at[h], q_ref.at[h], 11 + h),
         ):
             copy = pltpu.make_async_copy(src, dst, out_sem.at[i])
-            copy.start()
-            outs.append(copy)
-
-    settle(2)
-    settle(3)
-    for copy in across + smalls + slices + wide + list(hops.values()) + sent:
+            begin(copy, outs)
+
+    settle(1, 1)
+    settle(1, 2)
+    for copy in across + smalls + slices + [cross]:
         copy.wait_send()
-    own_block.wait()
-    for copy in shared + outs:
-        copy.wait()
+    drain(wide + hops + sent, False)
+    own_store.wait()
+    drain(shared + outs, True)
 
 
 def forward(x, small, pieces, shard):
@@ -775,19 +838,20 @@
             pltpu.VMEM(head, bf16),
             pltpu.VMEM(head, f32),
             pltpu.VMEM((OWN, GROUP, PAIR, 2 * HEAD), bf16),
-            dma((4,)),
+            pltpu.VMEM(shard.shape, bf16),
+            dma((5,)),
             dma((n,)),
             dma((n,)),
             dma((2 * GROUP,)),
             dma((2 * GROUP,)),
             dma((9,)),
             dma((9,)),
-            dma((7,)),
-            dma((7,)),
-            dma((15,)),
-            dma((15,)),
-            dma((7,)),
-            dma((7,)),
+            dma((13,)),
+            dma((13,)),
+            dma((27,)),
+            dma((27,)),
+            dma((13,)),
+            dma((13,)),
             dma((OWN, GROUP)),
             dma((OWN, GROUP)),
             dma((14,)),

time: 263 us -> 254 us (0.966)
  the two profiles are of different devices: /device:TPU:1 before, /device:TPU:0 now
where the time goes in v6:
time: 254 us; the launch traced here: 249 us
  Pallas kernels  247 us (97%)
    pallas_call x1, Pallas kernels, backward(): pl.pallas_call(backward_kernel, name='backward', out_shape=(shape((TOK, D...  112 us
    pallas_call x1, Pallas kernels, forward(): pl.pallas_call(forward_kernel, name='forward', out_shape=(shape((n, UNIT,...  88.1 us
    pallas_call x1, Pallas kernels, middle(): pl.pallas_call(middle_kernel, name='middle', grid=(FF // CHUNK,), out_sha...  39.5 us

profile of v6, /device:TPU:0, one launch (start us, length us, event | category | flops | bytes accessed | tf_op | source)
XLA Modules:
  0.0 249.1 jit_solution(7895278972362472771)
XLA Ops:
  1.9 2.4 pick.1
  4.3 88.1 %forward.1 = (bf16[16,432,768]{2,1,0:T(8,128)(2,1)}, bf16[16,2,640]{2,1,0:T(2,128)(2,1)}, bf16[768,576]{1,0:T(8,128)(2,1)}, bf16[4,768,768]{2,1,0:T(8,128)(2,1)}...) custom-call(bf16[768,768]{1,0:T(8,128)(2,1)} %x_ref.5, ...), custom_call_target="tpu_custom_call" | custom-call | tf_op jit(solution)/shard_map/forward/pallas_call | solution.py:815
  92.4 39.5 %middle.1 = (bf16[768,768]{1,0:T(8,128)(2,1)}, bf16[16,4,48,768]{3,2,1,0:T(8,128)(2,1)}, bf16[3072,768]{1,0:T(8,128)(2,1)}, f32[1,3072]{1,0:T(1,128)}, bf16[768,...) custom-call(bf16[768,768]{1,0:T(8,128)(2,1)} %x_ref.5, ...), custom_call_target="tpu_custom_call" | custom-call | tf_op jit(solution)/shard_map/middle/pallas_call | solution.py:951
  131.9 112.0 %backward.1 = (f32[768,768]{1,0:T(8,128)}, f32[48,2304]{1,0:T(8,128)}, f32[192,768]{1,0:T(8,128)}, f32[48,768]{1,0:T(8,128)}, f32[48,3072]{1,0:T(8,128)}, /*index=5*/f32[16,768]{1,0:T(8,128)}) custom-call(bf16[4,3,384,128]{3,2,1,0:T(8,128)(2,1)} %get-tuple-element.60.do_ref, bf16[3,3072,128]{2,1,0:T(8,128)(2,1)} %get-tuple-element.61.q_ref, ...), custom_call_target="tpu_custom_call" | custom-call | tf_op jit(solution)/shard_map/backward/pallas_call | solution.py:1614
  243.9 4.9 %land.1 = (f32[768,768]{1,0:T(8,128)}, f32[48,2304]{1,0:T(8,128)}, f32[48,768]{1,0:T(8,128)}, f32[48,3072]{1,0:T(8,128)}, f32[192,768]{1,0:T(8,128)}, /*index=5*...) custom-call(f32[16,768]{1,0:T(8,128)} %get-tuple-element.73.sums_ref, ...), custom_call_target="tpu_custom_call" | custom-call | tf_op jit(solution)/shard_map/land/pallas_call | solution.py:1730

commit v7 on v6

--- a/solution.py
+++ b/solution.py
@@ -1440,7 +1440,7 @@
         db_s[h, 1:2, W3 : W3 + D] = jnp.sum(dot_nt(split, w_h[h]), axis=0, keepdims=True)
         db_s[h, 2:3, W3 : W3 + D] = gain_rows[0:1]
 
-        @pl.when(h == 0)
+        @pl.when(h == 1)
         def _():
             ring_step(3)
 

time: 254 us -> 251 us (0.988)
  no operation moved by 1% of the time
where the time goes in v7:
time: 251 us; the launch traced here: 247 us
  Pallas kernels  245 us (98%)
    pallas_call x1, Pallas kernels, backward(): pl.pallas_call(backward_kernel, name='backward', out_shape=(shape((TOK, D...  110 us
    pallas_call x1, Pallas kernels, forward(): pl.pallas_call(forward_kernel, name='forward', out_shape=(shape((n, UNIT,...  88.1 us
    pallas_call x1, Pallas kernels, middle(): pl.pallas_call(middle_kernel, name='middle', grid=(FF // CHUNK,), out_sha...  39.5 us

profile of v7, /device:TPU:0, one launch (start us, length us, event | category | flops | bytes accessed | tf_op | source)
XLA Modules:
  0.0 246.7 jit_solution(16750363954339247032)
XLA Ops:
  1.9 2.4 pick.1
  4.3 88.1 %forward.1 = (bf16[16,432,768]{2,1,0:T(8,128)(2,1)}, bf16[16,2,640]{2,1,0:T(2,128)(2,1)}, bf16[768,576]{1,0:T(8,128)(2,1)}, bf16[4,768,768]{2,1,0:T(8,128)(2,1)}...) custom-call(bf16[768,768]{1,0:T(8,128)(2,1)} %x_ref.5, ...), custom_call_target="tpu_custom_call" | custom-call | tf_op jit(solution)/shard_map/forward/pallas_call | solution.py:815
  92.4 39.5 %middle.1 = (bf16[768,768]{1,0:T(8,128)(2,1)}, bf16[16,4,48,768]{3,2,1,0:T(8,128)(2,1)}, bf16[3072,768]{1,0:T(8,128)(2,1)}, f32[1,3072]{1,0:T(1,128)}, bf16[768,...) custom-call(bf16[768,768]{1,0:T(8,128)(2,1)} %x_ref.5, ...), custom_call_target="tpu_custom_call" | custom-call | tf_op jit(solution)/shard_map/middle/pallas_call | solution.py:951
  131.9 109.7 %backward.1 = (f32[768,768]{1,0:T(8,128)}, f32[48,2304]{1,0:T(8,128)}, f32[192,768]{1,0:T(8,128)}, f32[48,768]{1,0:T(8,128)}, f32[48,3072]{1,0:T(8,128)}, /*index=5*/f32[16,768]{1,0:T(8,128)}) custom-call(bf16[4,3,384,128]{3,2,1,0:T(8,128)(2,1)} %get-tuple-element.60.do_ref, bf16[3,3072,128]{2,1,0:T(8,128)(2,1)} %get-tuple-element.61.q_ref, ...), custom_call_target="tpu_custom_call" | custom-call | tf_op jit(solution)/shard_map/backward/pallas_call | solution.py:1614
  241.6 4.9 %land.1 = (f32[768,768]{1,0:T(8,128)}, f32[48,2304]{1,0:T(8,128)}, f32[48,768]{1,0:T(8,128)}, f32[48,3072]{1,0:T(8,128)}, f32[192,768]{1,0:T(8,128)}, /*index=5*...) custom-call(f32[16,768]{1,0:T(8,128)} %get-tuple-element.73.sums_ref, ...), custom_call_target="tpu_custom_call" | custom-call | tf_op jit(solution)/shard_map/land/pallas_call | solution.py:1730
